TPU v7x, 32 devices: a whole 2x2x4 slice. The times are simulated.
32 devices in a mesh: dp: 2 (over core), row: 4 (over y, x), col: 4 (over z).
Axes of the slice: x: 2, y: 2, z: 4, core: 2. Of those that a mesh axis runs over, the one named last changes fastest.
Arguments:
- tokens: bfloat16 [768, 32768], P('col', ('dp', 'row')), may hold values from -6 to 6
- w_qkv: bfloat16 [768, 3, 768], P(('dp', 'row'), None, 'col'), may hold values from -0.3125 to 0.3125
- bias_qv: float32 [2, 768], P(None, 'col'), may hold values from -3 to 3
- w_attn_out: bfloat16 [768, 768], P(('dp', 'row'), 'col'), may hold values from -0.875 to 0.875
- bias_attn_out: float32 [768], P('col'), may hold values from -3 to 3
- w_in: bfloat16 [768, 3072], P(('dp', 'row'), 'col'), may hold values from -0.21875 to 0.21875
- bias_in: float32 [3072], P('col'), may hold values from -3 to 3
- w_out: bfloat16 [768, 3072], P(('dp', 'row'), 'col'), may hold values from -0.21875 to 0.21875
- bias_out: float32 [768], P('col'), may hold values from -3 to 3
- norm_gains: float32 [2, 768], P(None, 'col'), may hold values from 0.5 to 1.5
- norm_biases: float32 [2, 768], P(None, 'col'), may hold values from -3 to 3
- seq_lengths: int32 [32], P(('dp', 'row')), may hold values from 256 to 1024, as said below
- seq_offsets: int32 [32], P(('dp', 'row')), may hold values from 0 to 768, as said below
- cotangent: bfloat16 [768, 32768], P('col', ('dp', 'row')), may hold values from -6 to 6
Outputs:
- activations: float32 [768, 32768], P('col', ('dp', 'row'))
- token_grad: float32 [768, 32768], P('col', ('dp', 'row'))
- grad_qkv: float32 [768, 3, 768], P(('dp', 'row'), None, 'col')
- grad_bias_qv: float32 [2, 768], P(None, 'col')
- grad_attn_out: float32 [768, 768], P(('dp', 'row'), 'col')
- grad_bias_attn_out: float32 [768], P('col')
- grad_in: float32 [768, 3072], P(('dp', 'row'), 'col')
- grad_bias_in: float32 [3072], P('col')
- grad_out: float32 [768, 3072], P(('dp', 'row'), 'col')
- grad_bias_out: float32 [768], P('col')
- grad_norm_gains: float32 [2, 768], P(None, 'col')
- grad_norm_biases: float32 [2, 768], P(None, 'col')
Inputs may be any that keep to these rules, and one draw needn't show every extreme that they name: seq_lengths[j] is the length of the one sequence of window j (tokens j * 1024 to (j + 1) * 1024 - 1); 1024 and 256 occur in every draw. seq_offsets[j] + seq_lengths[j] <= 1024: the sequence lies inside its window, the rest of the window is padding.
All inputs are finite; a program needn't handle non-finite values.
Results may differ from a plain program's by a relative error of at most 0.014.
The roundings to bfloat16 on the way count: a program that leaves them out, or rounds other values in their place, can miss the bound.
Values may be sent and summed in bfloat16 or wider, within the bound.
A program may use at most 192 MiB of HBM per device.

v0:
```python
import jax
import jax.numpy as jnp
from jax import lax
from jax.sharding import PartitionSpec as P

D = 768
HEAD_DIM = 64
PACK = 2048
SEQ_MAX = 1024
QBLOCK = 512


EPSILON = 1e-12


def row_totals(first, second):
    return lax.psum((jnp.sum(first, axis=1), jnp.sum(second, axis=1)), "col")


def norm_forward(values, gain_row, shift_row):
    totals = row_totals(values, values * values)
    average = totals[0] / D
    spread = totals[1] / D - average * average
    inverse = lax.rsqrt(spread + EPSILON)
    scaled = (values - average[:, None]) * inverse[:, None]
    return (scaled * gain_row + shift_row, scaled, inverse)


def norm_backward(upstream, scaled, inverse, gain_row):
    weighted = upstream * gain_row
    totals = row_totals(weighted, weighted * scaled)
    return inverse[:, None] * (
        weighted - (totals[0] / D)[:, None] - scaled * (totals[1] / D)[:, None]
    )


def input_total(partial_rows):
    return lax.psum_scatter(partial_rows, "col", scatter_dimension=1, tiled=True)


def grad_rows(values):
    return lax.all_gather(values, "col", axis=1, tiled=True)


def masked_scores(query_block, key_rows, live_mask, first_row):
    scores = jnp.einsum(
        "wqhe,wkhe->whqk", query_block, key_rows, preferred_element_type=jnp.float32
    ) * HEAD_DIM ** (-0.5)
    allowed = live_mask[:, first_row : first_row + QBLOCK, None] == live_mask[:, None, :]
    return jnp.where(allowed[:, None], scores, -1e30)


def attend_forward(queries, key_rows, values, live_mask):
    outputs = []
    log_totals = []
    for first_row in range(0, SEQ_MAX, QBLOCK):
        scores = masked_scores(
            queries[:, first_row : first_row + QBLOCK], key_rows, live_mask, first_row
        )
        largest = jnp.max(scores, axis=-1, keepdims=True)
        exponent = jnp.exp(scores - largest)
        row_total = jnp.sum(exponent, axis=-1, keepdims=True)
        soft_weights = (exponent / row_total).astype(jnp.bfloat16)
        outputs.append(
            jnp.einsum("whqk,wkhe->wqhe", soft_weights, values, preferred_element_type=jnp.float32)
        )
        log_totals.append(largest + jnp.log(row_total))
    return (jnp.concatenate(outputs, axis=1), log_totals)


def attend_backward(queries, key_rows, values, live_mask, log_totals, d_attended):
    score_scale = HEAD_DIM ** (-0.5)
    grad_keys = jnp.zeros(key_rows.shape, jnp.float32)
    grad_values = jnp.zeros(values.shape, jnp.float32)
    grad_queries = []
    for block_index in range(SEQ_MAX // QBLOCK):
        first_row = block_index * QBLOCK
        query_block = queries[:, first_row : first_row + QBLOCK]
        grad_block = d_attended[:, first_row : first_row + QBLOCK]
        scores = masked_scores(query_block, key_rows, live_mask, first_row)
        soft_weights = jnp.exp(scores - log_totals[block_index])
        d_weights = jnp.einsum(
            "wqhe,wkhe->whqk", grad_block, values, preferred_element_type=jnp.float32
        )
        centre = jnp.sum(soft_weights * d_weights, axis=-1, keepdims=True)
        d_scores = (soft_weights * (d_weights - centre)).astype(jnp.bfloat16)
        grad_queries.append(
            jnp.einsum("whqk,wkhe->wqhe", d_scores, key_rows, preferred_element_type=jnp.float32)
            * score_scale
        )
        grad_keys = (
            grad_keys
            + jnp.einsum(
                "whqk,wqhe->wkhe", d_scores, query_block, preferred_element_type=jnp.float32
            )
            * score_scale
        )
        grad_values = grad_values + jnp.einsum(
            "whqk,wqhe->wkhe",
            soft_weights.astype(jnp.bfloat16),
            grad_block,
            preferred_element_type=jnp.float32,
        )
    return (jnp.concatenate(grad_queries, axis=1), grad_keys, grad_values)


def contract_last(left, right):
    return lax.dot_general(
        left, right, (((1,), (1,)), ((), ())), preferred_element_type=jnp.float32
    )


def contract_first(left, right):
    return lax.dot_general(
        left, right, (((0,), (0,)), ((), ())), preferred_element_type=jnp.float32
    )


def local(
    tokens,
    w_qkv,
    bias_qv,
    w_attn_out,
    bias_attn_out,
    w_in,
    bias_in,
    w_out,
    bias_out,
    norm_gains,
    norm_biases,
    seq_lengths,
    seq_offsets,
    cotangent,
):
    part_width = tokens.shape[0]
    head_width = w_qkv.shape[2]
    head_count = head_width // HEAD_DIM
    micro_count = tokens.shape[1] // PACK
    windows = PACK // SEQ_MAX
    window_shape = (windows, SEQ_MAX, head_count, HEAD_DIM)
    places = jnp.arange(SEQ_MAX, dtype=jnp.int32)
    weight_zero = (
        jnp.zeros(w_qkv.shape, jnp.float32),
        jnp.zeros(w_attn_out.shape, jnp.float32),
        jnp.zeros(w_in.shape, jnp.float32),
        jnp.zeros(w_out.shape, jnp.float32),
    )
    small_zero = (
        jnp.zeros(bias_qv.shape, jnp.float32),
        jnp.zeros(bias_attn_out.shape, jnp.float32),
        jnp.zeros(bias_in.shape, jnp.float32),
        jnp.zeros(bias_out.shape, jnp.float32),
        jnp.zeros(norm_gains.shape, jnp.float32),
        jnp.zeros(norm_biases.shape, jnp.float32),
    )

    def micro_step(carried, inputs):
        token_cols, upstream_cols, lengths, offsets = inputs
        weight_sums, small_sums = carried
        gathered = (
            lax.all_gather(w_qkv, ("dp", "row"), axis=0, tiled=True),
            lax.all_gather(w_attn_out, ("dp", "row"), axis=0, tiled=True),
            lax.all_gather(w_in, ("dp", "row"), axis=0, tiled=True),
            lax.all_gather(w_out, ("dp", "row"), axis=0, tiled=True),
        )
        full_qkv, full_attn_out, full_in, full_out = gathered
        live_mask = (places[None, :] >= offsets[:, None]) & (
            places[None, :] < offsets[:, None] + lengths[:, None]
        )
        live_rows = live_mask.reshape(PACK).astype(jnp.float32)[:, None]
        token_full_cols = lax.all_gather(token_cols, "col", axis=0, tiled=True)
        projected = jnp.einsum(
            "dt,dke->tke", token_full_cols, full_qkv, preferred_element_type=jnp.float32
        )
        queries = (projected[:, 0] + bias_qv[0]).astype(jnp.bfloat16).reshape(window_shape)
        key_rows = projected[:, 1].astype(jnp.bfloat16).reshape(window_shape)
        values = (projected[:, 2] + bias_qv[1]).astype(jnp.bfloat16).reshape(window_shape)
        attended, log_totals = attend_forward(queries, key_rows, values, live_mask)
        attended = attended.reshape(PACK, head_width).astype(jnp.bfloat16)
        branch = lax.psum_scatter(
            contract_last(attended, full_attn_out), "col", scatter_dimension=1, tiled=True
        )
        first_sum = token_cols.astype(jnp.float32).T + branch + bias_attn_out
        normed, scaled_one, inverse_one = norm_forward(first_sum, norm_gains[0], norm_biases[0])
        normed_full = lax.all_gather(normed.astype(jnp.bfloat16), "col", axis=1, tiled=True)
        hidden = jnp.dot(normed_full, full_in, preferred_element_type=jnp.float32) + bias_in
        active_low = jax.nn.gelu(hidden, approximate=False).astype(jnp.bfloat16)
        second = lax.psum_scatter(
            contract_last(active_low, full_out), "col", scatter_dimension=1, tiled=True
        )
        second_sum = normed + second + bias_out
        result, scaled_two, inverse_two = norm_forward(second_sum, norm_gains[1], norm_biases[1])
        activations = (result * live_rows).T
        regathered = (
            lax.all_gather(w_qkv, ("dp", "row"), axis=0, tiled=True),
            lax.all_gather(w_attn_out, ("dp", "row"), axis=0, tiled=True),
            lax.all_gather(w_in, ("dp", "row"), axis=0, tiled=True),
            lax.all_gather(w_out, ("dp", "row"), axis=0, tiled=True),
        )
        back_qkv, back_attn_out, back_in, back_out = regathered
        upstream = upstream_cols.astype(jnp.float32).T * live_rows
        gain_two = jnp.sum(upstream * scaled_two, axis=0)
        shift_two = jnp.sum(upstream, axis=0)
        d_second = norm_backward(upstream, scaled_two, inverse_two, norm_gains[1])
        bias_out_grad = jnp.sum(d_second, axis=0)
        d_second_full = grad_rows(d_second.astype(jnp.bfloat16))
        out_grad = contract_first(d_second_full, active_low)
        d_active = jnp.dot(d_second_full, back_out, preferred_element_type=jnp.float32)
        gelu_pull = jax.vjp(lambda pre_act: jax.nn.gelu(pre_act, approximate=False), hidden)[1]
        d_hidden = gelu_pull(d_active)[0]
        bias_in_grad = jnp.sum(d_hidden, axis=0)
        d_hidden_low = d_hidden.astype(jnp.bfloat16)
        in_grad = contract_first(normed_full, d_hidden_low)
        d_normed = d_second + input_total(contract_last(d_hidden_low, back_in))
        gain_one = jnp.sum(d_normed * scaled_one, axis=0)
        shift_one = jnp.sum(d_normed, axis=0)
        d_first = norm_backward(d_normed, scaled_one, inverse_one, norm_gains[0])
        bias_attn_grad = jnp.sum(d_first, axis=0)
        d_first_full = grad_rows(d_first.astype(jnp.bfloat16))
        attn_out_grad = contract_first(d_first_full, attended)
        d_attended = jnp.dot(
            d_first_full, back_attn_out, preferred_element_type=jnp.float32
        ).astype(jnp.bfloat16)
        grad_q, grad_k, grad_v = attend_backward(
            queries, key_rows, values, live_mask, log_totals, d_attended.reshape(window_shape)
        )
        grad_q = grad_q.reshape(PACK, head_width)
        grad_k = grad_k.reshape(PACK, head_width)
        grad_v = grad_v.reshape(PACK, head_width)
        qv_grad = jnp.stack([jnp.sum(grad_q, axis=0), jnp.sum(grad_v, axis=0)])
        d_projected = jnp.stack([grad_q, grad_k, grad_v], axis=1).astype(jnp.bfloat16)
        qkv_grad = jnp.einsum(
            "dt,tke->dke", token_full_cols, d_projected, preferred_element_type=jnp.float32
        )
        token_grad = (
            d_first
            + input_total(
                jnp.einsum("tke,dke->td", d_projected, back_qkv, preferred_element_type=jnp.float32)
            )
        ).T
        summed = (
            lax.psum_scatter(qkv_grad, ("dp", "row"), scatter_dimension=0, tiled=True),
            lax.psum_scatter(attn_out_grad, ("dp", "row"), scatter_dimension=0, tiled=True),
            lax.psum_scatter(in_grad, ("dp", "row"), scatter_dimension=0, tiled=True),
            lax.psum_scatter(out_grad, ("dp", "row"), scatter_dimension=0, tiled=True),
        )
        weight_sums = jax.tree.map(jnp.add, weight_sums, summed)
        small_terms = (
            qv_grad,
            bias_attn_grad,
            bias_in_grad,
            bias_out_grad,
            jnp.stack([gain_one, gain_two]),
            jnp.stack([shift_one, shift_two]),
        )
        small_sums = jax.tree.map(jnp.add, small_sums, small_terms)
        return ((weight_sums, small_sums), (activations, token_grad))

    token_blocks = tokens.reshape(part_width, micro_count, PACK).transpose(1, 0, 2)
    upstream_blocks = cotangent.reshape(part_width, micro_count, PACK).transpose(1, 0, 2)
    inputs = (
        token_blocks,
        upstream_blocks,
        seq_lengths.reshape(micro_count, windows),
        seq_offsets.reshape(micro_count, windows),
    )
    finals, stacked = lax.scan(micro_step, (weight_zero, small_zero), inputs)
    weight_sums, small_sums = finals
    small_sums = lax.psum(
        (small_sums[0], small_sums[1], small_sums[2], small_sums[3], small_sums[4], small_sums[5]),
        ("dp", "row"),
    )
    activations = stacked[0].transpose(1, 0, 2).reshape(part_width, micro_count * PACK)
    token_grads = stacked[1].transpose(1, 0, 2).reshape(part_width, micro_count * PACK)
    return (
        activations,
        token_grads,
        weight_sums[0],
        small_sums[0],
        weight_sums[1],
        small_sums[1],
        weight_sums[2],
        small_sums[2],
        weight_sums[3],
        small_sums[3],
        small_sums[4],
        small_sums[5],
    )


def solution(mesh):
    return jax.shard_map(
        local,
        mesh=mesh,
        in_specs=(
            P("col", ("dp", "row")),
            P(("dp", "row"), None, "col"),
            P(None, "col"),
            P(("dp", "row"), "col"),
            P("col"),
            P(("dp", "row"), "col"),
            P("col"),
            P(("dp", "row"), "col"),
            P("col"),
            P(None, "col"),
            P(None, "col"),
            P(("dp", "row")),
            P(("dp", "row")),
            P("col", ("dp", "row")),
        ),
        out_specs=(
            P("col", ("dp", "row")),
            P("col", ("dp", "row")),
            P(("dp", "row"), None, "col"),
            P(None, "col"),
            P(("dp", "row"), "col"),
            P("col"),
            P(("dp", "row"), "col"),
            P("col"),
            P(("dp", "row"), "col"),
            P("col"),
            P(None, "col"),
            P(None, "col"),
        ),
        check_vma=False,
    )
```

profile of v0, /device:TPU:0, one launch (start us, length us, event | category | flops | bytes accessed | tf_op | source)
XLA Modules:
  0.0 2195.7 jit_solution(1545050451613228207)
XLA Ops:
  19.6 2136.5 %while.34 = (s32[]{:T(128)}, f32[96,3,192]{2,0,1:T(8,128)}, f32[96,192]{1,0:T(8,128)}, f32[96,768]{1,0:T(8,128)}, f32[96,768]{1,0:T(8,128)}, /*index=5*/f32[2,19...) while((s32[]{:T(128)}, f32[96,3,192]{2,0,1:T(8,128)}, ...), condition=%wide.region_41.42_spmd.clone.clone, body=%wide.region_0.41_spmd.clone.clone.sunk | while | flops 26853322752 | bytes 1020480256 | solution.py:267
  21.6 35.7 %all_gather.50 = bf16[768,3,192]{2,1,0:T(4,128)(2,1)S(1)} all-gather(bf16[96,3,192]{2,1,0:T(4,128)(2,1)} %get-tuple-element.915), channel_id=1, replica_groups=mesh['dp'=2,'row'=4,'col'=4] {'dp','row'}, dimensions={0}, use_global_device_ids=true | all-gather | bytes 995328 | tf_op jit(solution)/shard_map/while/body/eval_jaxpr/all_gather | solution.py:161
  59.5 24.0 %all_gather.51 = bf16[768,192]{1,0:T(8,128)(2,1)S(1)} all-gather(bf16[96,192]{1,0:T(8,128)(2,1)S(1)} %copy-done.45), channel_id=1, replica_groups=mesh['dp'=2,'row'=4,'col'=4] {'dp','row'}, dimensions={0}, use_global_device_ids=true | all-gather | bytes 331776 | tf_op jit(solution)/shard_map/while/body/eval_jaxpr/all_gather | solution.py:162
  101.6 4.3 fusion.240
  131.7 106.2 %reduce-scatter.9.cloned.1.call-done = f32[2048,192]{0,1:T(8,128)} async-done(((f32[2048,768]{0,1:T(8,128)}), f32[2048,192]{0,1:T(8,128)}) %reduce-scatter.9.cloned.1.call-update) | async-done | bytes 1572880 | tf_op jit(solution)/shard_map/while/body/eval_jaxpr/reduce_scatter | solution.py:180
  239.7 18.0 all-reduce.9
  264.2 65.5 %all-gather.13.cloned.1.call-done = bf16[2048,768]{0,1:T(8,128)(2,1)} async-done(((bf16[2048,192]{0,1:T(8,128)(2,1)}), bf16[2048,768]{0,1:T(8,128)(2,1)}) %all-gather.13.cloned.1.call-update) | async-done | bytes 3145744 | tf_op jit(solution)/shard_map/while/body/eval_jaxpr/all_gather | solution.py:185
  329.6 19.3 multiply_convert_fusion.7
  348.9 5.0 all-gather.17.cloned.1.call-done
  354.0 7.5 fusion.247
  362.1 110.3 %reduce-scatter.11.cloned.1.call-done = f32[2048,192]{0,1:T(8,128)} async-done(((f32[2048,768]{0,1:T(8,128)}), f32[2048,192]{0,1:T(8,128)}) %reduce-scatter.11.cloned.1.call-update) | async-done | bytes 1572880 | tf_op jit(solution)/shard_map/while/body/eval_jaxpr/reduce_scatter | solution.py:188
  475.0 19.4 all-reduce.10
  497.9 16.7 all-reduce.11
  519.2 62.3 %all-gather.19.cloned.1.call-done = bf16[2048,768]{0,1:T(8,128)(2,1)} async-done(((bf16[2048,192]{0,1:T(8,128)(2,1)}), bf16[2048,768]{0,1:T(8,128)(2,1)}) %all-gather.19.cloned.1.call-update) | async-done | bytes 3145744 | tf_op jit(solution)/shard_map/while/body/eval_jaxpr/all_gather | solution.py:42
  581.6 11.4 fusion.250
  594.6 4.5 fusion.251
  599.1 109.5 %reduce-scatter.13.cloned.1.call-done = f32[2048,192]{0,1:T(8,128)} async-done(((f32[2048,768]{0,1:T(8,128)}), f32[2048,192]{0,1:T(8,128)}) %reduce-scatter.13.cloned.1.call-update) | async-done | bytes 1572880 | tf_op jit(solution)/shard_map/while/body/eval_jaxpr/reduce_scatter | solution.py:38
  708.7 4.9 fusion.252
  713.6 18.6 all-reduce.12
  736.9 6.8 fusion.262
  743.9 7.0 fusion.263
  751.5 47.3 %all-gather.21.cloned.1.call-done = bf16[2048,768]{0,1:T(8,128)(2,1)} async-done(((bf16[2048,192]{0,1:T(8,128)(2,1)}), bf16[2048,768]{0,1:T(8,128)(2,1)}) %all-gather.21.cloned.1.call-update) | async-done | bytes 3145744 | tf_op jit(solution)/shard_map/while/body/eval_jaxpr/all_gather | solution.py:42
  802.6 6.1 fusion.259
  808.8 10.3 multiply_reduce_fusion.13
  819.1 6.1 multiply_reduce_fusion.14
  830.8 9.8 multiply_convert_fusion.9
  845.4 6.4 multiply_convert_fusion.8
  873.4 6.8 fusion.260
  880.3 4.7 convolution_bitcast_fusion.2
  898.9 27.8 %reduce-scatter.17.cloned.1.call-done = f32[96,192]{1,0:T(8,128)} async-done(((f32[768,192]{1,0:T(8,128)}), f32[96,192]{1,0:T(8,128)}) %reduce-scatter.17.cloned.1.call-update) | async-done | bytes 73744 | tf_op jit(solution)/shard_map/while/body/eval_jaxpr/reduce_scatter | solution.py:243
  927.6 44.8 %reduce-scatter.15.cloned.1.call-done = f32[96,3,192]{2,0,1:T(8,128)} async-done(((f32[768,3,192]{2,0,1:T(8,128)}), f32[96,3,192]{2,0,1:T(8,128)}) %reduce-scatter.15.cloned.1.call-update) | async-done | bytes 221200 | tf_op jit(solution)/shard_map/while/body/eval_jaxpr/reduce_scatter | solution.py:242
  974.1 111.2 %reduce-scatter.23.cloned.1.call-done = f32[2048,192]{0,1:T(8,128)} async-done(((f32[2048,768]{0,1:T(8,128)}), f32[2048,192]{0,1:T(8,128)}) %reduce-scatter.23.cloned.1.call-update) | async-done | bytes 1572880 | tf_op jit(solution)/shard_map/while/body/eval_jaxpr/reduce_scatter | solution.py:38
  1090.6 34.1 %all_gather.50 = bf16[768,3,192]{2,1,0:T(4,128)(2,1)S(1)} all-gather(bf16[96,3,192]{2,1,0:T(4,128)(2,1)} %get-tuple-element.915), channel_id=1, replica_groups=mesh['dp'=2,'row'=4,'col'=4] {'dp','row'}, dimensions={0}, use_global_device_ids=true | all-gather | bytes 995328 | tf_op jit(solution)/shard_map/while/body/eval_jaxpr/all_gather | solution.py:161
  1126.8 24.0 %all_gather.51 = bf16[768,192]{1,0:T(8,128)(2,1)S(1)} all-gather(bf16[96,192]{1,0:T(8,128)(2,1)S(1)} %copy-done.45), channel_id=1, replica_groups=mesh['dp'=2,'row'=4,'col'=4] {'dp','row'}, dimensions={0}, use_global_device_ids=true | all-gather | bytes 331776 | tf_op jit(solution)/shard_map/while/body/eval_jaxpr/all_gather | solution.py:162
  1168.1 4.3 fusion.240
  1197.6 106.3 %reduce-scatter.9.cloned.1.call-done = f32[2048,192]{0,1:T(8,128)} async-done(((f32[2048,768]{0,1:T(8,128)}), f32[2048,192]{0,1:T(8,128)}) %reduce-scatter.9.cloned.1.call-update) | async-done | bytes 1572880 | tf_op jit(solution)/shard_map/while/body/eval_jaxpr/reduce_scatter | solution.py:180
  1305.7 18.0 all-reduce.9
  1330.1 65.5 %all-gather.13.cloned.1.call-done = bf16[2048,768]{0,1:T(8,128)(2,1)} async-done(((bf16[2048,192]{0,1:T(8,128)(2,1)}), bf16[2048,768]{0,1:T(8,128)(2,1)}) %all-gather.13.cloned.1.call-update) | async-done | bytes 3145744 | tf_op jit(solution)/shard_map/while/body/eval_jaxpr/all_gather | solution.py:185
  1395.6 19.3 multiply_convert_fusion.7
  1414.9 5.2 all-gather.17.cloned.1.call-done
  1420.0 7.5 fusion.247
  1428.2 110.3 %reduce-scatter.11.cloned.1.call-done = f32[2048,192]{0,1:T(8,128)} async-done(((f32[2048,768]{0,1:T(8,128)}), f32[2048,192]{0,1:T(8,128)}) %reduce-scatter.11.cloned.1.call-update) | async-done | bytes 1572880 | tf_op jit(solution)/shard_map/while/body/eval_jaxpr/reduce_scatter | solution.py:188
  1541.1 19.6 all-reduce.10
  1564.2 16.7 all-reduce.11
  1585.5 62.3 %all-gather.19.cloned.1.call-done = bf16[2048,768]{0,1:T(8,128)(2,1)} async-done(((bf16[2048,192]{0,1:T(8,128)(2,1)}), bf16[2048,768]{0,1:T(8,128)(2,1)}) %all-gather.19.cloned.1.call-update) | async-done | bytes 3145744 | tf_op jit(solution)/shard_map/while/body/eval_jaxpr/all_gather | solution.py:42
  1647.8 11.4 fusion.250
  1660.9 4.5 fusion.251
  1665.4 109.5 %reduce-scatter.13.cloned.1.call-done = f32[2048,192]{0,1:T(8,128)} async-done(((f32[2048,768]{0,1:T(8,128)}), f32[2048,192]{0,1:T(8,128)}) %reduce-scatter.13.cloned.1.call-update) | async-done | bytes 1572880 | tf_op jit(solution)/shard_map/while/body/eval_jaxpr/reduce_scatter | solution.py:38
  1775.0 4.9 fusion.252
  1779.8 18.6 all-reduce.12
  1803.2 6.8 fusion.262
  1810.2 7.0 fusion.263
  1817.5 47.6 %all-gather.21.cloned.1.call-done = bf16[2048,768]{0,1:T(8,128)(2,1)} async-done(((bf16[2048,192]{0,1:T(8,128)(2,1)}), bf16[2048,768]{0,1:T(8,128)(2,1)}) %all-gather.21.cloned.1.call-update) | async-done | bytes 3145744 | tf_op jit(solution)/shard_map/while/body/eval_jaxpr/all_gather | solution.py:42
  1868.9 6.1 fusion.259
  1875.1 10.3 multiply_reduce_fusion.13
  1885.4 6.1 multiply_reduce_fusion.14
  1897.0 9.8 multiply_convert_fusion.9
  1911.7 6.5 multiply_convert_fusion.8
  1939.8 6.8 fusion.260
  1946.6 4.9 convolution_bitcast_fusion.2
  1966.5 26.6 %reduce-scatter.17.cloned.1.call-done = f32[96,192]{1,0:T(8,128)} async-done(((f32[768,192]{1,0:T(8,128)}), f32[96,192]{1,0:T(8,128)}) %reduce-scatter.17.cloned.1.call-update) | async-done | bytes 73744 | tf_op jit(solution)/shard_map/while/body/eval_jaxpr/reduce_scatter | solution.py:243
  1994.0 44.6 %reduce-scatter.15.cloned.1.call-done = f32[96,3,192]{2,0,1:T(8,128)} async-done(((f32[768,3,192]{2,0,1:T(8,128)}), f32[96,3,192]{2,0,1:T(8,128)}) %reduce-scatter.15.cloned.1.call-update) | async-done | bytes 221200 | tf_op jit(solution)/shard_map/while/body/eval_jaxpr/reduce_scatter | solution.py:242
  2040.5 111.3 %reduce-scatter.23.cloned.1.call-done = f32[2048,192]{0,1:T(8,128)} async-done(((f32[2048,768]{0,1:T(8,128)}), f32[2048,192]{0,1:T(8,128)}) %reduce-scatter.23.cloned.1.call-update) | async-done | bytes 1572880 | tf_op jit(solution)/shard_map/while/body/eval_jaxpr/reduce_scatter | solution.py:38
  2160.3 26.5 %all-reduce.4 = (f32[2,192]{1,0:T(2,128)}, f32[192]{0:T(256)}, f32[768]{0:T(1024)}, f32[192]{0:T(256)}, f32[2,192]{1,0:T(2,128)}, /*index=5*/f32[2,192]{1,0:T(2,128)}) all-reduce(f32[2,192]{1,0:T(2,128)S(1)} %copy-done.54, f32[192]{0:T(256)S(1)} %copy-done.56, ...), channel_id=1, replica_groups=mesh['dp'=2,'row'=4,'col'=4] {'dp','row'}, use_global_device_ids=true, to_apply=%region_42.43 | all-reduce | flops 2304 | bytes 18432 | tf_op jit(solution)/shard_map/psum | solution.py:269
  (507 shorter events, 276.3 us)
Async XLA Ops:
  19.6 69.1 %all-gather.11.cloned.1.call-start = ((), (), s32[]{:S(2)}) async-start(), calls=%async_computation.8 | async-start | bytes 3932160 | tf_op jit(solution)/shard_map/while/body/eval_jaxpr/all_gather | solution.py:171
  19.6 39.9 %copy-start.45 = (bf16[96,192]{1,0:T(8,128)(2,1)S(1)}, bf16[96,192]{1,0:T(8,128)(2,1)}, u32[]{:S(2)}) copy-start(bf16[96,192]{1,0:T(8,128)(2,1)} %get-tuple-element.919) | copy-start | bytes 110596 | tf_op jit(solution)/shard_map/while
  20.7 217.2 %reduce-scatter.9.cloned.1.call-start = ((), (), s32[]{:S(2)}) async-start(), calls=%async_computation.9 | async-start | bytes 7864320 | tf_op jit(solution)/shard_map/while/body/eval_jaxpr/reduce_scatter | solution.py:180
  58.2 34.4 %copy-start.23 = (bf16[768,3,192]{0,2,1:T(8,128)(2,1)}, bf16[768,3,192]{0,2,1:T(8,128)(2,1)S(1)}, u32[]{:S(2)}) copy-start(bf16[768,3,192]{0,2,1:T(8,128)(2,1)S(1)} %copy.146) | copy-start | bytes 2654212 | tf_op jit(solution)/shard_map/while
  128.2 109.6 %copy-start.20 = (bf16[2,192,2048]{2,1,0:T(8,128)(2,1)S(1)}, bf16[2,192,2048]{2,1,0:T(8,128)(2,1)}, u32[]{:S(2)}) copy-start(bf16[2,192,2048]{2,1,0:T(8,128)(2,1)} %copy-done.19) | copy-start | bytes 4718596 | tf_op jit(solution)/shard_map/while
  128.3 135.9 %all-gather.15.cloned.1.call-start = ((), (), s32[]{:S(2)}) async-start(), calls=%async_computation.11 | async-start | bytes 1327104 | tf_op jit(solution)/shard_map/while/body/eval_jaxpr/all_gather | solution.py:163
  129.0 200.6 %all-gather.13.cloned.1.call-start = ((), (), s32[]{:S(2)}) async-start(), calls=%async_computation.10 | async-start | bytes 3932160 | tf_op jit(solution)/shard_map/while/body/eval_jaxpr/all_gather | solution.py:185
  239.7 90.0 %copy-start.58 = (f32[768]{0:T(1024)S(1)}, f32[768]{0:T(1024)}, u32[]{:S(2)}) copy-start(f32[768]{0:T(1024)} %get-tuple-element.924) | copy-start | bytes 9220 | tf_op jit(solution)/shard_map/while
  257.7 91.3 %copy-start.31 = (f32[2048]{0:T(1024)}, f32[2048]{0:T(1024)S(1)}, u32[]{:S(2)}) copy-start(f32[2048]{0:T(1024)S(1)} %get-tuple-element.795) | copy-start | bytes 24580 | tf_op jit(solution)/shard_map/while
  257.7 214.7 %copy-start.30 = (f32[2048]{0:T(1024)}, f32[2048]{0:T(1024)S(1)}, u32[]{:S(2)}) copy-start(f32[2048]{0:T(1024)S(1)} %get-tuple-element.796) | copy-start | bytes 24580 | tf_op jit(solution)/shard_map/while
  259.6 94.4 %all-gather.17.cloned.1.call-start = ((), (), s32[]{:S(2)}) async-start(), calls=%async_computation.12 | async-start | bytes 1327104 | tf_op jit(solution)/shard_map/while/body/eval_jaxpr/all_gather | solution.py:164
  260.2 212.2 %reduce-scatter.11.cloned.1.call-start = ((), (), s32[]{:S(2)}) async-start(), calls=%async_computation.13 | async-start | bytes 7864320 | tf_op jit(solution)/shard_map/while/body/eval_jaxpr/reduce_scatter | solution.py:188
  361.5 220.1 %all-gather.19.cloned.1.call-start = ((), (), s32[]{:S(2)}) async-start(), calls=%async_computation.14 | async-start | bytes 3932160 | tf_op jit(solution)/shard_map/while/body/eval_jaxpr/all_gather | solution.py:42
  475.0 233.6 %copy-start.4 = (f32[2048,192]{0,1:T(8,128)}, f32[2048,192]{0,1:T(8,128)S(1)}, u32[]{:S(2)}) copy-start(f32[2048,192]{0,1:T(8,128)S(1)} %get-tuple-element.798) | copy-start | bytes 4718596 | tf_op jit(solution)/shard_map/while
  519.2 189.5 %reduce-scatter.13.cloned.1.call-start = ((), (), s32[]{:S(2)}) async-start(), calls=%async_computation.15 | async-start | bytes 7864320 | tf_op jit(solution)/shard_map/while/body/eval_jaxpr/reduce_scatter | solution.py:38
  599.1 199.7 %all-gather.21.cloned.1.call-start = ((), (), s32[]{:S(2)}) async-start(), calls=%async_computation.16 | async-start | bytes 3932160 | tf_op jit(solution)/shard_map/while/body/eval_jaxpr/all_gather | solution.py:42
  736.9 153.2 %reduce-scatter.19.cloned.1.call-start = ((), (), s32[]{:S(2)}) async-start(), calls=%async_computation.19 | async-start | bytes 2654208 | tf_op jit(solution)/shard_map/while/body/eval_jaxpr/reduce_scatter | solution.py:244
  743.8 148.0 %reduce-scatter.21.cloned.1.call-start = ((), (), s32[]{:S(2)}) async-start(), calls=%async_computation.20 | async-start | bytes 2654208 | tf_op jit(solution)/shard_map/while/body/eval_jaxpr/reduce_scatter | solution.py:245
  751.0 175.7 %reduce-scatter.17.cloned.1.call-start = ((), (), s32[]{:S(2)}) async-start(), calls=%async_computation.18 | async-start | bytes 884736 | tf_op jit(solution)/shard_map/while/body/eval_jaxpr/reduce_scatter | solution.py:243
  802.6 16.5 slice-start.3
  802.6 16.4 slice-start.4
  830.7 13.0 slice-start
  830.7 13.0 slice-start.1
  830.8 14.6 slice-start.2
  871.5 100.9 %reduce-scatter.15.cloned.1.call-start = ((), (), s32[]{:S(2)}) async-start(), calls=%async_computation.17 | async-start | bytes 2654208 | tf_op jit(solution)/shard_map/while/body/eval_jaxpr/reduce_scatter | solution.py:242
  880.2 205.2 %reduce-scatter.23.cloned.1.call-start = ((), (), s32[]{:S(2)}) async-start(), calls=%async_computation.21 | async-start | bytes 7864320 | tf_op jit(solution)/shard_map/while/body/eval_jaxpr/reduce_scatter | solution.py:38
  887.2 198.2 %copy-start.7 = (f32[2048,192]{0,1:T(8,128)S(1)}, f32[2048,192]{0,1:T(8,128)}, u32[]{:S(2)}) copy-start(f32[2048,192]{0,1:T(8,128)} %copy-done.6) | copy-start | bytes 4718596 | tf_op jit(solution)/shard_map/while
  888.8 37.9 %copy-start.33 = (f32[96,192]{1,0:T(8,128)S(1)}, f32[96,192]{1,0:T(8,128)}, u32[]{:S(2)}) copy-start(f32[96,192]{1,0:T(8,128)} %get-tuple-element.874) | copy-start | bytes 221188 | tf_op jit(solution)/shard_map/while
  892.9 195.3 %copy-start.26 = (f32[96,768]{1,0:T(8,128)}, f32[96,768]{1,0:T(8,128)S(1)}, u32[]{:S(2)}) copy-start(f32[96,768]{1,0:T(8,128)S(1)} %select_add_fusion.17) | copy-start | bytes 884740 | tf_op jit(solution)/shard_map/while
  898.1 190.0 %copy-start.21 = (bf16[2,192,2048]{2,1,0:T(8,128)(2,1)S(1)}, bf16[2,192,2048]{2,1,0:T(8,128)(2,1)}, u32[]{:S(2)}) copy-start(bf16[2,192,2048]{2,1,0:T(8,128)(2,1)} %copy-done.19) | copy-start | bytes 4718596 | tf_op jit(solution)/shard_map/while
  927.6 160.5 %copy-start.34 = (f32[96,192]{1,0:T(8,128)}, f32[96,192]{1,0:T(8,128)S(1)}, u32[]{:S(2)}) copy-start(f32[96,192]{1,0:T(8,128)S(1)} %select_add_fusion.15) | copy-start | bytes 221188 | tf_op jit(solution)/shard_map/while
  1088.6 66.6 %all-gather.11.cloned.1.call-start = ((), (), s32[]{:S(2)}) async-start(), calls=%async_computation.8 | async-start | bytes 3932160 | tf_op jit(solution)/shard_map/while/body/eval_jaxpr/all_gather | solution.py:171
  1088.6 38.2 %copy-start.45 = (bf16[96,192]{1,0:T(8,128)(2,1)S(1)}, bf16[96,192]{1,0:T(8,128)(2,1)}, u32[]{:S(2)}) copy-start(bf16[96,192]{1,0:T(8,128)(2,1)} %get-tuple-element.919) | copy-start | bytes 110596 | tf_op jit(solution)/shard_map/while
  1089.6 214.3 %reduce-scatter.9.cloned.1.call-start = ((), (), s32[]{:S(2)}) async-start(), calls=%async_computation.9 | async-start | bytes 7864320 | tf_op jit(solution)/shard_map/while/body/eval_jaxpr/reduce_scatter | solution.py:180
  1125.6 33.5 %copy-start.23 = (bf16[768,3,192]{0,2,1:T(8,128)(2,1)}, bf16[768,3,192]{0,2,1:T(8,128)(2,1)S(1)}, u32[]{:S(2)}) copy-start(bf16[768,3,192]{0,2,1:T(8,128)(2,1)S(1)} %copy.146) | copy-start | bytes 2654212 | tf_op jit(solution)/shard_map/while
  1194.3 109.6 %copy-start.20 = (bf16[2,192,2048]{2,1,0:T(8,128)(2,1)S(1)}, bf16[2,192,2048]{2,1,0:T(8,128)(2,1)}, u32[]{:S(2)}) copy-start(bf16[2,192,2048]{2,1,0:T(8,128)(2,1)} %copy-done.19) | copy-start | bytes 4718596 | tf_op jit(solution)/shard_map/while
  1194.3 135.8 %all-gather.15.cloned.1.call-start = ((), (), s32[]{:S(2)}) async-start(), calls=%async_computation.11 | async-start | bytes 1327104 | tf_op jit(solution)/shard_map/while/body/eval_jaxpr/all_gather | solution.py:163
  1194.9 200.6 %all-gather.13.cloned.1.call-start = ((), (), s32[]{:S(2)}) async-start(), calls=%async_computation.10 | async-start | bytes 3932160 | tf_op jit(solution)/shard_map/while/body/eval_jaxpr/all_gather | solution.py:185
  1305.7 89.8 %copy-start.58 = (f32[768]{0:T(1024)S(1)}, f32[768]{0:T(1024)}, u32[]{:S(2)}) copy-start(f32[768]{0:T(1024)} %get-tuple-element.924) | copy-start | bytes 9220 | tf_op jit(solution)/shard_map/while
  1323.8 91.1 %copy-start.31 = (f32[2048]{0:T(1024)}, f32[2048]{0:T(1024)S(1)}, u32[]{:S(2)}) copy-start(f32[2048]{0:T(1024)S(1)} %get-tuple-element.795) | copy-start | bytes 24580 | tf_op jit(solution)/shard_map/while
  1323.8 214.7 %copy-start.30 = (f32[2048]{0:T(1024)}, f32[2048]{0:T(1024)S(1)}, u32[]{:S(2)}) copy-start(f32[2048]{0:T(1024)S(1)} %get-tuple-element.796) | copy-start | bytes 24580 | tf_op jit(solution)/shard_map/while
  1325.7 94.4 %all-gather.17.cloned.1.call-start = ((), (), s32[]{:S(2)}) async-start(), calls=%async_computation.12 | async-start | bytes 1327104 | tf_op jit(solution)/shard_map/while/body/eval_jaxpr/all_gather | solution.py:164
  1326.4 212.0 %reduce-scatter.11.cloned.1.call-start = ((), (), s32[]{:S(2)}) async-start(), calls=%async_computation.13 | async-start | bytes 7864320 | tf_op jit(solution)/shard_map/while/body/eval_jaxpr/reduce_scatter | solution.py:188
  1427.5 220.3 %all-gather.19.cloned.1.call-start = ((), (), s32[]{:S(2)}) async-start(), calls=%async_computation.14 | async-start | bytes 3932160 | tf_op jit(solution)/shard_map/while/body/eval_jaxpr/all_gather | solution.py:42
  1541.1 233.9 %copy-start.4 = (f32[2048,192]{0,1:T(8,128)}, f32[2048,192]{0,1:T(8,128)S(1)}, u32[]{:S(2)}) copy-start(f32[2048,192]{0,1:T(8,128)S(1)} %get-tuple-element.798) | copy-start | bytes 4718596 | tf_op jit(solution)/shard_map/while
  1585.5 189.5 %reduce-scatter.13.cloned.1.call-start = ((), (), s32[]{:S(2)}) async-start(), calls=%async_computation.15 | async-start | bytes 7864320 | tf_op jit(solution)/shard_map/while/body/eval_jaxpr/reduce_scatter | solution.py:38
  1647.8 13.0 copy-start.57
  1665.4 199.7 %all-gather.21.cloned.1.call-start = ((), (), s32[]{:S(2)}) async-start(), calls=%async_computation.16 | async-start | bytes 3932160 | tf_op jit(solution)/shard_map/while/body/eval_jaxpr/all_gather | solution.py:42
  1803.2 153.5 %reduce-scatter.19.cloned.1.call-start = ((), (), s32[]{:S(2)}) async-start(), calls=%async_computation.19 | async-start | bytes 2654208 | tf_op jit(solution)/shard_map/while/body/eval_jaxpr/reduce_scatter | solution.py:244
  1810.1 148.4 %reduce-scatter.21.cloned.1.call-start = ((), (), s32[]{:S(2)}) async-start(), calls=%async_computation.20 | async-start | bytes 2654208 | tf_op jit(solution)/shard_map/while/body/eval_jaxpr/reduce_scatter | solution.py:245
  1817.3 175.8 %reduce-scatter.17.cloned.1.call-start = ((), (), s32[]{:S(2)}) async-start(), calls=%async_computation.18 | async-start | bytes 884736 | tf_op jit(solution)/shard_map/while/body/eval_jaxpr/reduce_scatter | solution.py:243
  1868.9 16.5 slice-start.3
  1868.9 16.4 slice-start.4
  1897.0 13.0 slice-start
  1897.0 13.0 slice-start.1
  1897.0 14.6 slice-start.2
  1937.8 100.8 %reduce-scatter.15.cloned.1.call-start = ((), (), s32[]{:S(2)}) async-start(), calls=%async_computation.17 | async-start | bytes 2654208 | tf_op jit(solution)/shard_map/while/body/eval_jaxpr/reduce_scatter | solution.py:242
  1946.6 205.2 %reduce-scatter.23.cloned.1.call-start = ((), (), s32[]{:S(2)}) async-start(), calls=%async_computation.21 | async-start | bytes 7864320 | tf_op jit(solution)/shard_map/while/body/eval_jaxpr/reduce_scatter | solution.py:38
  1953.8 198.0 %copy-start.7 = (f32[2048,192]{0,1:T(8,128)S(1)}, f32[2048,192]{0,1:T(8,128)}, u32[]{:S(2)}) copy-start(f32[2048,192]{0,1:T(8,128)} %copy-done.6) | copy-start | bytes 4718596 | tf_op jit(solution)/shard_map/while
  1955.3 37.8 %copy-start.33 = (f32[96,192]{1,0:T(8,128)S(1)}, f32[96,192]{1,0:T(8,128)}, u32[]{:S(2)}) copy-start(f32[96,192]{1,0:T(8,128)} %get-tuple-element.874) | copy-start | bytes 221188 | tf_op jit(solution)/shard_map/while
  1959.5 195.0 %copy-start.26 = (f32[96,768]{1,0:T(8,128)}, f32[96,768]{1,0:T(8,128)S(1)}, u32[]{:S(2)}) copy-start(f32[96,768]{1,0:T(8,128)S(1)} %select_add_fusion.17) | copy-start | bytes 884740 | tf_op jit(solution)/shard_map/while
  1964.9 189.6 %copy-start.21 = (bf16[2,192,2048]{2,1,0:T(8,128)(2,1)S(1)}, bf16[2,192,2048]{2,1,0:T(8,128)(2,1)}, u32[]{:S(2)}) copy-start(bf16[2,192,2048]{2,1,0:T(8,128)(2,1)} %copy-done.19) | copy-start | bytes 4718596 | tf_op jit(solution)/shard_map/while
  1994.0 160.5 %copy-start.34 = (f32[96,192]{1,0:T(8,128)}, f32[96,192]{1,0:T(8,128)S(1)}, u32[]{:S(2)}) copy-start(f32[96,192]{1,0:T(8,128)S(1)} %select_add_fusion.15) | copy-start | bytes 221188 | tf_op jit(solution)/shard_map/while
  2156.1 30.6 %copy-start.32 = (f32[2,192,2048]{2,1,0:T(8,128)S(1)}, f32[2,192,2048]{2,1,0:T(8,128)}, u32[]{:S(2)}) copy-start(f32[2,192,2048]{2,1,0:T(8,128)} %get-tuple-element.168) | copy-start | bytes 9437188
  (93 other events, 464.2 us)
Sparse Core Ops, SparseCore 0:
  22.5 66.1 all-gather.10
  128.4 109.4 reduce-scatter.8
  239.7 24.3 all-gather.14
  266.2 63.4 all-gather.12
  331.4 22.5 all-gather.16
  361.6 110.7 reduce-scatter.10
  519.3 62.2 all-gather.18
  599.2 109.4 reduce-scatter.12
  737.0 61.7 all-gather.20
  802.0 40.9 reduce-scatter.18
  846.3 42.3 reduce-scatter.20
  891.8 34.9 reduce-scatter.16
  930.1 42.3 reduce-scatter.14
  974.6 110.7 reduce-scatter.22
  1091.2 63.9 all-gather.10
  1194.5 109.4 reduce-scatter.8
  1305.6 24.3 all-gather.14
  1332.1 63.4 all-gather.12
  1397.4 22.5 all-gather.16
  1427.6 110.7 reduce-scatter.10
  1585.6 62.2 all-gather.18
  1665.5 109.4 reduce-scatter.12
  1803.2 61.7 all-gather.20
  1868.3 40.9 reduce-scatter.18
  1912.6 42.3 reduce-scatter.20
  1958.1 34.9 reduce-scatter.16
  1996.3 42.3 reduce-scatter.14
  2040.9 110.7 reduce-scatter.22
where the time goes:
time: 2200 us
  waiting for transfers between devices  1390 us (63%)
  blocking collectives  290 us (13%)
  matrix products  265 us (12%)
  other arithmetic  136 us (6%)
  local copies, waits for them, and re-layouts  90.8 us (4%)
    reduce_scatter x4, waiting for transfers between devices, input_total(): lax.psum_scatter(partial_rows, 'col', scatter_dimension=1, tiled=True)  442 us
    reduce_scatter x2, waiting for transfers between devices, micro_step(): lax.psum_scatter(contract_last(active_low, full_out), 'col', scatter_dime...  221 us
    all_gather x4, waiting for transfers between devices, grad_rows(): return lax.all_gather(values, 'col', axis=1, tiled=True)  220 us
    reduce_scatter x2, waiting for transfers between devices, micro_step(): lax.psum_scatter(contract_last(attended, full_attn_out), 'col', scatter_d...  212 us
    psum x8, blocking collectives, row_totals(): return lax.psum((jnp.sum(first, axis=1), jnp.sum(second, axis=1)), 'col')  146 us
    all_gather x2, waiting for transfers between devices, micro_step(): lax.all_gather(normed.astype(jnp.bfloat16), 'col', axis=1, tiled=True)  131 us
    reduce_scatter x2, waiting for transfers between devices, micro_step(): lax.psum_scatter(qkv_grad, ('dp', 'row'), scatter_dimension=0, tiled=True)  89.4 us
    all_gather x2, blocking collectives, micro_step(): lax.all_gather(w_qkv, ('dp', 'row'), axis=0, tiled=True)  69.8 us
  transfers between devices with their start and end apart: 28, of which 24 were waited for; matrix products, arithmetic and copies ran while one was open for 13% of the time, Pallas kernels for 0%

commit v1 on v0

v1 whole, which is shorter than its diff:
```python
import jax
import jax.numpy as jnp
from jax import lax
from jax.sharding import PartitionSpec as P

HEAD_DIM = 64
SEQ_MAX = 1024
EPSILON = 1e-12
ROWS = ("dp", "row")
ALL = ("dp", "row", "col")
BF = jnp.bfloat16
F32 = jnp.float32


def dot_nn(a, b):
    return lax.dot_general(a, b, (((1,), (0,)), ((), ())), preferred_element_type=F32)


def dot_tn(a, b):
    return lax.dot_general(a, b, (((0,), (0,)), ((), ())), preferred_element_type=F32)


def dot_nt(a, b):
    return lax.dot_general(a, b, (((1,), (1,)), ((), ())), preferred_element_type=F32)


def norm_forward(values, gain, shift):
    average = jnp.mean(values, axis=0, keepdims=True)
    centred = values - average
    spread = jnp.mean(centred * centred, axis=0, keepdims=True)
    inverse = lax.rsqrt(spread + EPSILON)
    scaled = centred * inverse
    return scaled * gain[:, None] + shift[:, None], scaled, inverse


def norm_backward(upstream, scaled, inverse, gain):
    weighted = upstream * gain[:, None]
    first = jnp.mean(weighted, axis=0, keepdims=True)
    second = jnp.mean(weighted * scaled, axis=0, keepdims=True)
    return inverse * (weighted - first - scaled * second)


def masked_scores(queries, keys, live):
    scores = jnp.einsum("hek,heq->hkq", keys, queries, preferred_element_type=F32)
    scores = scores * HEAD_DIM ** (-0.5)
    return jnp.where((live[:, None] == live[None, :])[None], scores, -1e30)


def attend_forward(queries, keys, values, live):
    scores = masked_scores(queries, keys, live)
    largest = jnp.max(scores, axis=1, keepdims=True)
    exponent = jnp.exp(scores - largest)
    total = jnp.sum(exponent, axis=1, keepdims=True)
    weights = (exponent / total).astype(BF)
    out = jnp.einsum("hek,hkq->heq", values, weights, preferred_element_type=F32)
    return out, largest + jnp.log(total)


def attend_backward(queries, keys, values, live, log_total, d_attended):
    scores = masked_scores(queries, keys, live)
    weights = jnp.exp(scores - log_total)
    d_weights = jnp.einsum("hek,heq->hkq", values, d_attended, preferred_element_type=F32)
    centre = jnp.sum(weights * d_weights, axis=1, keepdims=True)
    d_scores = (weights * (d_weights - centre)).astype(BF)
    scale = HEAD_DIM ** (-0.5)
    d_q = jnp.einsum("hek,hkq->heq", keys, d_scores, preferred_element_type=F32) * scale
    d_k = jnp.einsum("heq,hkq->hek", queries, d_scores, preferred_element_type=F32) * scale
    d_v = jnp.einsum("heq,hkq->hek", d_attended, weights.astype(BF), preferred_element_type=F32)
    return d_q, d_k, d_v


def local(
    tokens, w_qkv, bias_qv, w_attn_out, bias_attn_out, w_in, bias_in, w_out, bias_out,
    norm_gains, norm_biases, seq_lengths, seq_offsets, cotangent,
):
    cols = lax.axis_size("col")
    col = lax.axis_index("col")
    groups = lax.axis_size("dp") * lax.axis_size("row")

    def gather(shard):
        rows, width = shard.shape
        full = lax.all_gather(shard, ALL, axis=0, tiled=False)
        full = full.reshape(groups, cols, rows, width).transpose(0, 2, 1, 3)
        return full.reshape(groups * rows, cols * width)

    def scatter(grad):
        rows, width = grad.shape[0] // groups, grad.shape[1] // cols
        parts = grad.astype(BF).reshape(groups, rows, cols, width).transpose(0, 2, 1, 3)
        parts = parts.reshape(groups * cols * rows, width)
        return lax.psum_scatter(parts, ALL, scatter_dimension=0, tiled=True).astype(F32)

    d_local = w_qkv.shape[0]
    width = w_qkv.shape[2]
    d = d_local * groups
    heads = d // HEAD_DIM

    def whole_vector(v):
        return lax.all_gather(v, "col", axis=v.ndim - 1, tiled=True)

    full_q = gather(w_qkv[:, 0])
    full_k = gather(w_qkv[:, 1])
    full_v = gather(w_qkv[:, 2])
    full_qkv = jnp.concatenate([full_q, full_k, full_v], axis=1)
    full_attn_out = gather(w_attn_out)
    full_in = gather(w_in)
    full_out = gather(w_out)
    bias_qv = whole_vector(bias_qv)
    bias_attn_out = whole_vector(bias_attn_out)
    bias_in = whole_vector(bias_in)
    bias_out = whole_vector(bias_out)
    gains = whole_vector(norm_gains)
    shifts = whole_vector(norm_biases)

    def to_window(a):
        return lax.all_to_all(a, "col", split_axis=1, concat_axis=0, tiled=True)

    def from_window(a):
        return lax.all_to_all(a.astype(BF), "col", split_axis=0, concat_axis=1, tiled=True).astype(F32)

    x = to_window(tokens)
    up = to_window(cotangent)
    length = lax.dynamic_index_in_dim(seq_lengths, col, keepdims=False)
    offset = lax.dynamic_index_in_dim(seq_offsets, col, keepdims=False)
    places = jnp.arange(SEQ_MAX, dtype=jnp.int32)
    live_mask = (places >= offset) & (places < offset + length)
    live = live_mask.astype(F32)[None, :]

    proj = dot_tn(full_qkv, x)
    queries = (proj[:d] + bias_qv[0][:, None]).astype(BF).reshape(heads, HEAD_DIM, SEQ_MAX)
    keys = proj[d : 2 * d].astype(BF).reshape(heads, HEAD_DIM, SEQ_MAX)
    values = (proj[2 * d :] + bias_qv[1][:, None]).astype(BF).reshape(heads, HEAD_DIM, SEQ_MAX)
    def forward_group(group):
        return attend_forward(group[0], group[1], group[2], live_mask)

    def split_heads(a):
        return a.reshape(cols, heads // cols, *a.shape[1:])

    def join_heads(a):
        return a.reshape(heads, *a.shape[2:])

    groups_in = tuple(split_heads(a) for a in (queries, keys, values))
    attended, log_total = lax.map(forward_group, groups_in)
    attended = join_heads(attended)
    attended = attended.astype(BF).reshape(d, SEQ_MAX)
    first_sum = x.astype(F32) + dot_nn(full_attn_out, attended) + bias_attn_out[:, None]
    normed, xhat1, rstd1 = norm_forward(first_sum, gains[0], shifts[0])
    normed_low = normed.astype(BF)
    hidden = dot_tn(full_in, normed_low) + bias_in[:, None]
    cdf = 0.5 * (1.0 + lax.erf(hidden * 0.5**0.5))
    active = (hidden * cdf).astype(BF)
    slope = cdf + hidden * jnp.exp(-0.5 * hidden * hidden) * 0.3989422804014327
    second_sum = normed + dot_nn(full_out, active) + bias_out[:, None]
    result, xhat2, rstd2 = norm_forward(second_sum, gains[1], shifts[1])
    activations = from_window(result * live)

    upstream = up.astype(F32) * live
    gain_two = jnp.sum(upstream * xhat2, axis=1)
    shift_two = jnp.sum(upstream, axis=1)
    d_second = norm_backward(upstream, xhat2, rstd2, gains[1])
    g_bias_out = jnp.sum(d_second, axis=1)
    d_second_low = d_second.astype(BF)
    g_out = scatter(dot_nt(d_second_low, active))
    d_hidden = dot_tn(full_out, d_second_low) * slope
    g_bias_in = jnp.sum(d_hidden, axis=1)
    d_hidden_low = d_hidden.astype(BF)
    g_in = scatter(dot_nt(normed_low, d_hidden_low))
    d_normed = d_second + dot_nn(full_in, d_hidden_low)
    gain_one = jnp.sum(d_normed * xhat1, axis=1)
    shift_one = jnp.sum(d_normed, axis=1)
    d_first = norm_backward(d_normed, xhat1, rstd1, gains[0])
    g_bias_attn = jnp.sum(d_first, axis=1)
    d_first_low = d_first.astype(BF)
    g_attn = scatter(dot_nt(d_first_low, attended))
    d_attended = dot_tn(full_attn_out, d_first_low).astype(BF).reshape(heads, HEAD_DIM, SEQ_MAX)
    def backward_group(group):
        return attend_backward(group[0], group[1], group[2], live_mask, group[3], group[4])

    d_q, d_k, d_v = lax.map(backward_group, (*groups_in, log_total, split_heads(d_attended)))
    d_q, d_k, d_v = d_q.reshape(d, -1), d_k.reshape(d, -1), d_v.reshape(d, -1)
    g_bias_q = jnp.sum(d_q, axis=1)
    g_bias_v = jnp.sum(d_v, axis=1)
    d_proj = jnp.concatenate([d_q, d_k, d_v], axis=0).astype(BF)
    grad = dot_nt(x, d_proj).reshape(d, 3, d)
    g_qkv = jnp.stack([scatter(grad[:, k]) for k in range(3)], axis=1)
    token_grad = from_window(d_first + dot_nn(full_qkv, d_proj))

    small = jnp.stack([g_bias_q, g_bias_v, g_bias_attn, g_bias_out, gain_one, gain_two, shift_one, shift_two])
    small = jnp.concatenate([small, g_bias_in.reshape(-1, d)], axis=0)
    small = lax.psum(small, ALL)
    own = lax.dynamic_slice_in_dim(small[:8], col * width, width, axis=1)
    hid = bias_in.shape[0] // cols
    own_in = lax.dynamic_slice_in_dim(small[8:].reshape(-1), col * hid, hid, axis=0)
    return (
        activations, token_grad, g_qkv, own[0:2], g_attn, own[2], g_in, own_in, g_out, own[3],
        own[4:6], own[6:8],
    )


def solution(mesh):
    return jax.shard_map(
        local,
        mesh=mesh,
        in_specs=(
            P("col", ROWS), P(ROWS, None, "col"), P(None, "col"), P(ROWS, "col"), P("col"),
            P(ROWS, "col"), P("col"), P(ROWS, "col"), P("col"), P(None, "col"), P(None, "col"),
            P(ROWS), P(ROWS), P("col", ROWS),
        ),
        out_specs=(
            P("col", ROWS), P("col", ROWS), P(ROWS, None, "col"), P(None, "col"), P(ROWS, "col"),
            P("col"), P(ROWS, "col"), P("col"), P(ROWS, "col"), P("col"), P(None, "col"), P(None, "col"),
        ),
        check_vma=False,
    )
```

time: 2200 us -> 1160 us (0.53)
  waiting for transfers between devices: 1390 us -> 515 us
  blocking collectives: 290 us -> 187 us
  other arithmetic: 136 us -> 83.3 us
  matrix products: 265 us -> 213 us
  local copies, waits for them, and re-layouts: 90.8 us -> 119 us
    reduce_scatter x16 -> x6, waiting for transfers between devices: 1020 us -> 343 us  [scatter(): lax.psum_scatter(parts, ALL, scatter_dimension=0, tiled=True).astype(F32)]
    all_gather x12 -> x6, waiting for transfers between devices: 372 us -> 170 us  [gather(): full = lax.all_gather(shard, ALL, axis=0, tiled=False)]
    psum x9 -> x1, blocking collectives: 172 us -> 56.2 us  [local(): small = lax.psum(small, ALL)]
    dot_general x46 -> x40, matrix products: 258 us -> 213 us  [the longest x4 39.6 us: attend_backward(): jnp.einsum('hek,heq->hkq', values, d_attended, preferred_element_type=F32)]
    all_to_all x0 -> x1, blocking collectives: none -> 41.5 us  [from_window(): lax.all_to_all(a.astype(BF), 'col', split_axis=0, concat_axis=1, tiled=True)]
    all_gather x4, blocking collectives: 118 us -> 80 us  [whole_vector(): return lax.all_gather(v, 'col', axis=v.ndim - 1, tiled=True)]
    reshape x14 -> x15, local copies, waits for them, and re-layouts: 26.3 us -> 52.2 us  [the longest x3 24.1 us: scatter(): grad.astype(BF).reshape(groups, rows, cols, width).transpose(0, 2, 1, 3)]
    add x24 -> x0, other arithmetic: 24.4 us -> none  [the longest x10 12.1 us: micro_step(): small_sums = jax.tree.map(jnp.add, small_sums, small_terms)]
  transfers between devices with their start and end apart: 28 -> 15, of which waited for: 24 -> 8; matrix products, arithmetic and copies ran while one was open for 13% -> 29% of each run, Pallas kernels for 0% -> 0%
where the time goes in v1:
time: 1160 us; the launch traced here: 1150 us
  waiting for transfers between devices  515 us (44%)
  matrix products  213 us (18%)
  blocking collectives  187 us (16%)
  local copies, waits for them, and re-layouts  119 us (10%)
  other arithmetic  83.3 us (7%)
  between operations  17.4 us (1%)
  starting transfers between devices  15.2 us (1%)
    reduce_scatter x6, waiting for transfers between devices, scatter(): lax.psum_scatter(parts, ALL, scatter_dimension=0, tiled=True).astype(F32)  343 us
    all_gather x6, waiting for transfers between devices, gather(): full = lax.all_gather(shard, ALL, axis=0, tiled=False)  170 us
    all_gather x4, blocking collectives, whole_vector(): return lax.all_gather(v, 'col', axis=v.ndim - 1, tiled=True)  80 us
    psum x1, blocking collectives, local(): small = lax.psum(small, ALL)  56.2 us
    all_to_all x1, blocking collectives, from_window(): lax.all_to_all(a.astype(BF), 'col', split_axis=0, concat_axis=1, tiled=True)  41.5 us
    dot_general x4, matrix products, attend_backward(): jnp.einsum('hek,heq->hkq', values, d_attended, preferred_element_type=F32)  39.6 us
    dot_general x4, matrix products, dot_tn(): lax.dot_general(a, b, (((0,), (0,)), ((), ())), preferred_element_type=F32)  32.8 us
    dot_general x4, matrix products, dot_nt(): lax.dot_general(a, b, (((1,), (1,)), ((), ())), preferred_element_type=F32)  32.2 us
  transfers between devices with their start and end apart: 15, of which 8 were waited for; matrix products, arithmetic and copies ran while one was open for 29% of the time, Pallas kernels for 0%

profile of v1, /device:TPU:0, one launch (start us, length us, event | category | flops | bytes accessed | tf_op | source)
XLA Modules:
  0.0 1150.8 jit_solution(17955930172822750493)
XLA Ops:
  14.2 6.3 all-to-all-start
  22.3 42.3 %all-gather.6 = f32[4,192,2]{1,2,0:T(2,128)S(1)} all-gather(f32[1,192,2]{1,2,0:T(2,128)S(1)} %bitcast.342), channel_id=1, replica_groups=mesh['dp'=2,'row'=4,'col'=4] {'col'}, dimensions={0}, use_global_device_ids=true | all-gather | bytes 7680 | tf_op jit(solution)/shard_map/all_gather | solution.py:98
  67.3 11.9 %all-gather.7 = f32[4,192,2]{1,2,0:T(2,128)S(1)} all-gather(f32[1,192,2]{1,2,0:T(2,128)S(1)} %bitcast.343), channel_id=1, replica_groups=mesh['dp'=2,'row'=4,'col'=4] {'col'}, dimensions={0}, use_global_device_ids=true | all-gather | bytes 7680 | tf_op jit(solution)/shard_map/all_gather | solution.py:98
  79.3 11.9 %all-gather.8 = f32[4,192,2]{1,2,0:T(2,128)S(1)} all-gather(f32[1,192,2]{1,2,0:T(2,128)S(1)} %bitcast.344), channel_id=1, replica_groups=mesh['dp'=2,'row'=4,'col'=4] {'col'}, dimensions={0}, use_global_device_ids=true | all-gather | bytes 7680 | tf_op jit(solution)/shard_map/all_gather | solution.py:98
  97.0 9.1 all-reduce.2
  106.1 13.8 %all-gather.9 = f32[4,1,768]{2,1,0:T(1,128)} all-gather(f32[1,1,768]{2,1,0:T(1,128)S(1)} %reshape.351), channel_id=1, replica_groups=mesh['dp'=2,'row'=4,'col'=4] {'col'}, dimensions={0}, use_global_device_ids=true | all-gather | bytes 15360 | tf_op jit(solution)/shard_map/all_gather | solution.py:98
  125.1 17.5 %all-gather.19.cloned.1.call-done = bf16[3072,1,192]{2,0,1:T(8,128)(2,1)} async-done(((bf16[96,1,192]{2,0,1:T(8,128)(2,1)}), bf16[3072,1,192]{2,0,1:T(8,128)(2,1)}) %all-gather.19.cloned.1.call-update) | async-done | bytes 1179664 | tf_op jit(solution)/shard_map/all_gather | solution.py:82
  146.8 53.2 %all-gather.21.cloned.1.call-done = bf16[3072,1,192]{2,0,1:T(8,128)(2,1)} async-done(((bf16[96,1,192]{2,0,1:T(8,128)(2,1)}), bf16[3072,1,192]{2,0,1:T(8,128)(2,1)}) %all-gather.21.cloned.1.call-update) | async-done | bytes 1179664 | tf_op jit(solution)/shard_map/all_gather | solution.py:82
  204.3 52.5 %all-gather.23.cloned.1.call-done = bf16[3072,192]{1,0:T(8,128)(2,1)} async-done(((bf16[96,192]{1,0:T(8,128)(2,1)}), bf16[3072,192]{1,0:T(8,128)(2,1)}) %all-gather.23.cloned.1.call-update) | async-done | bytes 1179664 | tf_op jit(solution)/shard_map/all_gather | solution.py:82
  264.8 4.4 all-to-all-start.2
  269.7 6.6 fusion.104
  279.9 60.7 %while.30 = (s32[]{:T(128)}, bf16[4,3,64,1024]{3,2,1,0:T(8,128)(2,1)}, f32[4,3,1,1024]{3,1,2,0:T(4,128)S(1)}, bf16[4,3,64,1024]{3,2,1,0:T(8,128)(2,1)}, bf16[4,3...) while((s32[]{:T(128)}, ...), condition=%wide.region_3.4_spmd.clone.clone, body=%wide.region_0.3_spmd.clone.sunk.clone | while | flops 844103680 | bytes 48218236 | solution.py:142
  281.2 4.2 fusion.161
  285.4 3.9 fusion.162
  289.3 5.7 fusion.163
  296.3 4.2 fusion.161
  300.5 3.9 fusion.162
  304.4 5.7 fusion.163
  311.4 4.2 fusion.161
  315.6 3.9 fusion.162
  319.5 5.7 fusion.163
  326.5 4.2 fusion.161
  330.8 3.9 fusion.162
  334.7 5.7 fusion.163
  340.6 3.8 fusion.101
  348.2 6.0 copy.63
  354.2 3.2 copy.78
  357.4 46.4 %all-gather.27.cloned.1.call-done = bf16[3072,768]{1,0:T(8,128)(2,1)} async-done(((bf16[96,768]{1,0:T(8,128)(2,1)}), bf16[3072,768]{1,0:T(8,128)(2,1)}) %all-gather.27.cloned.1.call-update) | async-done | bytes 4718608 | tf_op jit(solution)/shard_map/all_gather | solution.py:82
  403.8 6.1 copy.64
  411.3 10.2 fusion.67
  421.5 5.3 fusion.102
  430.6 4.5 fusion.92
  435.1 13.4 %fusion.103 = (f32[3072]{0:T(1024)}, bf16[3072,1024]{0,1:T(8,128)(2,1)S(1)}) fusion(f32[1024,3072]{1,0:T(8,128)} %get-tuple-element.240, f32[3072]{0:T(1024)S(1)} %bitcast.341, bf16[768,3072]{1,0:T(8,128)(2,1)S(1)} %bitcast.316, f32[768,1024]{1,0:T(8,128)S(1)} %get-tuple-element.210), kind=kOutput, calls=%fused_computation.166 | convolution fusion | flops 4870370304 | bytes 26763264 | tf_op jit(solution)/shard_map/dot_general | solution.py:20
  448.6 6.6 multiply_reduce_fusion.2
  462.0 4.5 reshape.316
  469.6 123.7 %while.31 = (s32[]{:T(128)}, f32[4,3,64,1024]{3,2,1,0:T(8,128)}, bf16[4,3,64,1024]{3,2,1,0:T(8,128)(2,1)}, f32[4,3,64,1024]{3,2,1,0:T(8,128)}, bf16[4,3,64,1024]...) while((s32[]{:T(128)}, f32[4,3,64,1024]{3,2,1,0:T(8,128)}, ...), condition=%wide.region_14.15_spmd.clone.clone, body=%wide.region_12.14_spmd.clone.sunk.clone | while | flops 2061893632 | bytes 116354232 | solution.py:178
  472.9 9.9 multiply_reduce_fusion.10
  482.8 7.0 multiply_convert_fusion.4
  495.2 5.5 fusion.176
  503.8 9.9 multiply_reduce_fusion.10
  513.7 7.0 multiply_convert_fusion.4
  526.1 5.5 fusion.176
  534.7 9.9 multiply_reduce_fusion.10
  544.6 7.0 multiply_convert_fusion.4
  556.9 5.5 fusion.176
  565.5 9.9 multiply_reduce_fusion.10
  575.4 6.9 multiply_convert_fusion.4
  587.6 5.4 fusion.176
  593.3 5.6 fusion.95
  599.0 9.9 convolution_convert_fusion.2
  624.8 9.9 convolution_convert_fusion
  634.7 9.8 reshape.321
  644.5 5.4 copy.73
  651.9 9.9 convolution_convert_fusion.1
  661.7 9.8 reshape.318
  671.5 5.5 copy.72
  678.9 7.4 add_convert_fusion
  686.4 41.5 %all_to_all.58 = bf16[4,192,1024]{2,1,0:T(8,128)(2,1)S(1)} all-to-all(bf16[4,192,1024]{2,1,0:T(8,128)(2,1)S(1)} %bitcast.333), channel_id=1, replica_groups=mesh['dp'=2,'row'=4,'col'=4] {'col'}, dimensions={0} | all-to-all | bytes 3145728 | tf_op jit(solution)/shard_map/all_to_all | solution.py:118
  727.8 3.6 all-to-all-start.1
  731.9 56.2 %psum.7 = f32[12,768]{1,0:T(8,128)S(1)} all-reduce(f32[12,768]{1,0:T(8,128)S(1)} %concatenate.12), channel_id=1, replica_groups=mesh['dp'=2,'row'=4,'col'=4] {'dp','row','col'}, use_global_device_ids=true, to_apply=%region_27.28 | all-reduce | flops 9216 | bytes 73728 | tf_op jit(solution)/shard_map/psum | solution.py:189
  791.5 24.2 %reduce-scatter.9.cloned.1.call-done = bf16[96,192]{1,0:T(8,128)(2,1)} async-done(((bf16[3072,192]{1,0:T(8,128)(2,1)}), bf16[96,192]{1,0:T(8,128)(2,1)}) %reduce-scatter.9.cloned.1.call-update) | async-done | bytes 36880 | tf_op jit(solution)/shard_map/reduce_scatter | solution.py:90
  815.7 102.2 %reduce-scatter.11.cloned.1.call-done = bf16[96,192]{1,0:T(8,128)(2,1)} async-done(((bf16[3072,192]{1,0:T(8,128)(2,1)}), bf16[96,192]{1,0:T(8,128)(2,1)}) %reduce-scatter.11.cloned.1.call-update) | async-done | bytes 36880 | tf_op jit(solution)/shard_map/reduce_scatter | solution.py:90
  924.1 106.0 %reduce-scatter.17.cloned.1.call-done = bf16[96,768]{1,0:T(8,128)(2,1)} async-done(((bf16[3072,768]{1,0:T(8,128)(2,1)}), bf16[96,768]{1,0:T(8,128)(2,1)}) %reduce-scatter.17.cloned.1.call-update) | async-done | bytes 147472 | tf_op jit(solution)/shard_map/reduce_scatter | solution.py:90
  1031.7 110.2 %reduce-scatter.15.cloned.1.call-done = bf16[96,768]{1,0:T(8,128)(2,1)} async-done(((bf16[3072,768]{1,0:T(8,128)(2,1)}), bf16[96,768]{1,0:T(8,128)(2,1)}) %reduce-scatter.15.cloned.1.call-update) | async-done | bytes 147472 | tf_op jit(solution)/shard_map/reduce_scatter | solution.py:90
  (286 shorter events, 131.5 us)
Async XLA Ops:
  7.2 114.6 %all-gather.17.cloned.1.call-start = ((), (), s32[]{:S(2)}) async-start(), calls=%async_computation.16 | async-start | bytes 1622016 | tf_op jit(solution)/shard_map/all_gather | solution.py:82
  8.8 133.9 %all-gather.19.cloned.1.call-start = ((), (), s32[]{:S(2)}) async-start(), calls=%async_computation.17 | async-start | bytes 1622016 | tf_op jit(solution)/shard_map/all_gather | solution.py:82
  9.5 190.5 %all-gather.21.cloned.1.call-start = ((), (), s32[]{:S(2)}) async-start(), calls=%async_computation.18 | async-start | bytes 1622016 | tf_op jit(solution)/shard_map/all_gather | solution.py:82
  10.2 246.5 %all-gather.23.cloned.1.call-start = ((), (), s32[]{:S(2)}) async-start(), calls=%async_computation.19 | async-start | bytes 1622016 | tf_op jit(solution)/shard_map/all_gather | solution.py:82
  10.8 337.4 %all-gather.25.cloned.1.call-start = ((), (), s32[]{:S(2)}) async-start(), calls=%async_computation.20 | async-start | bytes 4866048 | tf_op jit(solution)/shard_map/all_gather | solution.py:82
  11.4 9.7 copy-start.49
  11.4 10.3 copy-start.50
  11.4 10.9 copy-start.42
  14.2 250.7 %all-to-all-start = ((bf16[192,4,1024]{2,0,1:T(8,128)(2,1)}), bf16[192,4,1024]{2,0,1:T(8,128)(2,1)}, u32[]{:S(2)}, u32[]{:S(2)}) async-start(bf16[192,4,1024]{2,0,1:T(8,128)(2,1)} %bitcast.234), calls=%async_computation | async-start | bytes 3145728 | tf_op jit(solution)/shard_map/all_to_all | solution.py:115
  20.5 46.8 %copy-start.43 = (f32[2,192]{1,0:T(2,128)S(1)}, f32[2,192]{1,0:T(2,128)}, u32[]{:S(2)}) copy-start(f32[2,192]{1,0:T(2,128)} %param.27) | copy-start | bytes 4612
  20.5 58.8 %copy-start.44 = (f32[2,192]{1,0:T(2,128)S(1)}, f32[2,192]{1,0:T(2,128)}, u32[]{:S(2)}) copy-start(f32[2,192]{1,0:T(2,128)} %param.28) | copy-start | bytes 4612
  20.5 70.9 %copy-start.39 = (f32[768]{0:T(1024)S(1)}, f32[768]{0:T(1024)}, u32[]{:S(2)}) copy-start(f32[768]{0:T(1024)} %param.24) | copy-start | bytes 9220
  20.5 70.9 %copy-start.17 = (bf16[192,4096]{1,0:T(8,128)(2,1)S(1)}, bf16[192,4096]{1,0:T(8,128)(2,1)}, u32[]{:S(2)}) copy-start(bf16[192,4096]{1,0:T(8,128)(2,1)} %param.31) | copy-start | bytes 4718596
  20.5 383.3 %all-gather.27.cloned.1.call-start = ((), (), s32[]{:S(2)}) async-start(), calls=%async_computation.21 | async-start | bytes 4866048 | tf_op jit(solution)/shard_map/all_gather | solution.py:82
  66.1 29.2 %copy-start.51 = (u32[32]{0:T(128)S(1)}, u32[32]{0:T(128)}, u32[]{:S(2)}) copy-start(u32[32]{0:T(128)} %constant.91) | copy-start | bytes 388
  66.1 30.4 %copy-start.45 = (f32[192]{0:T(256)S(1)}, f32[192]{0:T(256)}, u32[]{:S(2)}) copy-start(f32[192]{0:T(256)} %param.22) | copy-start | bytes 2308
  66.1 30.7 %copy-start.46 = (f32[192]{0:T(256)S(1)}, f32[192]{0:T(256)}, u32[]{:S(2)}) copy-start(f32[192]{0:T(256)} %param.26) | copy-start | bytes 2308
  93.3 28.5 %copy-start.21 = (f32[768]{0:T(1024)}, f32[768]{0:T(1024)S(1)}, u32[]{:S(2)}) copy-start(f32[768]{0:T(1024)S(1)} %get-tuple-element.163) | copy-start | bytes 9220
  260.9 2.8 copy-start.11
  264.8 80.0 %all-to-all-start.2 = ((bf16[192,4,1024]{2,0,1:T(8,128)(2,1)}), bf16[192,4,1024]{2,0,1:T(8,128)(2,1)}, u32[]{:S(2)}, u32[]{:S(2)}) async-start(bf16[192,4,1024]{2,0,1:T(8,128)(2,1)} %bitcast.233), calls=%async_computation.2 | async-start | bytes 3145728 | tf_op jit(solution)/shard_map/all_to_all | solution.py:115
  269.2 520.9 %reduce-scatter.13.cloned.1.call-start = ((), (), s32[]{:S(2)}) async-start(), calls=%async_computation.13 | async-start | bytes 1622016 | tf_op jit(solution)/shard_map/reduce_scatter | solution.py:90
  279.8 60.7 %copy-start.48 = (f32[768]{0:T(1024)S(1)}, f32[768]{0:T(1024)}, u32[]{:S(2)}) copy-start(f32[768]{0:T(1024)} %get-tuple-element.207) | copy-start | bytes 9220
  281.1 4.2 copy-start
  296.3 4.2 copy-start
  311.4 4.2 copy-start
  326.5 4.2 copy-start
  344.4 110.7 %copy-start.3 = (f32[768,1024]{1,0:T(8,128)}, f32[768,1024]{1,0:T(8,128)S(1)}, u32[]{:S(2)}) copy-start(f32[768,1024]{1,0:T(8,128)S(1)} %get-tuple-element.238) | copy-start | bytes 9437188
  344.4 110.7 %copy-start.23 = (f32[1024]{0:T(1024)}, f32[1024]{0:T(1024)S(1)}, u32[]{:S(2)}) copy-start(f32[1024]{0:T(1024)S(1)} %broadcast_multiply_fusion.5) | copy-start | bytes 12292
  344.8 110.3 %copy-start.32 = (f32[1024]{0:T(1024)}, f32[1024]{0:T(1024)S(1)}, u32[]{:S(2)}) copy-start(f32[1024]{0:T(1024)S(1)} %add_rsqrt_fusion.1) | copy-start | bytes 12292
  403.8 7.4 slice-start
  411.3 10.2 copy-start.47
  421.5 5.3 copy-start.52
  427.2 3.4 copy-start.27
  435.1 13.4 %copy-start.13 = (f32[768,1024]{1,0:T(8,128)}, f32[768,1024]{1,0:T(8,128)S(1)}, u32[]{:S(2)}) copy-start(f32[768,1024]{1,0:T(8,128)S(1)} %get-tuple-element.210) | copy-start | bytes 9437188
  448.6 6.6 copy-start.53
  456.9 2.6 copy-start.12
  456.9 2.6 copy-start.19
  462.0 7.5 copy-start.1
  462.0 7.5 copy-start.2
  469.5 322.0 %reduce-scatter.7.cloned.1.call-start = ((), (), s32[]{:S(2)}) async-start(), calls=%async_computation.10 | async-start | bytes 1622016 | tf_op jit(solution)/shard_map/reduce_scatter | solution.py:90
  489.8 2.1 copy-start.6
  520.7 2.1 copy-start.6
  551.5 2.1 copy-start.6
  582.3 2.1 copy-start.6
  593.3 5.7 copy-start.8
  598.9 9.9 copy-start.14
  599.0 9.9 copy-start.16
  615.7 200.0 %reduce-scatter.9.cloned.1.call-start = ((), (), s32[]{:S(2)}) async-start(), calls=%async_computation.11 | async-start | bytes 1622016 | tf_op jit(solution)/shard_map/reduce_scatter | solution.py:90
  620.9 297.0 %reduce-scatter.11.cloned.1.call-start = ((), (), s32[]{:S(2)}) async-start(), calls=%async_computation.12 | async-start | bytes 1622016 | tf_op jit(solution)/shard_map/reduce_scatter | solution.py:90
  624.8 405.3 %reduce-scatter.17.cloned.1.call-start = ((), (), s32[]{:S(2)}) async-start(), calls=%async_computation.15 | async-start | bytes 4866048 | tf_op jit(solution)/shard_map/reduce_scatter | solution.py:90
  649.9 1.9 copy-start.4
  649.9 1.9 copy-start.24
  649.9 1.9 copy-start.26
  649.9 1.9 copy-start.33
  649.9 1.9 copy-start.38
  650.0 491.9 %reduce-scatter.15.cloned.1.call-start = ((), (), s32[]{:S(2)}) async-start(), calls=%async_computation.14 | async-start | bytes 4866048 | tf_op jit(solution)/shard_map/reduce_scatter | solution.py:90
  686.3 45.1 %copy-start.28 = (f32[4,192]{1,0:T(4,128)S(1)}, f32[4,192]{1,0:T(4,128)}, u32[]{:S(2)}) copy-start(f32[4,192]{1,0:T(4,128)} %get-tuple-element.161) | copy-start | bytes 9220
  686.3 45.4 %copy-start.31 = (f32[768]{0:T(1024)S(1)}, f32[768]{0:T(1024)}, u32[]{:S(2)}) copy-start(f32[768]{0:T(1024)} %get-tuple-element.211) | copy-start | bytes 9220
  686.3 45.4 %copy-start.41 = (f32[768]{0:T(1024)S(1)}, f32[768]{0:T(1024)}, u32[]{:S(2)}) copy-start(f32[768]{0:T(1024)} %get-tuple-element.155) | copy-start | bytes 9220
  686.3 45.4 %copy-start.40 = (f32[768]{0:T(1024)S(1)}, f32[768]{0:T(1024)}, u32[]{:S(2)}) copy-start(f32[768]{0:T(1024)} %get-tuple-element.160) | copy-start | bytes 9220
  686.3 45.4 %copy-start.35 = (f32[3072]{0:T(1024)S(1)}, f32[3072]{0:T(1024)}, u32[]{:S(2)}) copy-start(f32[3072]{0:T(1024)} %get-tuple-element.244) | copy-start | bytes 36868
  686.3 45.4 %copy-start.30 = (f32[768]{0:T(1024)S(1)}, f32[768]{0:T(1024)}, u32[]{:S(2)}) copy-start(f32[768]{0:T(1024)} %get-tuple-element.209) | copy-start | bytes 9220
  686.3 45.4 %copy-start.29 = (f32[768]{0:T(1024)S(1)}, f32[768]{0:T(1024)}, u32[]{:S(2)}) copy-start(f32[768]{0:T(1024)} %get-tuple-element.157) | copy-start | bytes 9220
  727.8 194.0 %all-to-all-start.1 = ((bf16[4,192,1024]{2,1,0:T(8,128)(2,1)}), bf16[4,192,1024]{2,1,0:T(8,128)(2,1)S(1)}, u32[]{:S(2)}, u32[]{:S(2)}) async-start(bf16[4,192,1024]{2,1,0:T(8,128)(2,1)} %bitcast.35), calls=%async_computation.1 | async-start | bytes 3145728 | tf_op jit(solution)/shard_map/all_to_all | solution.py:118
  (16 other events, 19.9 us)
Sparse Core Ops, SparseCore 0:
  11.4 73.7 all-gather.16
  88.7 53.9 all-gather.18
  146.1 53.8 all-gather.20
  202.8 53.8 all-gather.22
  259.4 79.7 all-gather.24
  341.9 61.8 all-gather.26
  469.6 96.1 reduce-scatter.12
  615.8 98.5 reduce-scatter.6
  719.7 96.0 reduce-scatter.8
  820.8 97.0 reduce-scatter.10
  923.4 106.5 reduce-scatter.16
  1035.4 106.4 reduce-scatter.14

commit v2 on v1

v2 whole, which is shorter than its diff:
```python
import jax
import jax.numpy as jnp
from jax import lax
from jax.experimental import pallas as pl
from jax.experimental.pallas import tpu as pltpu
from jax.sharding import PartitionSpec as P

HEAD_DIM = 64
SEQ_MAX = 1024
EPSILON = 1e-12
ROWS = ("dp", "row")
ALL = ("dp", "row", "col")
OWNERS = ("col", "dp", "row")
BF = jnp.bfloat16
F32 = jnp.float32
LOG2E = 1.4426950408889634
SCALE = HEAD_DIM ** (-0.5)
QBLOCK = 256
EXTRA = 16


def dot_nn(a, b):
    return lax.dot_general(a, b, (((1,), (0,)), ((), ())), preferred_element_type=F32)


def dot_tn(a, b):
    return lax.dot_general(a, b, (((0,), (0,)), ((), ())), preferred_element_type=F32)


def dot_nt(a, b):
    return lax.dot_general(a, b, (((1,), (1,)), ((), ())), preferred_element_type=F32)


def mean_rows(v):
    return jnp.mean(v, axis=0, keepdims=True)


def norm_forward(values, gain, shift):
    centred = values - mean_rows(values)
    inverse = lax.rsqrt(mean_rows(centred * centred) + EPSILON)
    scaled = centred * inverse
    return scaled * gain[:, None] + shift[:, None], scaled, inverse


def norm_backward(upstream, scaled, inverse, gain):
    weighted = upstream * gain[:, None]
    return inverse * (weighted - mean_rows(weighted) - scaled * mean_rows(weighted * scaled))


def stack_rows(rows, width):
    place = lax.broadcasted_iota(jnp.int32, (EXTRA, width), 0)
    out = jnp.zeros((EXTRA, width), F32)
    for i, row in enumerate(rows):
        out = jnp.where(place == i, row, out)
    return out.astype(BF)


def three_parts(row):
    high = row.astype(BF).astype(F32)
    middle = (row - high).astype(BF).astype(F32)
    return high, middle, row - high - middle


def attend_forward_kernel(q_ref, k_ref, v_ref, mask_ref, out_ref, total_ref):
    seq = q_ref.shape[-1]
    one = jnp.ones((1, seq), F32)
    keys = jnp.concatenate([k_ref[0, 0, 0], stack_rows([mask_ref[...]], seq)], axis=0).T
    queries = jnp.concatenate([q_ref[0, 0, 0], stack_rows([one], seq)], axis=0)
    values = v_ref[0, 0, 0]
    for j in range(seq // QBLOCK):
        cols = slice(j * QBLOCK, (j + 1) * QBLOCK)
        scores = dot_nn(keys, queries[:, cols])
        largest = jnp.max(scores, axis=0, keepdims=True)
        exponent = jnp.exp2((scores - largest) * (SCALE * LOG2E))
        total = jnp.sum(exponent, axis=0, keepdims=True)
        weights = (exponent * (1.0 / total)).astype(BF)
        out_ref[0, :, cols] = dot_nn(values, weights).astype(BF)
        total_ref[0, :, cols] = largest + jnp.log(total) * (1.0 / SCALE)


def attend_backward_kernel(
    q_ref, k_ref, v_ref, mask_ref, out_ref, total_ref, up_ref, grad_ref, bias_ref, dk_ref, dv_ref
):
    seq = q_ref.shape[-1]
    one = jnp.ones((1, seq), F32)
    keys = k_ref[0, 0, 0]
    queries = q_ref[0, 0, 0]
    up = up_ref[0]
    delta = jnp.sum(up.astype(F32) * out_ref[0].astype(F32), axis=0, keepdims=True)
    key_side = jnp.concatenate([keys, stack_rows([mask_ref[...], one, one, one], seq)], axis=0).T
    value_side = jnp.concatenate([v_ref[0, 0, 0], stack_rows([one, one, one], seq)], axis=0).T
    query_side = jnp.concatenate([queries, stack_rows([one, *three_parts(-total_ref[0])], seq)], axis=0)
    up_side = jnp.concatenate([up, stack_rows(three_parts(-delta), seq)], axis=0)
    lanes = 128
    sum_q = jnp.zeros((HEAD_DIM, lanes), F32)
    for j in range(seq // QBLOCK):
        cols = slice(j * QBLOCK, (j + 1) * QBLOCK)
        weights = jnp.exp2(dot_nn(key_side, query_side[:, cols]) * (SCALE * LOG2E))
        d_scores = (weights * dot_nn(value_side, up_side[:, cols])).astype(BF)
        d_q = dot_nn(keys, d_scores) * SCALE
        for part in range(QBLOCK // lanes):
            sum_q += d_q[:, part * lanes : (part + 1) * lanes]
        grad_ref[0, 0, 0, :, cols] = d_q.astype(BF)
        d_k = dot_nt(queries[:, cols], d_scores)
        d_v = dot_nt(up[:, cols], weights.astype(BF))
        if j == 0:
            dk_ref[...] = d_k
            dv_ref[...] = d_v
        else:
            dk_ref[...] += d_k
            dv_ref[...] += d_v
    grad_ref[0, 1, 0] = (dk_ref[...] * SCALE).astype(BF)
    grad_ref[0, 2, 0] = dv_ref[...].astype(BF)
    bias_ref[0, 0] = sum_q
    sum_v = jnp.zeros((HEAD_DIM, lanes), F32)
    for part in range(seq // lanes):
        sum_v += dv_ref[:, part * lanes : (part + 1) * lanes]
    bias_ref[0, 1] = sum_v


def projection_spec(which, per_col, seq):
    return pl.BlockSpec((1, 1, 1, HEAD_DIM, seq), lambda h: (h // per_col, which, h % per_col, 0, 0))


def head_spec(rows, seq):
    return pl.BlockSpec((1, rows, seq), lambda h: (h, 0, 0))


def attend_forward(qkv, mask):
    cols, _, per_col, _, seq = qkv.shape
    heads = cols * per_col
    return pl.pallas_call(
        attend_forward_kernel,
        grid=(heads,),
        in_specs=[projection_spec(k, per_col, seq) for k in range(3)]
        + [pl.BlockSpec((1, seq), lambda h: (0, 0))],
        out_specs=[head_spec(HEAD_DIM, seq), head_spec(1, seq)],
        out_shape=[
            jax.ShapeDtypeStruct((heads, HEAD_DIM, seq), BF),
            jax.ShapeDtypeStruct((heads, 1, seq), F32),
        ],
        cost_estimate=pl.CostEstimate(
            flops=heads * seq * seq * HEAD_DIM * 16, bytes_accessed=heads * seq * HEAD_DIM * 8,
            transcendentals=heads * seq * seq,
        ),
        name="attend_forward",
    )(qkv, qkv, qkv, mask)


def attend_backward(qkv, mask, attended, total, d_attended):
    cols, _, per_col, _, seq = qkv.shape
    heads = cols * per_col
    return pl.pallas_call(
        attend_backward_kernel,
        grid=(heads,),
        in_specs=[projection_spec(k, per_col, seq) for k in range(3)]
        + [pl.BlockSpec((1, seq), lambda h: (0, 0))]
        + [head_spec(HEAD_DIM, seq), head_spec(1, seq), head_spec(HEAD_DIM, seq)],
        out_specs=[
            pl.BlockSpec((1, 3, 1, HEAD_DIM, seq), lambda h: (h // per_col, 0, h % per_col, 0, 0)),
            pl.BlockSpec((1, 2, HEAD_DIM, 128), lambda h: (h, 0, 0, 0)),
        ],
        out_shape=[
            jax.ShapeDtypeStruct(qkv.shape, BF),
            jax.ShapeDtypeStruct((heads, 2, HEAD_DIM, 128), F32),
        ],
        scratch_shapes=[pltpu.VMEM((HEAD_DIM, seq), F32), pltpu.VMEM((HEAD_DIM, seq), F32)],
        cost_estimate=pl.CostEstimate(
            flops=heads * seq * seq * HEAD_DIM * 40, bytes_accessed=heads * seq * HEAD_DIM * 16,
            transcendentals=heads * seq * seq,
        ),
        name="attend_backward",
    )(qkv, qkv, qkv, mask, attended, total, d_attended)


def local(
    tokens, w_qkv, bias_qv, w_attn_out, bias_attn_out, w_in, bias_in, w_out, bias_out,
    norm_gains, norm_biases, seq_lengths, seq_offsets, cotangent,
):
    cols = lax.axis_size("col")
    col = lax.axis_index("col")
    rows, _, width = w_qkv.shape
    groups = lax.axis_size("dp") * lax.axis_size("row")
    d = rows * groups
    heads = d // HEAD_DIM
    hid = w_in.shape[1]

    def gather(shard):
        return lax.all_gather(shard, OWNERS, axis=0, tiled=True).reshape(cols, d, shard.shape[1])

    def scatter(grad):
        parts = grad.astype(BF).reshape(cols * d, grad.shape[2])
        return lax.psum_scatter(parts, OWNERS, scatter_dimension=0, tiled=True).astype(F32)

    w_mix = gather(jnp.concatenate([w_qkv.reshape(rows, 3 * width), w_attn_out], axis=1))
    full_in = gather(w_in)
    full_out = gather(w_out)
    full_qkv = w_mix[:, :, : 3 * width]
    full_attn = w_mix[:, :, 3 * width :]

    vectors = jnp.concatenate(
        [bias_qv, bias_attn_out[None], bias_out[None], norm_gains, norm_biases, bias_in.reshape(-1, width)], axis=0
    )
    vectors = lax.all_gather(vectors, "col", axis=0, tiled=False)
    bias_q, bias_v = vectors[:, 0], vectors[:, 1]
    bias_attn_out, bias_out = vectors[:, 2].reshape(d), vectors[:, 3].reshape(d)
    gains = [vectors[:, 4].reshape(d), vectors[:, 5].reshape(d)]
    shifts = [vectors[:, 6].reshape(d), vectors[:, 7].reshape(d)]
    bias_in = vectors[:, 8:].reshape(cols, hid)

    def to_window(a):
        return lax.all_to_all(a, "col", split_axis=1, concat_axis=0, tiled=True)

    def from_window(a):
        return lax.all_to_all(a.astype(BF), "col", split_axis=0, concat_axis=1, tiled=True).astype(F32)

    x = to_window(tokens)
    up = to_window(cotangent)
    length = lax.dynamic_index_in_dim(seq_lengths, col, keepdims=False)
    offset = lax.dynamic_index_in_dim(seq_offsets, col, keepdims=False)
    places = lax.broadcasted_iota(jnp.int32, (1, SEQ_MAX), 1)
    live_mask = (places >= offset) & (places < offset + length)
    live = live_mask.astype(F32)
    key_mask = jnp.where(live_mask, 0.0, -1e30).astype(F32)

    proj = jnp.einsum("cdn,dt->cnt", full_qkv, x, preferred_element_type=F32)
    shift_qkv = jnp.concatenate([bias_q, jnp.zeros_like(bias_q), bias_v], axis=1)
    qkv = (proj + shift_qkv[:, :, None]).astype(BF).reshape(cols, 3, width // HEAD_DIM, HEAD_DIM, SEQ_MAX)
    attended, total = attend_forward(qkv, key_mask)
    attended_cols = attended.reshape(cols, width, SEQ_MAX)
    first_sum = (
        x.astype(F32) + jnp.einsum("cde,cet->dt", full_attn, attended_cols, preferred_element_type=F32)
        + bias_attn_out[:, None]
    )
    normed, xhat1, rstd1 = norm_forward(first_sum, gains[0], shifts[0])
    normed_low = normed.astype(BF)
    hidden = jnp.einsum("cdf,dt->cft", full_in, normed_low, preferred_element_type=F32) + bias_in[:, :, None]
    cdf = 0.5 * (1.0 + lax.erf(hidden * 0.5**0.5))
    active = (hidden * cdf).astype(BF)
    slope = cdf + hidden * jnp.exp(-0.5 * hidden * hidden) * 0.3989422804014327
    second_sum = (
        normed + jnp.einsum("cdf,cft->dt", full_out, active, preferred_element_type=F32) + bias_out[:, None]
    )
    result, xhat2, rstd2 = norm_forward(second_sum, gains[1], shifts[1])
    activations = from_window(result * live)

    upstream = up.astype(F32) * live
    gain_two = jnp.sum(upstream * xhat2, axis=1)
    shift_two = jnp.sum(upstream, axis=1)
    d_second = norm_backward(upstream, xhat2, rstd2, gains[1])
    g_bias_out = jnp.sum(d_second, axis=1)
    d_second_low = d_second.astype(BF)
    g_out = scatter(jnp.einsum("dt,cft->cdf", d_second_low, active, preferred_element_type=F32))
    d_hidden = jnp.einsum("cdf,dt->cft", full_out, d_second_low, preferred_element_type=F32) * slope
    g_bias_in = jnp.sum(d_hidden, axis=2)
    d_hidden_low = d_hidden.astype(BF)
    g_in = scatter(jnp.einsum("dt,cft->cdf", normed_low, d_hidden_low, preferred_element_type=F32))
    d_normed = d_second + jnp.einsum("cdf,cft->dt", full_in, d_hidden_low, preferred_element_type=F32)
    gain_one = jnp.sum(d_normed * xhat1, axis=1)
    shift_one = jnp.sum(d_normed, axis=1)
    d_first = norm_backward(d_normed, xhat1, rstd1, gains[0])
    g_bias_attn = jnp.sum(d_first, axis=1)
    d_first_low = d_first.astype(BF)
    d_attended = jnp.einsum("cde,dt->cet", full_attn, d_first_low, preferred_element_type=F32).astype(BF)
    d_attended = d_attended.reshape(heads, HEAD_DIM, SEQ_MAX)
    grads, bias_sums = attend_backward(qkv, key_mask, attended, total, d_attended)
    d_proj = grads.reshape(cols, 3 * width, SEQ_MAX)
    bias_sums = jnp.sum(bias_sums, axis=3)
    g_bias_q, g_bias_v = bias_sums[:, 0].reshape(d), bias_sums[:, 1].reshape(d)
    g_attn = jnp.einsum("dt,cet->cde", d_first_low, attended_cols, preferred_element_type=F32)
    g_qkv = jnp.einsum("dt,cnt->cdn", x, d_proj, preferred_element_type=F32)
    g_mix = scatter(jnp.concatenate([g_qkv.astype(BF), g_attn.astype(BF)], axis=2))
    token_grad = from_window(d_first + jnp.einsum("cdn,cnt->dt", full_qkv, d_proj, preferred_element_type=F32))

    small = jnp.stack([g_bias_q, g_bias_v, g_bias_attn, g_bias_out, gain_one, gain_two, shift_one, shift_two])
    small = small.reshape(8, cols, width).transpose(1, 0, 2)
    small = jnp.concatenate([small, g_bias_in.reshape(cols, -1, width)], axis=1)
    small = lax.psum(small, ALL)
    own = lax.dynamic_index_in_dim(small, col, axis=0, keepdims=False)
    return (
        activations, token_grad, g_mix[:, : 3 * width].reshape(rows, 3, width), own[0:2],
        g_mix[:, 3 * width :], own[2], g_in, own[8:].reshape(hid), g_out, own[3], own[4:6], own[6:8],
    )


def solution(mesh):
    return jax.shard_map(
        local,
        mesh=mesh,
        in_specs=(
            P("col", ROWS), P(ROWS, None, "col"), P(None, "col"), P(ROWS, "col"), P("col"),
            P(ROWS, "col"), P("col"), P(ROWS, "col"), P("col"), P(None, "col"), P(None, "col"),
            P(ROWS), P(ROWS), P("col", ROWS),
        ),
        out_specs=(
            P("col", ROWS), P("col", ROWS), P(ROWS, None, "col"), P(None, "col"), P(ROWS, "col"),
            P("col"), P(ROWS, "col"), P("col"), P(ROWS, "col"), P("col"), P(None, "col"), P(None, "col"),
        ),
        check_vma=False,
    )
```

time: 1160 us -> 713 us (0.61)
  waiting for transfers between devices: 515 us -> 283 us
  matrix products: 213 us -> 96.6 us
  local copies, waits for them, and re-layouts: 119 us -> 32.2 us
  Pallas kernels: 0 us -> 82.3 us
  other arithmetic: 83.3 us -> 17.1 us
  blocking collectives: 187 us -> 168 us
    reduce_scatter x6 -> x3, waiting for transfers between devices: 343 us -> 192 us  [scatter(): lax.psum_scatter(parts, OWNERS, scatter_dimension=0, tiled=True).astype(F32)]
    all_gather x6 -> x3, waiting for transfers between devices: 170 us -> 50.1 us  [gather(): lax.all_gather(shard, OWNERS, axis=0, tiled=True)]
    dot_general x40 -> x12, matrix products: 213 us -> 96.6 us  [the longest x1 13.5 us: local(): jnp.einsum('cdf,dt->cft', full_in, normed_low, preferred_element_type=F32)]
    pallas_call x0 -> x2, Pallas kernels: none -> 82.3 us  [the longest x1 41.5 us: attend_forward(): pl.pallas_call(attend_forward_kernel, grid=(heads,), in_specs=[projection...]
    reshape x15 -> x4, local copies, waits for them, and re-layouts: 52.2 us -> 0.84 us  [the longest x1 0.67 us: local(): own[8:].reshape(hid)]
    all_to_all x2, waiting for transfers between devices: 0.01 us -> 39.2 us  [to_window(): return lax.all_to_all(a, 'col', split_axis=1, concat_axis=0, tiled=True)]
    convert_element_type x9 -> x3, other arithmetic: 36.1 us -> 3.93 us  [the longest x2 3.29 us: scatter(): lax.psum_scatter(parts, OWNERS, scatter_dimension=0, tiled=True).astype(F32)]
    all_gather x4 -> x1, blocking collectives: 80 us -> 54.8 us  [local(): vectors = lax.all_gather(vectors, 'col', axis=0, tiled=False)]
  transfers between devices with their start and end apart: 15 -> 9, of which waited for: 8 -> 4; matrix products, arithmetic and copies ran while one was open for 29% -> 11% of each run, Pallas kernels for 0% -> 6%
where the time goes in v2:
time: 713 us; the launch traced here: 709 us
  waiting for transfers between devices  283 us (40%)
  blocking collectives  168 us (24%)
  matrix products  96.6 us (14%)
  Pallas kernels  82.3 us (12%)
  local copies, waits for them, and re-layouts  32.2 us (5%)
  other arithmetic  17.1 us (2%)
  between operations  16.1 us (2%)
  starting transfers between devices  13.8 us (2%)
    reduce_scatter x3, waiting for transfers between devices, scatter(): lax.psum_scatter(parts, OWNERS, scatter_dimension=0, tiled=True).astype(F32)  192 us
    psum x1, blocking collectives, local(): small = lax.psum(small, ALL)  61 us
    all_gather x1, blocking collectives, local(): vectors = lax.all_gather(vectors, 'col', axis=0, tiled=False)  54.8 us
    all_to_all x1, blocking collectives, from_window(): lax.all_to_all(a.astype(BF), 'col', split_axis=0, concat_axis=1, tiled=True)  52.7 us
    all_gather x3, waiting for transfers between devices, gather(): lax.all_gather(shard, OWNERS, axis=0, tiled=True)  50.1 us
    pallas_call x1, Pallas kernels, attend_forward(): pl.pallas_call(attend_forward_kernel, grid=(heads,), in_specs=[projection...  41.5 us
    pallas_call x1, Pallas kernels, attend_backward(): pl.pallas_call(attend_backward_kernel, grid=(heads,), in_specs=[projectio...  40.8 us
    all_to_all x2, waiting for transfers between devices, to_window(): return lax.all_to_all(a, 'col', split_axis=1, concat_axis=0, tiled=True)  39.2 us
  transfers between devices with their start and end apart: 9, of which 4 were waited for; matrix products, arithmetic and copies ran while one was open for 11% of the time, Pallas kernels for 6%

profile of v2, /device:TPU:0, one launch (start us, length us, event | category | flops | bytes accessed | tf_op | source)
XLA Modules:
  0.0 709.5 jit_solution(2635662751565000363)
XLA Ops:
  7.2 1.1 copy.76
  8.3 0.9 copy.77
  9.3 0.8 copy.78
  10.1 0.7 all-gather.8.cloned.1.call-update
  10.9 2.8 copy.123
  13.7 6.3 all-to-all-start.2
  20.0 0.7 all-gather.10.cloned.1.call-update
  20.9 1.3 copy.124
  22.2 39.1 %all-to-all-done.2 = bf16[192,4,1024]{2,0,1:T(8,128)(2,1)S(1)} async-done(((bf16[192,4,1024]{2,0,1:T(8,128)(2,1)}), bf16[192,4,1024]{2,0,1:T(8,128)(2,1)S(1)}, u32[]{:S(2)}, u32[]{:S(2)}) %all-to-all-start.2) | async-done | bytes 1572896 | tf_op jit(solution)/shard_map/all_to_all | solution.py:212
  61.3 3.7 all-to-all-start
  65.1 0.6 dynamic_slice.11
  65.7 0.6 dynamic_slice.12
  66.3 54.8 %all-gather.1 = f32[4,12,192]{2,1,0:T(8,128)S(1)} all-gather(f32[1,12,192]{2,1,0:T(8,128)S(1)} %bitcast.174), channel_id=2, replica_groups=mesh['dp'=2,'row'=4,'col'=4] {'col'}, dimensions={0}, use_global_device_ids=true | all-gather | bytes 46080 | tf_op jit(solution)/shard_map/all_gather | solution.py:204
  121.1 0.1 slice_reduce_fusion.7
  123.1 1.2 and_select_fusion.mask_ref
  124.4 0.6 fusion.51
  125.0 1.3 bitcast_reduce_fusion
  126.3 8.2 %add_convert_fusion = bf16[4,576,1024]{2,1,0:T(8,128)(2,1)} fusion(f32[4,576]{1,0:T(4,128)S(1)} %pad_maximum_fusion.3, bf16[768,1024,1]{1,0,2:T(8,128)(2,1)S(1)} %bitcast.168, bf16[4,768,768]{2,1,0:T(8,128)(2,1)} %bitcast.184), kind=kOutput, calls=%fused_computation.12 | convolution fusion | flops 3628597248 | bytes 10232832 | tf_op jit(solution)/shard_map/cdn,dt->cnt/dot_general | solution.py:226
  134.6 41.5 %attend_forward.1 = (bf16[12,64,1024]{2,1,0:T(8,128)(2,1)}, f32[12,1,1024]{2,1,0:T(1,128)}) custom-call(bf16[4,3,3,64,1024]{4,3,2,1,0:T(8,128)(2,1)} %bitcast.194, bf16[4,3,3,64,1024]{4,3,2,1,0:T(8,128)(2,1)} %bitcast.195, bf16[4,3,3,64,1024]{4,3,2,1,0:T(8,128)(2,1)} %bitcast.196, f32[1,1024]{1,0:T(1,128)} %and_select_fusion.mask_ref), custom_call_target="tpu_custom_call" | custom-call | flops 12884901888 | bytes 6291456 | tf_op jit(solution)/shard_map/attend_forward/pallas_call | solution.py:132
  176.1 4.1 fusion.57
  180.2 1.6 copy-done
  181.9 0.4 multiply_reduce_fusion.5
  182.3 13.5 %fusion.8 = (bf16[4,768,1024]{1,2,0:T(8,128)(2,1)}, f32[1024,4,768]{2,0,1:T(8,128)}) fusion(f32[4,768]{1,0:T(4,128)S(1)} %add.128, bf16[4,768,768]{2,1,0:T(8,128)(2,1)} %bitcast.188, f32[768,1024]{1,0:T(8,128)} %copy-done, f32[768]{0:T(1024)S(1)} %add.125, f32[768]{0:T(1024)S(1)} %mul.163, f32[1024]{0:T(1024)S(1)} %add_rsqrt_fusion.1, ...), kind=kOutput, calls=%fused_computation.11 | convolution fusion | flops 4854644736 | bytes 26765312 | tf_op jit(solution)/shard_map/cdf,dt->cft/dot_general | solution.py:237
  195.8 50.0 %all-gather.10.cloned.1.call-done = bf16[3072,768]{1,0:T(8,128)(2,1)} async-done(((bf16[96,768]{1,0:T(8,128)(2,1)}), bf16[3072,768]{1,0:T(8,128)(2,1)}) %all-gather.10.cloned.1.call-update) | async-done | bytes 4718608 | tf_op jit(solution)/shard_map/all_gather | solution.py:189
  245.8 9.6 %fusion.58 = (f32[1024]{0:T(1024)S(1)}, f32[768,1024]{1,0:T(8,128)S(1)}) fusion(f32[768]{0:T(1024)S(1)} %add.135, bf16[4,768,1024]{1,2,0:T(8,128)(2,1)} %get-tuple-element.87, bf16[4,768,768]{2,1,0:T(8,128)(2,1)} %bitcast.192, f32[768]{0:T(1024)S(1)} %add.125, f32[768]{0:T(1024)S(1)} %mul.163, f32[1024]{0:T(1024)S(1)} %add_rsqrt_fusion.1, ...), kind=kOutput, calls=%fused_computation.119 | convolution fusion | flops 4837342208 | bytes 17323008 | tf_op jit(solution)/shard_map/cdf,cft->dt/dot_general | solution.py:242
  255.4 0.4 multiply_reduce_fusion.4
  255.8 1.2 multiply_reduce_fusion
  257.0 2.8 fusion.55
  259.9 11.2 %fusion.59 = (f32[4,768]{1,0:T(4,128)S(1)}, bf16[4,768,1024]{1,2,0:T(8,128)(2,1)}) fusion(f32[1024,4,768]{2,0,1:T(8,128)S(1)} %copy-done.20, f32[4,768]{1,0:T(4,128)S(1)} %add.128, bf16[4,768,768]{2,1,0:T(8,128)(2,1)S(1)} %bitcast.193, f32[768,1024]{1,0:T(8,128)S(1)} %get-tuple-element.73), kind=kOutput, calls=%fused_computation.120 | convolution fusion | flops 4870370304 | bytes 26763264 | tf_op jit(solution)/shard_map/cdf,dt->cft/dot_general | solution.py:254
  271.1 8.2 %multiply_reduce_fusion.1 = (f32[768]{0:T(1024)S(1)}, f32[1024]{0:T(1024)S(1)}, f32[1024]{0:T(1024)S(1)}, f32[768]{0:T(1024)S(1)}, f32[768,1024]{1,0:T(8,128)S(1)}) fusion(f32[768,1024]{1,0:T(8,128)S(1)} %copy-done.1, f32[1024]{0:T(1024)S(1)} %add_rsqrt_fusion.1, f32[1024]{0:T(1024)S(1)} %broadcast_multiply_fusion.5, f32[768]{0:T(1024)S(1)} %mul.163, ...), kind=kOutput, calls=%fused_computation.33 | convolution fusion | flops 4839698432 | bytes 20472832 | tf_op jit(solution)/shard_map/cdf,cft->dt/dot_general | solution.py:258
  279.3 1.1 fusion.56
  280.5 5.4 convolution_convert_fusion.1
  285.9 2.5 fusion.41
  288.4 40.8 %attend_backward.1 = (bf16[4,3,3,64,1024]{4,3,2,1,0:T(8,128)(2,1)}, f32[12,2,64,128]{3,2,1,0:T(8,128)}) custom-call(bf16[4,3,3,64,1024]{4,3,2,1,0:T(8,128)(2,1)} %bitcast.197, bf16[4,3,3,64,1024]{4,3,2,1,0:T(8,128)(2,1)} %bitcast.198, bf16[4,3,3,64,1024]{4,3,2,1,0:T(8,128)(2,1)} %bitcast.199, f32[1,1024]{1,0:T(1,128)} %and_select_fusion.mask_ref, ...), custom_call_target="tpu_custom_call" | custom-call | flops 32212254720 | bytes 12582912 | tf_op jit(solution)/shard_map/attend_backward/pallas_call | solution.py:153
  329.2 6.8 convert_bitcast_fusion
  336.1 2.5 pad_maximum_fusion
  338.5 6.7 copy.89
  345.3 9.8 %fusion.22 = bf16[4,768,768]{1,2,0:T(8,128)(2,1)} fusion(bf16[4,768,1024]{1,2,0:T(8,128)(2,1)} %get-tuple-element.93, f32[768,1024]{1,0:T(8,128)S(1)} %copy-done.1, f32[768]{0:T(1024)S(1)} %add.125, f32[768]{0:T(1024)S(1)} %mul.163, f32[1024]{0:T(1024)S(1)} %add_rsqrt_fusion.1, f32[1024]{0:T(1024)S(1)} %broadcast_multiply_fusion.5), kind=kOutput, calls=%fused_computation.51 | convolution fusion | flops 4838129664 | bytes 14170112 | tf_op jit(solution)/shard_map/dt,cft->cdf/dot_general | solution.py:257
  355.1 1.9 copy-done.3
  357.0 9.8 %convolution_convert_fusion = bf16[4,768,768]{1,2,0:T(8,128)(2,1)} fusion(bf16[4,768,1024]{1,2,0:T(8,128)(2,1)} %get-tuple-element.87, f32[768,1024]{1,0:T(8,128)S(1)} %copy-done.3), kind=kOutput, calls=%fused_computation.50 | convolution fusion | flops 4834983936 | bytes 14155776 | tf_op jit(solution)/shard_map/dt,cft->cdf/dot_general | solution.py:253
  366.8 1.9 copy-done.5
  368.8 7.5 %fusion.14 = bf16[768,1024]{1,0:T(8,128)(2,1)S(1)} fusion(f32[768,1024]{1,0:T(8,128)S(1)} %copy-done.5, bf16[4,576,1024]{2,1,0:T(8,128)(2,1)} %bitcast.201, bf16[4,768,768]{2,1,0:T(8,128)(2,1)} %bitcast.187), kind=kOutput, calls=%fused_computation.24 | convolution fusion | flops 3625451520 | bytes 13369344 | tf_op jit(solution)/shard_map/cdn,cnt->dt/dot_general | solution.py:273
  376.3 52.7 %all_to_all.58 = bf16[4,192,1024]{2,1,0:T(8,128)(2,1)S(1)} all-to-all(bf16[4,192,1024]{2,1,0:T(8,128)(2,1)S(1)} %bitcast.171), channel_id=1, replica_groups=mesh['dp'=2,'row'=4,'col'=4] {'col'}, dimensions={0} | all-to-all | bytes 3145728 | tf_op jit(solution)/shard_map/all_to_all | solution.py:215
  429.0 3.6 all-to-all-start.1
  432.6 1.4 reduce_sum.152
  434.6 0.1 reshape.216
  434.8 61.0 %psum.7 = f32[4,12,192]{2,0,1:T(4,128)S(1)} all-reduce(f32[4,12,192]{2,0,1:T(4,128)S(1)} %pad_maximum_fusion.2), channel_id=1, replica_groups=mesh['dp'=2,'row'=4,'col'=4] {'dp','row','col'}, use_global_device_ids=true, to_apply=%region_17.18 | all-reduce | flops 9216 | bytes 73728 | tf_op jit(solution)/shard_map/psum | solution.py:278
  495.9 0.7 reshape.218
  496.6 0.6 copy.126
  497.1 0.6 copy.127
  497.7 0.6 copy.128
  498.3 0.6 constant_dynamic-slice_fusion.1
  498.9 0.4 convert_bitcast_fusion.1
  499.3 1.9 copy.114
  501.2 0.4 convert_bitcast_fusion.2
  501.5 1.9 copy.113
  503.4 0.9 slice.110
  504.4 0.1 copy.90
  504.5 0.9 copy.94
  505.4 1.5 slice.113
  506.9 81.8 %reduce-scatter.6.cloned.1.call-done = bf16[96,768]{1,0:T(8,128)(2,1)} async-done(((bf16[3072,768]{1,0:T(8,128)(2,1)}), bf16[96,768]{1,0:T(8,128)(2,1)}) %reduce-scatter.6.cloned.1.call-update) | async-done | bytes 147472 | tf_op jit(solution)/shard_map/reduce_scatter | solution.py:193
  588.7 1.6 convert_element_type.131
  590.4 110.3 %reduce-scatter.8.cloned.1.call-done = bf16[96,768]{1,0:T(8,128)(2,1)} async-done(((bf16[3072,768]{1,0:T(8,128)(2,1)}), bf16[96,768]{1,0:T(8,128)(2,1)}) %reduce-scatter.8.cloned.1.call-update) | async-done | bytes 147472 | tf_op jit(solution)/shard_map/reduce_scatter | solution.py:193
  700.7 1.6 convert_element_type.134
  (103 shorter events, 1.9 us)
Async XLA Ops:
  7.2 119.2 %all-gather.6.cloned.1.call-start = ((), (), s32[]{:S(2)}) async-start(), calls=%async_computation.7 | async-start | bytes 4866048 | tf_op jit(solution)/shard_map/all_gather | solution.py:189
  10.1 172.2 %all-gather.8.cloned.1.call-start = ((), (), s32[]{:S(2)}) async-start(), calls=%async_computation.8 | async-start | bytes 4866048 | tf_op jit(solution)/shard_map/all_gather | solution.py:189
  10.8 9.9 %copy-start.6 = (bf16[192,4096]{1,0:T(8,128)(2,1)S(1)}, bf16[192,4096]{1,0:T(8,128)(2,1)}, u32[]{:S(2)}) copy-start(bf16[192,4096]{1,0:T(8,128)(2,1)} %param.14) | copy-start | bytes 4718596
  13.7 47.6 %all-to-all-start.2 = ((bf16[192,4,1024]{2,0,1:T(8,128)(2,1)}), bf16[192,4,1024]{2,0,1:T(8,128)(2,1)S(1)}, u32[]{:S(2)}, u32[]{:S(2)}) async-start(bf16[192,4,1024]{2,0,1:T(8,128)(2,1)} %bitcast.155), calls=%async_computation.2 | async-start | bytes 3145728 | tf_op jit(solution)/shard_map/all_to_all | solution.py:212
  20.0 225.8 %all-gather.10.cloned.1.call-start = ((), (), s32[]{:S(2)}) async-start(), calls=%async_computation.9 | async-start | bytes 4866048 | tf_op jit(solution)/shard_map/all_gather | solution.py:189
  20.8 44.2 %copy-start.10 = (f32[768]{0:T(1024)S(1)}, f32[768]{0:T(1024)}, u32[]{:S(2)}) copy-start(f32[768]{0:T(1024)} %param.20) | copy-start | bytes 9220
  20.8 44.3 %copy-start.17 = (s32[4]{0:T(128)S(1)}, s32[4]{0:T(128)}, u32[]{:S(2)}) copy-start(s32[4]{0:T(128)} %param.26) | copy-start | bytes 52
  20.8 44.9 %copy-start.18 = (s32[4]{0:T(128)S(1)}, s32[4]{0:T(128)}, u32[]{:S(2)}) copy-start(s32[4]{0:T(128)} %param.25) | copy-start | bytes 52
  20.8 45.4 %copy-start.11 = (f32[2,192]{1,0:T(2,128)S(1)}, f32[2,192]{1,0:T(2,128)}, u32[]{:S(2)}) copy-start(f32[2,192]{1,0:T(2,128)} %param.16) | copy-start | bytes 4612
  20.8 45.4 %copy-start.12 = (f32[2,192]{1,0:T(2,128)S(1)}, f32[2,192]{1,0:T(2,128)}, u32[]{:S(2)}) copy-start(f32[2,192]{1,0:T(2,128)} %param.23) | copy-start | bytes 4612
  20.8 45.4 %copy-start.13 = (f32[2,192]{1,0:T(2,128)S(1)}, f32[2,192]{1,0:T(2,128)}, u32[]{:S(2)}) copy-start(f32[2,192]{1,0:T(2,128)} %param.24) | copy-start | bytes 4612
  20.8 45.4 %copy-start.14 = (f32[192]{0:T(256)S(1)}, f32[192]{0:T(256)}, u32[]{:S(2)}) copy-start(f32[192]{0:T(256)} %param.18) | copy-start | bytes 2308
  20.8 45.4 %copy-start.15 = (f32[192]{0:T(256)S(1)}, f32[192]{0:T(256)}, u32[]{:S(2)}) copy-start(f32[192]{0:T(256)} %param.22) | copy-start | bytes 2308
  61.3 65.0 %all-to-all-start = ((bf16[192,4,1024]{2,0,1:T(8,128)(2,1)}), bf16[192,4,1024]{2,0,1:T(8,128)(2,1)S(1)}, u32[]{:S(2)}, u32[]{:S(2)}) async-start(bf16[192,4,1024]{2,0,1:T(8,128)(2,1)} %bitcast.156), calls=%async_computation | async-start | bytes 3145728 | tf_op jit(solution)/shard_map/all_to_all | solution.py:212
  65.0 438.5 %reduce-scatter.4.cloned.1.call-start = ((), (), s32[]{:S(2)}) async-start(), calls=%async_computation.10 | async-start | bytes 4866048 | tf_op jit(solution)/shard_map/reduce_scatter | solution.py:193
  126.3 49.8 %copy-start.7 = (bf16[192,4,1024]{2,0,1:T(8,128)(2,1)}, bf16[192,4,1024]{2,0,1:T(8,128)(2,1)S(1)}, u32[]{:S(2)}) copy-start(bf16[192,4,1024]{2,0,1:T(8,128)(2,1)S(1)} %all-to-all-done) | copy-start | bytes 4718596
  180.2 1.7 copy-start
  245.8 14.0 %copy-start.20 = (f32[1024,4,768]{2,0,1:T(8,128)S(1)}, f32[1024,4,768]{2,0,1:T(8,128)}, u32[]{:S(2)}) copy-start(f32[1024,4,768]{2,0,1:T(8,128)} %get-tuple-element.88) | copy-start | bytes 37748740
  257.0 2.9 copy-start.16
  257.0 14.1 %slice-start = ((s8[4718592]{0:T(1024)(128)(4,1)}), s8[4194304]{0:T(1024)(128)(4,1)S(1)}, s32[]{:S(2)}) async-start(s8[4718592]{0:T(1024)(128)(4,1)} %bitcast.189), calls=%async_computation.13 | async-start | bytes 8388608
  259.8 11.2 %copy-start.2 = (f32[768,1024]{1,0:T(8,128)}, f32[768,1024]{1,0:T(8,128)S(1)}, u32[]{:S(2)}) copy-start(f32[768,1024]{1,0:T(8,128)S(1)} %get-tuple-element.73) | copy-start | bytes 9437188
  259.8 11.2 %copy-start.1 = (f32[768,1024]{1,0:T(8,128)S(1)}, f32[768,1024]{1,0:T(8,128)}, u32[]{:S(2)}) copy-start(f32[768,1024]{1,0:T(8,128)} %copy-done) | copy-start | bytes 9437188
  259.9 11.2 %slice-start.1 = ((s8[4718592]{0:T(1024)(128)(4,1)}), s8[524288]{0:T(1024)(128)(4,1)S(1)}, s32[]{:S(2)}) async-start(s8[4718592]{0:T(1024)(128)(4,1)} %bitcast.189), calls=%async_computation.14 | async-start | bytes 1048576
  280.4 5.4 copy-start.4
  280.5 5.4 copy-start.19
  329.2 6.9 copy-start.8
  345.2 243.5 %reduce-scatter.6.cloned.1.call-start = ((), (), s32[]{:S(2)}) async-start(), calls=%async_computation.11 | async-start | bytes 4866048 | tf_op jit(solution)/shard_map/reduce_scatter | solution.py:193
  355.0 2.0 copy-start.3
  355.1 345.6 %reduce-scatter.8.cloned.1.call-start = ((), (), s32[]{:S(2)}) async-start(), calls=%async_computation.12 | async-start | bytes 4866048 | tf_op jit(solution)/shard_map/reduce_scatter | solution.py:193
  366.8 2.0 copy-start.5
  376.3 58.5 %copy-start.9 = (f32[4,192]{1,0:T(4,128)S(1)}, f32[4,192]{1,0:T(4,128)}, u32[]{:S(2)}) copy-start(f32[4,192]{1,0:T(4,128)} %get-tuple-element.62) | copy-start | bytes 9220
  429.0 72.1 %all-to-all-start.1 = ((bf16[4,192,1024]{2,1,0:T(8,128)(2,1)}), bf16[4,192,1024]{2,1,0:T(8,128)(2,1)S(1)}, u32[]{:S(2)}, u32[]{:S(2)}) async-start(bf16[4,192,1024]{2,1,0:T(8,128)(2,1)} %bitcast.21), calls=%async_computation.1 | async-start | bytes 3145728 | tf_op jit(solution)/shard_map/all_to_all | solution.py:215
Sparse Core Ops, SparseCore 0:
  11.4 102.1 all-gather.5
  116.5 64.4 all-gather.7
  183.9 61.9 all-gather.9
  345.3 133.0 reduce-scatter.3
  483.7 104.9 reduce-scatter.5
  594.1 106.6 reduce-scatter.7

commit v3 on v2

--- a/solution.py
+++ b/solution.py
@@ -79,7 +79,8 @@
 
 
 def attend_backward_kernel(
-    q_ref, k_ref, v_ref, mask_ref, out_ref, total_ref, up_ref, grad_ref, bias_ref, dk_ref, dv_ref
+    q_ref, k_ref, v_ref, mask_ref, out_ref, total_ref, up_ref,
+    grad_qk_ref, grad_v_ref, bias_ref, dk_ref, dv_ref,
 ):
     seq = q_ref.shape[-1]
     one = jnp.ones((1, seq), F32)
@@ -100,7 +101,7 @@
         d_q = dot_nn(keys, d_scores) * SCALE
         for part in range(QBLOCK // lanes):
             sum_q += d_q[:, part * lanes : (part + 1) * lanes]
-        grad_ref[0, 0, 0, :, cols] = d_q.astype(BF)
+        grad_qk_ref[0, 0, 0, :, cols] = d_q.astype(BF)
         d_k = dot_nt(queries[:, cols], d_scores)
         d_v = dot_nt(up[:, cols], weights.astype(BF))
         if j == 0:
@@ -109,8 +110,8 @@
         else:
             dk_ref[...] += d_k
             dv_ref[...] += d_v
-    grad_ref[0, 1, 0] = (dk_ref[...] * SCALE).astype(BF)
-    grad_ref[0, 2, 0] = dv_ref[...].astype(BF)
+    grad_qk_ref[0, 1, 0] = (dk_ref[...] * SCALE).astype(BF)
+    grad_v_ref[0, 0, 0] = dv_ref[...].astype(BF)
     bias_ref[0, 0] = sum_q
     sum_v = jnp.zeros((HEAD_DIM, lanes), F32)
     for part in range(seq // lanes):
@@ -118,22 +119,28 @@
     bias_ref[0, 1] = sum_v
 
 
-def projection_spec(which, per_col, seq):
-    return pl.BlockSpec((1, 1, 1, HEAD_DIM, seq), lambda h: (h // per_col, which, h % per_col, 0, 0))
+def projection_spec(first, count, per_col, seq):
+    return pl.BlockSpec((1, count, 1, HEAD_DIM, seq), lambda h: (h // per_col, first, h % per_col, 0, 0))
 
 
 def head_spec(rows, seq):
     return pl.BlockSpec((1, rows, seq), lambda h: (h, 0, 0))
 
 
-def attend_forward(qkv, mask):
-    cols, _, per_col, _, seq = qkv.shape
+def qkv_specs(per_col, seq):
+    return [
+        projection_spec(0, 1, per_col, seq), projection_spec(1, 1, per_col, seq), projection_spec(0, 1, per_col, seq),
+        pl.BlockSpec((1, seq), lambda h: (0, 0)),
+    ]
+
+
+def attend_forward(qk, v, mask):
+    cols, _, per_col, _, seq = qk.shape
     heads = cols * per_col
     return pl.pallas_call(
         attend_forward_kernel,
         grid=(heads,),
-        in_specs=[projection_spec(k, per_col, seq) for k in range(3)]
-        + [pl.BlockSpec((1, seq), lambda h: (0, 0))],
+        in_specs=qkv_specs(per_col, seq),
         out_specs=[head_spec(HEAD_DIM, seq), head_spec(1, seq)],
         out_shape=[
             jax.ShapeDtypeStruct((heads, HEAD_DIM, seq), BF),
@@ -144,24 +151,25 @@
             transcendentals=heads * seq * seq,
         ),
         name="attend_forward",
-    )(qkv, qkv, qkv, mask)
-
-
-def attend_backward(qkv, mask, attended, total, d_attended):
-    cols, _, per_col, _, seq = qkv.shape
+    )(qk, qk, v, mask)
+
+
+def attend_backward(qk, v, mask, attended, total, d_attended):
+    cols, _, per_col, _, seq = qk.shape
     heads = cols * per_col
     return pl.pallas_call(
         attend_backward_kernel,
         grid=(heads,),
-        in_specs=[projection_spec(k, per_col, seq) for k in range(3)]
-        + [pl.BlockSpec((1, seq), lambda h: (0, 0))]
+        in_specs=qkv_specs(per_col, seq)
         + [head_spec(HEAD_DIM, seq), head_spec(1, seq), head_spec(HEAD_DIM, seq)],
         out_specs=[
-            pl.BlockSpec((1, 3, 1, HEAD_DIM, seq), lambda h: (h // per_col, 0, h % per_col, 0, 0)),
+            projection_spec(0, 2, per_col, seq),
+            projection_spec(0, 1, per_col, seq),
             pl.BlockSpec((1, 2, HEAD_DIM, 128), lambda h: (h, 0, 0, 0)),
         ],
         out_shape=[
-            jax.ShapeDtypeStruct(qkv.shape, BF),
+            jax.ShapeDtypeStruct(qk.shape, BF),
+            jax.ShapeDtypeStruct(v.shape, BF),
             jax.ShapeDtypeStruct((heads, 2, HEAD_DIM, 128), F32),
         ],
         scratch_shapes=[pltpu.VMEM((HEAD_DIM, seq), F32), pltpu.VMEM((HEAD_DIM, seq), F32)],
@@ -170,7 +178,58 @@
             transcendentals=heads * seq * seq,
         ),
         name="attend_backward",
-    )(qkv, qkv, qkv, mask, attended, total, d_attended)
+    )(qk, qk, v, mask, attended, total, d_attended)
+
+
+def axis_bits(name):
+    size = lax.axis_size(name)
+    return [(name, 1 << b) for b in reversed(range(size.bit_length() - 1))]
+
+
+def swap(a, name, bit):
+    return lax.ppermute(a, name, [(i, i ^ bit) for i in range(lax.axis_size(name))])
+
+
+def my_bit(name, bit):
+    return (lax.axis_index(name) // bit) % 2
+
+
+def gather_blocks(shard, order):
+    dims = axis_bits("col") + axis_bits("dp") + axis_bits("row")
+    a = shard.reshape((1,) * len(dims) + shard.shape)
+    for name, bit in order:
+        dim = dims.index((name, bit))
+        other = swap(a, name, bit)
+        high = my_bit(name, bit) == 1
+        a = jnp.concatenate([jnp.where(high, other, a), jnp.where(high, a, other)], axis=dim)
+    return a.reshape(lax.axis_size("col"), -1, shard.shape[1])
+
+
+def scatter_blocks(grad, order):
+    dims = axis_bits("col") + axis_bits("dp") + axis_bits("row")
+    rows = grad.shape[0] * grad.shape[1] >> len(dims)
+    a = grad.astype(BF).reshape((2,) * len(dims) + (rows, grad.shape[2]))
+    for name, bit in order:
+        dim = dims.index((name, bit))
+        mine = my_bit(name, bit)
+        other = swap(lax.dynamic_index_in_dim(a, 1 - mine, dim), name, bit)
+        a = lax.dynamic_index_in_dim(a, mine, dim).astype(F32) + other.astype(F32)
+        a = a.astype(BF)
+    return a.reshape(rows, grad.shape[2]).astype(F32)
+
+
+def spread_windows(a):
+    cols = lax.axis_size("col")
+    col = lax.axis_index("col")
+    rows, seq = a.shape[0] // cols, a.shape[1]
+    parts = [lax.dynamic_slice_in_dim(a, col * rows, rows, axis=0)]
+    for step in range(1, cols):
+        block = lax.dynamic_slice_in_dim(a, (col ^ step) * rows, rows, axis=0)
+        parts.append(lax.ppermute(block, "col", [(i, i ^ step) for i in range(cols)]))
+    out = jnp.zeros((rows, cols * seq), F32)
+    for step, part in enumerate(parts):
+        out = lax.dynamic_update_slice_in_dim(out, part.astype(F32), (col ^ step) * seq, axis=1)
+    return out
 
 
 def local(
@@ -185,23 +244,30 @@
     heads = d // HEAD_DIM
     hid = w_in.shape[1]
 
+    col_bits, row_bits, dp_bits = axis_bits("col"), axis_bits("row"), axis_bits("dp")
+    near_first = col_bits[::-1] + row_bits[::-1] + dp_bits
+    far_first = col_bits[::-1] + row_bits + dp_bits
+
     def gather(shard):
         return lax.all_gather(shard, OWNERS, axis=0, tiled=True).reshape(cols, d, shard.shape[1])
 
-    def scatter(grad):
-        parts = grad.astype(BF).reshape(cols * d, grad.shape[2])
-        return lax.psum_scatter(parts, OWNERS, scatter_dimension=0, tiled=True).astype(F32)
-
-    w_mix = gather(jnp.concatenate([w_qkv.reshape(rows, 3 * width), w_attn_out], axis=1))
+    w_flat = w_qkv.reshape(rows, 3 * width)
+    full_qk = gather_blocks(w_flat[:, : 2 * width], near_first)
+    full_vo = gather_blocks(jnp.concatenate([w_flat[:, 2 * width :], w_attn_out], axis=1), far_first)
     full_in = gather(w_in)
     full_out = gather(w_out)
-    full_qkv = w_mix[:, :, : 3 * width]
-    full_attn = w_mix[:, :, 3 * width :]
+    full_v = full_vo[:, :, :width]
+    full_attn = full_vo[:, :, width:]
 
     vectors = jnp.concatenate(
         [bias_qv, bias_attn_out[None], bias_out[None], norm_gains, norm_biases, bias_in.reshape(-1, width)], axis=0
     )
-    vectors = lax.all_gather(vectors, "col", axis=0, tiled=False)
+    vectors = vectors.reshape((1,) * len(col_bits) + vectors.shape)
+    for dim, (name, bit) in enumerate(col_bits):
+        other = swap(vectors, name, bit)
+        high = my_bit(name, bit) == 1
+        vectors = jnp.concatenate([jnp.where(high, other, vectors), jnp.where(high, vectors, other)], axis=dim)
+    vectors = vectors.reshape(cols, -1, width)
     bias_q, bias_v = vectors[:, 0], vectors[:, 1]
     bias_attn_out, bias_out = vectors[:, 2].reshape(d), vectors[:, 3].reshape(d)
     gains = [vectors[:, 4].reshape(d), vectors[:, 5].reshape(d)]
@@ -210,9 +276,6 @@
 
     def to_window(a):
         return lax.all_to_all(a, "col", split_axis=1, concat_axis=0, tiled=True)
-
-    def from_window(a):
-        return lax.all_to_all(a.astype(BF), "col", split_axis=0, concat_axis=1, tiled=True).astype(F32)
 
     x = to_window(tokens)
     up = to_window(cotangent)
@@ -223,10 +286,13 @@
     live = live_mask.astype(F32)
     key_mask = jnp.where(live_mask, 0.0, -1e30).astype(F32)
 
-    proj = jnp.einsum("cdn,dt->cnt", full_qkv, x, preferred_element_type=F32)
-    shift_qkv = jnp.concatenate([bias_q, jnp.zeros_like(bias_q), bias_v], axis=1)
-    qkv = (proj + shift_qkv[:, :, None]).astype(BF).reshape(cols, 3, width // HEAD_DIM, HEAD_DIM, SEQ_MAX)
-    attended, total = attend_forward(qkv, key_mask)
+    def project(weights, shift):
+        out = jnp.einsum("cdn,dt->cnt", weights, x, preferred_element_type=F32) + shift[:, :, None]
+        return out.astype(BF).reshape(cols, -1, width // HEAD_DIM, HEAD_DIM, SEQ_MAX)
+
+    qk = project(full_qk, jnp.concatenate([bias_q, jnp.zeros_like(bias_q)], axis=1))
+    values = project(full_v, bias_v)
+    attended, total = attend_forward(qk, values, key_mask)
     attended_cols = attended.reshape(cols, width, SEQ_MAX)
     first_sum = (
         x.astype(F32) + jnp.einsum("cde,cet->dt", full_attn, attended_cols, preferred_element_type=F32)
@@ -242,7 +308,7 @@
         normed + jnp.einsum("cdf,cft->dt", full_out, active, preferred_element_type=F32) + bias_out[:, None]
     )
     result, xhat2, rstd2 = norm_forward(second_sum, gains[1], shifts[1])
-    activations = from_window(result * live)
+    activations = spread_windows((result * live).astype(BF))
 
     upstream = up.astype(F32) * live
     gain_two = jnp.sum(upstream * xhat2, axis=1)
@@ -250,11 +316,13 @@
     d_second = norm_backward(upstream, xhat2, rstd2, gains[1])
     g_bias_out = jnp.sum(d_second, axis=1)
     d_second_low = d_second.astype(BF)
-    g_out = scatter(jnp.einsum("dt,cft->cdf", d_second_low, active, preferred_element_type=F32))
+    g_out = jnp.einsum("dt,cft->cdf", d_second_low, active, preferred_element_type=F32)
+    g_out = scatter_blocks(g_out, dp_bits + row_bits + col_bits)
     d_hidden = jnp.einsum("cdf,dt->cft", full_out, d_second_low, preferred_element_type=F32) * slope
     g_bias_in = jnp.sum(d_hidden, axis=2)
     d_hidden_low = d_hidden.astype(BF)
-    g_in = scatter(jnp.einsum("dt,cft->cdf", normed_low, d_hidden_low, preferred_element_type=F32))
+    g_in = jnp.einsum("dt,cft->cdf", normed_low, d_hidden_low, preferred_element_type=F32)
+    g_in = scatter_blocks(g_in, dp_bits + row_bits[::-1] + col_bits)
     d_normed = d_second + jnp.einsum("cdf,cft->dt", full_in, d_hidden_low, preferred_element_type=F32)
     gain_one = jnp.sum(d_normed * xhat1, axis=1)
     shift_one = jnp.sum(d_normed, axis=1)
@@ -263,23 +331,37 @@
     d_first_low = d_first.astype(BF)
     d_attended = jnp.einsum("cde,dt->cet", full_attn, d_first_low, preferred_element_type=F32).astype(BF)
     d_attended = d_attended.reshape(heads, HEAD_DIM, SEQ_MAX)
-    grads, bias_sums = attend_backward(qkv, key_mask, attended, total, d_attended)
-    d_proj = grads.reshape(cols, 3 * width, SEQ_MAX)
+    g_attn = jnp.einsum("dt,cet->cde", d_first_low, attended_cols, preferred_element_type=F32)
+    g_attn = scatter_blocks(g_attn, dp_bits + row_bits + col_bits)
+    d_qk, d_v, bias_sums = attend_backward(qk, values, key_mask, attended, total, d_attended)
+    d_qk = d_qk.reshape(cols, 2 * width, SEQ_MAX)
+    d_v = d_v.reshape(cols, width, SEQ_MAX)
     bias_sums = jnp.sum(bias_sums, axis=3)
     g_bias_q, g_bias_v = bias_sums[:, 0].reshape(d), bias_sums[:, 1].reshape(d)
-    g_attn = jnp.einsum("dt,cet->cde", d_first_low, attended_cols, preferred_element_type=F32)
-    g_qkv = jnp.einsum("dt,cnt->cdn", x, d_proj, preferred_element_type=F32)
-    g_mix = scatter(jnp.concatenate([g_qkv.astype(BF), g_attn.astype(BF)], axis=2))
-    token_grad = from_window(d_first + jnp.einsum("cdn,cnt->dt", full_qkv, d_proj, preferred_element_type=F32))
+    g_qk = jnp.einsum("dt,cnt->cdn", x, d_qk, preferred_element_type=F32)
+    g_qk = scatter_blocks(g_qk, dp_bits + row_bits[::-1] + col_bits)
+    g_v = jnp.einsum("dt,cnt->cdn", x, d_v, preferred_element_type=F32)
+    g_v = scatter_blocks(g_v, dp_bits + row_bits + col_bits)
+    token_grad = (
+        d_first + jnp.einsum("cdn,cnt->dt", full_qk, d_qk, preferred_element_type=F32)
+        + jnp.einsum("cdn,cnt->dt", full_v, d_v, preferred_element_type=F32)
+    )
+    token_grad = spread_windows(token_grad.astype(BF))
 
     small = jnp.stack([g_bias_q, g_bias_v, g_bias_attn, g_bias_out, gain_one, gain_two, shift_one, shift_two])
     small = small.reshape(8, cols, width).transpose(1, 0, 2)
     small = jnp.concatenate([small, g_bias_in.reshape(cols, -1, width)], axis=1)
-    small = lax.psum(small, ALL)
-    own = lax.dynamic_index_in_dim(small, col, axis=0, keepdims=False)
+    small = small.reshape((2,) * len(col_bits) + small.shape[1:])
+    for dim, (name, bit) in enumerate(col_bits):
+        mine = my_bit(name, bit)
+        other = swap(lax.dynamic_index_in_dim(small, 1 - mine, dim), name, bit)
+        small = lax.dynamic_index_in_dim(small, mine, dim) + other
+    own = small.reshape(small.shape[-2:])
+    for name, bit in row_bits + dp_bits:
+        own = own + swap(own, name, bit)
     return (
-        activations, token_grad, g_mix[:, : 3 * width].reshape(rows, 3, width), own[0:2],
-        g_mix[:, 3 * width :], own[2], g_in, own[8:].reshape(hid), g_out, own[3], own[4:6], own[6:8],
+        activations, token_grad, jnp.concatenate([g_qk, g_v], axis=1).reshape(rows, 3, width), own[0:2],
+        g_attn, own[2], g_in, own[8:].reshape(hid), g_out, own[3], own[4:6], own[6:8],
     )
 
 

time: 713 us -> 563 us (0.79)
  blocking collectives: 168 us -> 0 us
  waiting for transfers between devices: 283 us -> 170 us
  starting transfers between devices: 13.8 us -> 79.7 us
  other arithmetic: 17.1 us -> 46.7 us
  local copies, waits for them, and re-layouts: 32.2 us -> 59 us
    reduce_scatter x3 -> x0, waiting for transfers between devices: 192 us -> none  [scatter(): lax.psum_scatter(parts, OWNERS, scatter_dimension=0, tiled=True).astype(F32)]
    ppermute x0 -> x48, waiting for transfers between devices: none -> 169 us  [the longest x42 121 us: swap(): lax.ppermute(a, name, [(i, i ^ bit) for i in range(lax.axis_size(name))])]
    ppermute x0 -> x48, starting transfers between devices: none -> 71.4 us  [the longest x42 64.5 us: swap(): lax.ppermute(a, name, [(i, i ^ bit) for i in range(lax.axis_size(name))])]
    psum x1 -> x0, blocking collectives: 61 us -> none  [local(): small = lax.psum(small, ALL)]
    all_gather x1 -> x0, blocking collectives: 54.8 us -> none  [local(): vectors = lax.all_gather(vectors, 'col', axis=0, tiled=False)]
    all_to_all x1 -> x0, blocking collectives: 52.7 us -> none  [from_window(): lax.all_to_all(a.astype(BF), 'col', split_axis=0, concat_axis=1, tiled=True)]
    all_gather x3 -> x2, waiting for transfers between devices: 50.1 us -> 0.02 us  [gather(): lax.all_gather(shard, OWNERS, axis=0, tiled=True)]
    all_to_all x2, waiting for transfers between devices: 39.2 us -> 0.01 us  [to_window(): return lax.all_to_all(a, 'col', split_axis=1, concat_axis=0, tiled=True)]
  transfers between devices with their start and end apart: 9 -> 52, of which waited for: 4 -> 24; matrix products, arithmetic and copies ran while one was open for 11% -> 24% of each run, Pallas kernels for 6% -> 8%
where the time goes in v3:
time: 563 us; the launch traced here: 553 us
  waiting for transfers between devices  170 us (30%)
  matrix products  98.2 us (17%)
  Pallas kernels  82.3 us (15%)
  starting transfers between devices  79.7 us (14%)
  local copies, waits for them, and re-layouts  59 us (10%)
  other arithmetic  46.7 us (8%)
  between operations  17 us (3%)
    ppermute x42, waiting for transfers between devices, swap(): lax.ppermute(a, name, [(i, i ^ bit) for i in range(lax.axis_size(name))])  121 us
    ppermute x42, starting transfers between devices, swap(): lax.ppermute(a, name, [(i, i ^ bit) for i in range(lax.axis_size(name))])  64.5 us
    ppermute x6, waiting for transfers between devices, spread_windows(): lax.ppermute(block, 'col', [(i, i ^ step) for i in range(cols)])  47.7 us
    pallas_call x1, Pallas kernels, attend_forward(): pl.pallas_call(attend_forward_kernel, grid=(heads,), in_specs=qkv_specs(p...  41.6 us
    pallas_call x1, Pallas kernels, attend_backward(): pl.pallas_call(attend_backward_kernel, grid=(heads,), in_specs=qkv_specs(...  40.7 us
    dot_general x1, matrix products, local(): jnp.einsum('cdf,dt->cft', full_in, normed_low, preferred_element_type=F32)  13.6 us
    dot_general x1, matrix products, local(): jnp.einsum('cdf,dt->cft', full_out, d_second_low, preferred_element_type=...  12.8 us
    dynamic_update_slice x8, other arithmetic, spread_windows(): lax.dynamic_update_slice_in_dim(out, part.astype(F32), (col ^ step) * seq...  11.7 us
  transfers between devices with their start and end apart: 52, of which 24 were waited for; matrix products, arithmetic and copies ran while one was open for 24% of the time, Pallas kernels for 8%

profile of v3, /device:TPU:0, one launch (start us, length us, event | category | flops | bytes accessed | tf_op | source)
XLA Modules:
  0.0 553.4 jit_solution(6454121695921197820)
XLA Ops:
  9.9 3.1 collective-permute-start
  13.2 3.3 collective-permute-done
  17.2 3.1 collective-permute-start.1
  23.1 2.5 collective-permute-start.10
  26.9 4.5 all-to-all-start
  36.2 8.3 %collective-permute-done.1 = bf16[1,2,1,1,1,96,384]{5,6,4,3,2,1,0:T(8,128)(2,1)} collective-permute-done((bf16[1,2,1,1,1,96,384]{5,6,4,3,2,1,0:T(8,128)(2,1)}, bf16[1,2,1,1,1,96,384]{5,6,4,3,2,1,0:T(8,128)(2,1)}, u32[]{:S(2)}, u32[]{:S(2)}) %collective-permute-start.1) | collective-permute-done | bytes 147488 | tf_op jit(solution)/shard_map/ppermute | solution.py:190
  44.5 4.9 collective-permute-done.6
  56.4 5.9 %collective-permute-done.2 = bf16[2,2,1,1,1,96,384]{5,6,4,3,2,1,0:T(8,128)(2,1)S(1)} collective-permute-done((bf16[2,2,1,1,1,96,384]{5,6,4,3,2,1,0:T(8,128)(2,1)S(1)}, bf16[2,2,1,1,1,96,384]{5,6,4,3,2,1,0:T(8,128)(2,1)S(1)}, u32[]{:S(2)}, u32[]{:S(2)}) %collective-permute-start.2) | collective-permute-done | bytes 294944 | tf_op jit(solution)/shard_map/ppermute | solution.py:190
  63.8 4.5 collective-permute-done.7
  74.0 8.5 %collective-permute-done.3 = bf16[2,2,1,2,1,96,384]{6,5,4,3,2,1,0:T(8,128)(2,1)} collective-permute-done((bf16[2,2,1,2,1,96,384]{6,5,4,3,2,1,0:T(8,128)(2,1)S(1)}, bf16[2,2,1,2,1,96,384]{6,5,4,3,2,1,0:T(8,128)(2,1)}, u32[]{:S(2)}, u32[]{:S(2)}) %collective-permute-start.3) | collective-permute-done | bytes 589856 | tf_op jit(solution)/shard_map/ppermute | solution.py:190
  86.0 7.0 %collective-permute-done.8 = bf16[2,2,1,1,2,96,384]{6,5,4,3,2,1,0:T(8,128)(2,1)} collective-permute-done((bf16[2,2,1,1,2,96,384]{6,5,4,3,2,1,0:T(8,128)(2,1)}, bf16[2,2,1,1,2,96,384]{6,5,4,3,2,1,0:T(8,128)(2,1)}, u32[]{:S(2)}, u32[]{:S(2)}) %collective-permute-start.8) | collective-permute-done | bytes 589856 | tf_op jit(solution)/shard_map/ppermute | solution.py:190
  100.2 1.8 copy.72
  103.2 2.6 copy.74
  105.8 2.0 copy.80
  108.9 2.7 copy.82
  111.6 3.8 all-to-all-start.1
  115.4 4.6 add_convert_fusion.3
  120.0 5.4 add_convert_fusion
  125.5 41.6 %attend_forward.1 = (bf16[12,64,1024]{2,1,0:T(8,128)(2,1)}, f32[12,1,1024]{2,1,0:T(1,128)}) custom-call(bf16[4,2,3,64,1024]{4,3,2,1,0:T(8,128)(2,1)} %bitcast.246, bf16[4,2,3,64,1024]{4,3,2,1,0:T(8,128)(2,1)} %bitcast.247, bf16[4,1,3,64,1024]{4,3,2,1,0:T(8,128)(2,1)} %bitcast.252, f32[1,1024]{1,0:T(1,128)} %and_select_fusion.mask_ref), custom_call_target="tpu_custom_call" | custom-call | flops 12884901888 | bytes 6291456 | tf_op jit(solution)/shard_map/attend_forward/pallas_call | solution.py:140
  167.0 4.6 fusion.68
  174.0 13.6 %fusion.8 = (bf16[4,768,1024]{1,2,0:T(8,128)(2,1)}, f32[1024,4,768]{2,0,1:T(8,128)}) fusion(f32[4,768]{1,0:T(4,128)S(1)} %add.416, bf16[4,768,768]{2,1,0:T(8,128)(2,1)} %bitcast.238, f32[768,1024]{1,0:T(8,128)} %copy-done, f32[768]{0:T(1024)S(1)} %add.413, f32[768]{0:T(1024)S(1)} %mul.195, f32[1024]{0:T(1024)S(1)} %add_rsqrt_fusion.1, ...), kind=kOutput, calls=%fused_computation.11 | convolution fusion | flops 4854644736 | bytes 26765312 | tf_op jit(solution)/shard_map/cdf,dt->cft/dot_general | solution.py:303
  187.7 9.7 %fusion.69 = (f32[1024]{0:T(1024)S(1)}, f32[768,1024]{1,0:T(8,128)S(1)}) fusion(f32[768]{0:T(1024)S(1)} %add.423, bf16[4,768,1024]{1,2,0:T(8,128)(2,1)} %get-tuple-element.107, bf16[4,768,768]{2,1,0:T(8,128)(2,1)} %bitcast.242, f32[768]{0:T(1024)S(1)} %add.413, f32[768]{0:T(1024)S(1)} %mul.195, f32[1024]{0:T(1024)S(1)} %add_rsqrt_fusion.1, ...), kind=kOutput, calls=%fused_computation.231 | convolution fusion | flops 4837342208 | bytes 17323008 | tf_op jit(solution)/shard_map/cdf,cft->dt/dot_general | solution.py:308
  199.0 2.8 fusion.64
  201.8 6.8 %convolution_convert_fusion = bf16[4,768,768]{1,2,0:T(8,128)(2,1)} fusion(bf16[4,768,1024]{1,2,0:T(8,128)(2,1)S(1)} %copy-done.31, f32[768,1024]{1,0:T(8,128)S(1)} %get-tuple-element.63), kind=kOutput, calls=%fused_computation.48 | convolution fusion | flops 4834983936 | bytes 14155776 | tf_op jit(solution)/shard_map/dt,cft->cdf/dot_general | solution.py:319
  208.5 12.8 %fusion.70 = (f32[4,768]{1,0:T(4,128)}, bf16[4,768,1024]{1,2,0:T(8,128)(2,1)S(1)}) fusion(f32[1024,4,768]{2,0,1:T(8,128)} %get-tuple-element.108, f32[4,768]{1,0:T(4,128)S(1)} %add.416, bf16[4,768,768]{2,1,0:T(8,128)(2,1)S(1)} %bitcast.245, f32[768,1024]{1,0:T(8,128)S(1)} %get-tuple-element.63), kind=kOutput, calls=%fused_computation.232 | convolution fusion | flops 4870370304 | bytes 26763264 | tf_op jit(solution)/shard_map/cdf,dt->cft/dot_general | solution.py:321
  221.4 7.2 %fusion.18 = bf16[4,768,768]{1,2,0:T(8,128)(2,1)} fusion(bf16[4,768,1024]{1,2,0:T(8,128)(2,1)S(1)} %get-tuple-element.113, f32[768,1024]{1,0:T(8,128)S(1)} %copy-done.1, f32[768]{0:T(1024)S(1)} %add.413, f32[768]{0:T(1024)S(1)} %mul.195, f32[1024]{0:T(1024)S(1)} %add_rsqrt_fusion.1, f32[1024]{0:T(1024)S(1)} %broadcast_multiply_fusion.5), kind=kOutput, calls=%fused_computation.49 | convolution fusion | flops 4838129664 | bytes 14170112 | tf_op jit(solution)/shard_map/dt,cft->cdf/dot_general | solution.py:324
  228.6 6.5 %multiply_reduce_fusion.1 = (f32[768]{0:T(1024)}, f32[1024]{0:T(1024)S(1)}, f32[1024]{0:T(1024)S(1)}, f32[768]{0:T(1024)}, f32[768,1024]{1,0:T(8,128)S(1)}) fusion(f32[768,1024]{1,0:T(8,128)S(1)} %copy-done.1, f32[1024]{0:T(1024)S(1)} %add_rsqrt_fusion.1, f32[1024]{0:T(1024)S(1)} %broadcast_multiply_fusion.5, f32[768]{0:T(1024)S(1)} %mul.195, ...), kind=kOutput, calls=%fused_computation.30 | convolution fusion | flops 4839698432 | bytes 20472832 | tf_op jit(solution)/shard_map/cdf,cft->dt/dot_general | solution.py:326
  239.1 2.9 convolution_convert_fusion.1
  241.9 40.7 %attend_backward.1 = (bf16[4,2,3,64,1024]{4,3,2,1,0:T(8,128)(2,1)}, bf16[4,1,3,64,1024]{4,3,2,1,0:T(8,128)(2,1)}, f32[12,2,64,128]{3,2,1,0:T(8,128)}) custom-call(bf16[4,2,3,64,1024]{4,3,2,1,0:T(8,128)(2,1)} %bitcast.248, bf16[4,2,3,64,1024]{4,3,2,1,0:T(8,128)(2,1)} %bitcast.249, bf16[4,1,3,64,1024]{4,3,2,1,0:T(8,128)(2,1)} %bitcast.253, ...), custom_call_target="tpu_custom_call" | custom-call | flops 32212254720 | bytes 12582912 | tf_op jit(solution)/shard_map/attend_backward/pallas_call | solution.py:160
  282.7 4.5 fusion.33
  287.2 4.6 fusion.38
  301.8 2.5 collective-permute-start.28
  304.4 6.5 %convert_bitcast_fusion = bf16[4,768,384]{1,2,0:T(8,128)(2,1)} fusion(bf16[4,384,1024]{2,1,0:T(8,128)(2,1)} %bitcast.250, bf16[768,1024,1]{1,0,2:T(8,128)(2,1)} %bitcast.8), kind=kOutput, calls=%fused_computation.55 | convolution fusion | flops 2417098752 | bytes 7077888 | tf_op jit(solution)/shard_map/dt,cnt->cdn/dot_general | solution.py:341
  310.8 3.0 copy.90
  314.0 7.0 %fusion.10 = bf16[768,1024]{1,0:T(8,128)(2,1)S(1)} fusion(f32[768,1024,1]{1,0,2:T(8,128)} %fusion.38, f32[768,1024]{1,0:T(8,128)} %copy-done.11, bf16[4,768,384]{2,1,0:T(8,128)(2,1)} %bitcast.215, bf16[4,384,1024]{2,1,0:T(8,128)(2,1)} %bitcast.251), kind=kOutput, calls=%fused_computation.22 | convolution fusion | flops 2418278400 | bytes 13369344 | tf_op jit(solution)/shard_map/cdn,cnt->dt/dot_general | solution.py:346
  328.3 2.8 copy.110
  331.1 3.6 collective-permute-done.29
  337.2 2.1 constant_dynamic-slice_fusion.21
  339.6 2.0 broadcast.130.clone.1
  341.7 2.0 convert_dynamic-update-slice_fusion.3
  343.7 2.0 broadcast.130.clone
  345.7 2.0 convert_dynamic-update-slice_fusion.7
  352.9 2.0 convert_dynamic-update-slice_fusion.2
  354.8 7.6 %collective-permute-done.12 = bf16[192,1024]{1,0:T(8,128)(2,1)} collective-permute-done((bf16[192,1024]{1,0:T(8,128)(2,1)}, bf16[192,1024]{1,0:T(8,128)(2,1)}, u32[]{:S(2)}, u32[]{:S(2)}) %collective-permute-start.12) | collective-permute-done | bytes 393248 | tf_op jit(solution)/shard_map/ppermute | solution.py:228
  362.5 3.0 collective-permute-start.13
  365.4 2.0 convert_dynamic-update-slice_fusion.6
  367.4 15.0 %collective-permute-done.16 = bf16[192,1024]{1,0:T(8,128)(2,1)S(1)} collective-permute-done((bf16[192,1024]{1,0:T(8,128)(2,1)}, bf16[192,1024]{1,0:T(8,128)(2,1)S(1)}, u32[]{:S(2)}, u32[]{:S(2)}) %collective-permute-start.16) | collective-permute-done | bytes 393248 | tf_op jit(solution)/shard_map/ppermute | solution.py:228
  383.5 15.7 %collective-permute-done.13 = bf16[192,1024]{1,0:T(8,128)(2,1)S(1)} collective-permute-done((bf16[192,1024]{1,0:T(8,128)(2,1)}, bf16[192,1024]{1,0:T(8,128)(2,1)S(1)}, u32[]{:S(2)}, u32[]{:S(2)}) %collective-permute-start.13) | collective-permute-done | bytes 393248 | tf_op jit(solution)/shard_map/ppermute | solution.py:228
  401.4 9.4 %collective-permute-done.14 = bf16[192,1024]{1,0:T(8,128)(2,1)S(1)} collective-permute-done((bf16[192,1024]{1,0:T(8,128)(2,1)S(1)}, bf16[192,1024]{1,0:T(8,128)(2,1)S(1)}, u32[]{:S(2)}, u32[]{:S(2)}) %collective-permute-start.14) | collective-permute-done | bytes 393248 | tf_op jit(solution)/shard_map/ppermute | solution.py:228
  415.6 9.6 %collective-permute-done.34 = bf16[2,2,1,1,2,96,192]{6,5,4,3,2,1,0:T(8,128)(2,1)S(1)} collective-permute-done((bf16[2,2,1,1,2,96,192]{6,5,4,3,2,1,0:T(8,128)(2,1)S(1)}, bf16[2,2,1,1,2,96,192]{6,5,4,3,2,1,0:T(8,128)(2,1)S(1)}, u32[]{:S(2)}, u32[]{:S(2)}) %collective-permute-start.34) | collective-permute-done | bytes 294944 | tf_op jit(solution)/shard_map/ppermute | solution.py:190
  427.1 6.0 %collective-permute-done.24 = bf16[2,2,1,1,2,96,192]{6,5,4,3,2,1,0:T(8,128)(2,1)S(1)} collective-permute-done((bf16[2,2,1,1,2,96,192]{6,5,4,3,2,1,0:T(8,128)(2,1)S(1)}, bf16[2,2,1,1,2,96,192]{6,5,4,3,2,1,0:T(8,128)(2,1)S(1)}, u32[]{:S(2)}, u32[]{:S(2)}) %collective-permute-start.24) | collective-permute-done | bytes 294944 | tf_op jit(solution)/shard_map/ppermute | solution.py:190
  435.2 12.6 %collective-permute-start.36 = (bf16[1,2,1,1,1,96,192]{6,5,4,3,2,1,0:T(8,128)(2,1)S(1)}, bf16[1,2,1,1,1,96,192]{6,5,4,3,2,1,0:T(8,128)(2,1)S(1)}, u32[]{:S(2)}, u32[]{:S(2)}) collective-permute-start(bf16[1,2,1,1,1,96,192]{6,5,4,3,2,1,0:T(8,128)(2,1)S(1)} %constant_dynamic-slice_fusion.10), channel_id=1, source_target_pairs={{0,2},{1,3},{2,0},{3,1},{4,6},{5,7},{6,4},{7,5},{8,10},{9,11},{10,... | collective-permute-start | bytes 221192 | tf_op jit(solution)/shard_map/ppermute | solution.py:190
  447.9 4.6 collective-permute-start.26
  455.9 3.6 collective-permute-start.27
  460.2 6.6 %collective-permute-done.19 = bf16[2,2,1,2,1,96,384]{6,5,4,3,2,1,0:T(8,128)(2,1)S(1)} collective-permute-done((bf16[2,2,1,2,1,96,384]{6,5,4,3,2,1,0:T(8,128)(2,1)S(1)}, bf16[2,2,1,2,1,96,384]{6,5,4,3,2,1,0:T(8,128)(2,1)S(1)}, u32[]{:S(2)}, u32[]{:S(2)}) %collective-permute-start.19) | collective-permute-done | bytes 589856 | tf_op jit(solution)/shard_map/ppermute | solution.py:190
  468.7 2.4 add_convert_fusion.1
  472.0 2.4 add_convert_fusion.2
  477.6 5.2 collective-permute-done.21
  482.8 3.4 collective-permute-start.22
  486.1 13.0 %collective-permute-done.44 = bf16[2,2,1,1,2,96,768]{6,5,4,3,2,1,0:T(8,128)(2,1)S(1)} collective-permute-done((bf16[2,2,1,1,2,96,768]{6,5,4,3,2,1,0:T(8,128)(2,1)S(1)}, bf16[2,2,1,1,2,96,768]{6,5,4,3,2,1,0:T(8,128)(2,1)S(1)}, u32[]{:S(2)}, u32[]{:S(2)}) %collective-permute-start.44) | collective-permute-done | bytes 1179680 | tf_op jit(solution)/shard_map/ppermute | solution.py:190
  504.9 7.4 %collective-permute-done.45 = bf16[2,2,1,1,1,96,768]{6,5,4,3,2,1,0:T(8,128)(2,1)} collective-permute-done((bf16[2,2,1,1,1,96,768]{6,5,4,3,2,1,0:T(8,128)(2,1)S(1)}, bf16[2,2,1,1,1,96,768]{6,5,4,3,2,1,0:T(8,128)(2,1)}, u32[]{:S(2)}, u32[]{:S(2)}) %collective-permute-start.45) | collective-permute-done | bytes 589856 | tf_op jit(solution)/shard_map/ppermute | solution.py:190
  517.9 18.1 %collective-permute-done.46 = bf16[1,2,1,1,1,96,768]{6,5,4,3,2,1,0:T(8,128)(2,1)S(1)} collective-permute-done((bf16[1,2,1,1,1,96,768]{6,5,4,3,2,1,0:T(8,128)(2,1)S(1)}, bf16[1,2,1,1,1,96,768]{6,5,4,3,2,1,0:T(8,128)(2,1)S(1)}, u32[]{:S(2)}, u32[]{:S(2)}) %collective-permute-start.46) | collective-permute-done | bytes 294944 | tf_op jit(solution)/shard_map/ppermute | solution.py:190
  536.2 3.0 collective-permute-done.41
  539.3 3.5 collective-permute-done.47
  (323 shorter events, 108.2 us)
Async XLA Ops:
  7.2 18.4 %copy-start.14 = (bf16[192,4096]{1,0:T(8,128)(2,1)S(1)}, bf16[192,4096]{1,0:T(8,128)(2,1)}, u32[]{:S(2)}) copy-start(bf16[192,4096]{1,0:T(8,128)(2,1)} %param.14) | copy-start | bytes 4718596
  7.2 166.8 %all-gather.3.cloned.1.call-start = ((), (), s32[]{:S(2)}) async-start(), calls=%async_computation.2 | async-start | bytes 4866048 | tf_op jit(solution)/shard_map/all_gather | solution.py:252
  9.9 6.5 %collective-permute-start = (bf16[1,1,1,1,1,96,384]{5,6,4,3,2,1,0:T(8,128)(2,1)S(1)}, bf16[1,1,1,1,1,96,384]{5,6,4,3,2,1,0:T(8,128)(2,1)S(1)}, u32[]{:S(2)}, u32[]{:S(2)}) collective-permute-start(bf16[1,1,1,1,1,96,384]{5,6,4,3,2,1,0:T(8,128)(2,1)S(1)} %maximum_bitcast_fusion), channel_id=1, source_target_pairs={{0,1},{1,0},{2,3},{3,2},{4,5},{5,4},{6,7},{7,6},{8,9},{9,8},{10,11... | collective-permute-start | bytes 221192 | tf_op jit(solution)/shard_map/ppermute | solution.py:190
  13.1 7.2 %collective-permute-start.5 = (bf16[1,1,1,1,1,96,384]{5,6,4,3,2,1,0:T(8,128)(2,1)S(1)}, bf16[1,1,1,1,1,96,384]{5,6,4,3,2,1,0:T(8,128)(2,1)S(1)}, u32[]{:S(2)}, u32[]{:S(2)}) collective-permute-start(bf16[1,1,1,1,1,96,384]{5,6,4,3,2,1,0:T(8,128)(2,1)S(1)} %slice_bitcast_fusion), channel_id=1, source_target_pairs={{0,1},{1,0},{2,3},{3,2},{4,5},{5,4},{6,7},{7,6},{8,9},{9,8},{10,11... | collective-permute-start | bytes 221192 | tf_op jit(solution)/shard_map/ppermute | solution.py:190
  17.2 27.3 %collective-permute-start.1 = (bf16[1,2,1,1,1,96,384]{5,6,4,3,2,1,0:T(8,128)(2,1)}, bf16[1,2,1,1,1,96,384]{5,6,4,3,2,1,0:T(8,128)(2,1)}, u32[]{:S(2)}, u32[]{:S(2)}) collective-permute-start(bf16[1,2,1,1,1,96,384]{5,6,4,3,2,1,0:T(8,128)(2,1)} %pad_maximum_fusion.8), channel_id=1, source_target_pairs={{0,2},{1,3},{2,0},{3,1},{4,6},{5,7},{6,4},{7,5},{8,10},{9,11},{10,... | collective-permute-start | bytes 442376 | tf_op jit(solution)/shard_map/ppermute | solution.py:190
  21.0 28.4 %collective-permute-start.6 = (bf16[1,2,1,1,1,96,384]{5,6,4,3,2,1,0:T(8,128)(2,1)}, bf16[1,2,1,1,1,96,384]{5,6,4,3,2,1,0:T(8,128)(2,1)}, u32[]{:S(2)}, u32[]{:S(2)}) collective-permute-start(bf16[1,2,1,1,1,96,384]{5,6,4,3,2,1,0:T(8,128)(2,1)} %pad_maximum_fusion.9), channel_id=1, source_target_pairs={{0,2},{1,3},{2,0},{3,1},{4,6},{5,7},{6,4},{7,5},{8,10},{9,11},{10,... | collective-permute-start | bytes 442376 | tf_op jit(solution)/shard_map/ppermute | solution.py:190
  23.1 49.5 %collective-permute-start.10 = (f32[1,1,12,192]{3,2,1,0:T(8,128)S(1)}, f32[1,1,12,192]{3,2,1,0:T(8,128)}, u32[]{:S(2)}, u32[]{:S(2)}) collective-permute-start(f32[1,1,12,192]{3,2,1,0:T(8,128)S(1)} %bitcast.231), channel_id=1, source_target_pairs={{0,2},{1,3},{2,0},{3,1},{4,6},{5,7},{6,4},{7,5},{8,10},{9,11},{10,... | collective-permute-start | bytes 27656 | tf_op jit(solution)/shard_map/ppermute | solution.py:190
  26.9 84.7 %all-to-all-start = ((bf16[192,4,1024]{2,0,1:T(8,128)(2,1)}), bf16[192,4,1024]{2,0,1:T(8,128)(2,1)}, u32[]{:S(2)}, u32[]{:S(2)}) async-start(bf16[192,4,1024]{2,0,1:T(8,128)(2,1)} %bitcast.194), calls=%async_computation | async-start | bytes 3145728 | tf_op jit(solution)/shard_map/all_to_all | solution.py:278
  31.4 156.3 %all-gather.5.cloned.1.call-start = ((), (), s32[]{:S(2)}) async-start(), calls=%async_computation.3 | async-start | bytes 4866048 | tf_op jit(solution)/shard_map/all_gather | solution.py:252
  50.7 11.6 %collective-permute-start.2 = (bf16[2,2,1,1,1,96,384]{5,6,4,3,2,1,0:T(8,128)(2,1)S(1)}, bf16[2,2,1,1,1,96,384]{5,6,4,3,2,1,0:T(8,128)(2,1)S(1)}, u32[]{:S(2)}, u32[]{:S(2)}) collective-permute-start(bf16[2,2,1,1,1,96,384]{5,6,4,3,2,1,0:T(8,128)(2,1)S(1)} %pad_maximum_fusion.6), channel_id=1, source_target_pairs={{0,8},{4,12},{8,0},{12,4},{1,9},{5,13},{9,1},{13,5},{2,10},{6,14},... | collective-permute-start | bytes 884744 | tf_op jit(solution)/shard_map/ppermute | solution.py:190
  54.8 13.5 %collective-permute-start.7 = (bf16[2,2,1,1,1,96,384]{5,6,4,3,2,1,0:T(8,128)(2,1)S(1)}, bf16[2,2,1,1,1,96,384]{5,6,4,3,2,1,0:T(8,128)(2,1)}, u32[]{:S(2)}, u32[]{:S(2)}) collective-permute-start(bf16[2,2,1,1,1,96,384]{5,6,4,3,2,1,0:T(8,128)(2,1)S(1)} %pad_maximum_fusion.7), channel_id=1, source_target_pairs={{0,4},{4,0},{8,12},{12,8},{1,5},{5,1},{9,13},{13,9},{2,6},{6,2},{1... | collective-permute-start | bytes 884744 | tf_op jit(solution)/shard_map/ppermute | solution.py:190
  62.9 19.6 %collective-permute-start.3 = (bf16[2,2,1,2,1,96,384]{6,5,4,3,2,1,0:T(8,128)(2,1)S(1)}, bf16[2,2,1,2,1,96,384]{6,5,4,3,2,1,0:T(8,128)(2,1)}, u32[]{:S(2)}, u32[]{:S(2)}) collective-permute-start(bf16[2,2,1,2,1,96,384]{6,5,4,3,2,1,0:T(8,128)(2,1)S(1)} %copy.68), channel_id=1, source_target_pairs={{0,4},{4,0},{8,12},{12,8},{1,5},{5,1},{9,13},{13,9},{2,6},{6,2},{1... | collective-permute-start | bytes 1769480 | tf_op jit(solution)/shard_map/ppermute | solution.py:190
  71.4 21.6 %collective-permute-start.8 = (bf16[2,2,1,1,2,96,384]{6,5,4,3,2,1,0:T(8,128)(2,1)}, bf16[2,2,1,1,2,96,384]{6,5,4,3,2,1,0:T(8,128)(2,1)}, u32[]{:S(2)}, u32[]{:S(2)}) collective-permute-start(bf16[2,2,1,1,2,96,384]{6,5,4,3,2,1,0:T(8,128)(2,1)} %copy.76), channel_id=1, source_target_pairs={{0,8},{4,12},{8,0},{12,4},{1,9},{5,13},{9,1},{13,5},{2,10},{6,14},... | collective-permute-start | bytes 1769480 | tf_op jit(solution)/shard_map/ppermute | solution.py:190
  74.0 24.7 %collective-permute-start.11 = (f32[2,1,12,192]{3,2,1,0:T(8,128)}, f32[2,1,12,192]{3,2,1,0:T(8,128)}, u32[]{:S(2)}, u32[]{:S(2)}) collective-permute-start(f32[2,1,12,192]{3,2,1,0:T(8,128)} %pad_maximum_fusion.11), channel_id=1, source_target_pairs={{0,1},{1,0},{2,3},{3,2},{4,5},{5,4},{6,7},{7,6},{8,9},{9,8},{10,11... | collective-permute-start | bytes 55304 | tf_op jit(solution)/shard_map/ppermute | solution.py:190
  86.0 14.2 %collective-permute-start.4 = (bf16[2,2,1,2,2,96,384]{6,5,4,3,2,1,0:T(8,128)(2,1)}, bf16[2,2,1,2,2,96,384]{6,5,4,3,2,1,0:T(8,128)(2,1)}, u32[]{:S(2)}, u32[]{:S(2)}) collective-permute-start(bf16[2,2,1,2,2,96,384]{6,5,4,3,2,1,0:T(8,128)(2,1)} %copy.71), channel_id=1, source_target_pairs={{0,16},{16,0},{1,17},{17,1},{2,18},{18,2},{3,19},{19,3},{4,20},{20... | collective-permute-start | bytes 3538952 | tf_op jit(solution)/shard_map/ppermute | solution.py:190
  98.7 7.1 %collective-permute-start.9 = (bf16[2,2,1,2,2,96,384]{6,5,4,3,2,1,0:T(8,128)(2,1)}, bf16[2,2,1,2,2,96,384]{6,5,4,3,2,1,0:T(8,128)(2,1)}, u32[]{:S(2)}, u32[]{:S(2)}) collective-permute-start(bf16[2,2,1,2,2,96,384]{6,5,4,3,2,1,0:T(8,128)(2,1)} %copy.79), channel_id=1, source_target_pairs={{0,16},{16,0},{1,17},{17,1},{2,18},{18,2},{3,19},{19,3},{4,20},{20... | collective-permute-start | bytes 3538952 | tf_op jit(solution)/shard_map/ppermute | solution.py:190
  111.6 61.7 %all-to-all-start.1 = ((bf16[192,4,1024]{2,0,1:T(8,128)(2,1)}), bf16[192,4,1024]{2,0,1:T(8,128)(2,1)S(1)}, u32[]{:S(2)}, u32[]{:S(2)}) async-start(bf16[192,4,1024]{2,0,1:T(8,128)(2,1)} %bitcast.198), calls=%async_computation.1 | async-start | bytes 3145728 | tf_op jit(solution)/shard_map/all_to_all | solution.py:278
  201.8 26.8 %slice-start.8 = ((s8[4718592]{0:T(1024)(128)(4,1)}), s8[4194304]{0:T(1024)(128)(4,1)S(1)}, s32[]{:S(2)}) async-start(s8[4718592]{0:T(1024)(128)(4,1)} %bitcast.239), calls=%async_computation.12 | async-start | bytes 8388608
  208.5 12.9 %copy-start.1 = (f32[768,1024]{1,0:T(8,128)S(1)}, f32[768,1024]{1,0:T(8,128)}, u32[]{:S(2)}) copy-start(f32[768,1024]{1,0:T(8,128)} %copy-done) | copy-start | bytes 9437188
  208.5 20.1 %slice-start.9 = ((s8[4718592]{0:T(1024)(128)(4,1)}), s8[524288]{0:T(1024)(128)(4,1)S(1)}, s32[]{:S(2)}) async-start(s8[4718592]{0:T(1024)(128)(4,1)} %bitcast.239), calls=%async_computation.13 | async-start | bytes 1048576
  282.7 11.5 %slice-start = ((s8[4718592]{0:T(1024)(128)(4,1)}), s8[4194304]{0:T(1024)(128)(4,1)S(1)}, s32[]{:S(2)}) async-start(s8[4718592]{0:T(1024)(128)(4,1)} %bitcast.203), calls=%async_computation.4 | async-start | bytes 8388608
  293.4 175.3 %collective-permute-start.43 = (bf16[2,2,1,2,2,96,768]{6,5,4,3,2,1,0:T(8,128)(2,1)}, bf16[2,2,1,2,2,96,768]{6,5,4,3,2,1,0:T(8,128)(2,1)}, u32[]{:S(2)}, u32[]{:S(2)}) collective-permute-start(bf16[2,2,1,2,2,96,768]{6,5,4,3,2,1,0:T(8,128)(2,1)} %constant_dynamic-slice_fusion.3), channel_id=1, source_target_pairs={{0,16},{16,0},{1,17},{17,1},{2,18},{18,2},{3,19},{19,3},{4,20},{20... | collective-permute-start | bytes 7077896 | tf_op jit(solution)/shard_map/ppermute | solution.py:190
  295.8 176.2 %collective-permute-start.38 = (bf16[2,2,1,2,2,96,768]{6,5,4,3,2,1,0:T(8,128)(2,1)}, bf16[2,2,1,2,2,96,768]{6,5,4,3,2,1,0:T(8,128)(2,1)}, u32[]{:S(2)}, u32[]{:S(2)}) collective-permute-start(bf16[2,2,1,2,2,96,768]{6,5,4,3,2,1,0:T(8,128)(2,1)} %constant_dynamic-slice_fusion.8), channel_id=1, source_target_pairs={{0,16},{16,0},{1,17},{17,1},{2,18},{18,2},{3,19},{19,3},{4,20},{20... | collective-permute-start | bytes 7077896 | tf_op jit(solution)/shard_map/ppermute | solution.py:190
  297.6 114.1 %collective-permute-start.33 = (bf16[2,2,1,2,2,96,192]{6,5,4,3,2,1,0:T(8,128)(2,1)}, bf16[2,2,1,2,2,96,192]{6,5,4,3,2,1,0:T(8,128)(2,1)}, u32[]{:S(2)}, u32[]{:S(2)}) collective-permute-start(bf16[2,2,1,2,2,96,192]{6,5,4,3,2,1,0:T(8,128)(2,1)} %constant_dynamic-slice_fusion.13), channel_id=1, source_target_pairs={{0,16},{16,0},{1,17},{17,1},{2,18},{18,2},{3,19},{19,3},{4,20},{20... | collective-permute-start | bytes 1769480 | tf_op jit(solution)/shard_map/ppermute | solution.py:190
  301.8 22.9 %collective-permute-start.28 = (f32[1,2,12,192]{3,2,1,0:T(8,128)}, f32[1,2,12,192]{3,2,1,0:T(8,128)}, u32[]{:S(2)}, u32[]{:S(2)}) collective-permute-start(f32[1,2,12,192]{3,2,1,0:T(8,128)} %fusion.54), channel_id=1, source_target_pairs={{0,2},{1,3},{2,0},{3,1},{4,6},{5,7},{6,4},{7,5},{8,10},{9,11},{10,... | collective-permute-start | bytes 55304 | tf_op jit(solution)/shard_map/ppermute | solution.py:190
  314.0 10.7 %copy-start.21 = (f32[4,8,192]{2,1,0:T(8,128)S(1)}, f32[4,8,192]{2,1,0:T(8,128)}, u32[]{:S(2)}) copy-start(f32[4,8,192]{2,1,0:T(8,128)} %copy-done.20) | copy-start | bytes 73732
  323.2 29.1 %collective-permute-start.15 = (bf16[192,1024]{1,0:T(8,128)(2,1)}, bf16[192,1024]{1,0:T(8,128)(2,1)}, u32[]{:S(2)}, u32[]{:S(2)}) collective-permute-start(bf16[192,1024]{1,0:T(8,128)(2,1)} %get-tuple-element.73), channel_id=1, source_target_pairs={{0,1},{1,0},{2,3},{3,2},{4,5},{5,4},{6,7},{7,6},{8,9},{9,8},{10,11... | collective-permute-start | bytes 1179656 | tf_op jit(solution)/shard_map/ppermute | solution.py:228
  326.7 8.0 %collective-permute-start.29 = (f32[1,1,12,192]{3,2,1,0:T(8,128)}, f32[1,1,12,192]{3,2,1,0:T(8,128)S(1)}, u32[]{:S(2)}, u32[]{:S(2)}) collective-permute-start(f32[1,1,12,192]{3,2,1,0:T(8,128)} %constant_dynamic-slice_fusion.14), channel_id=1, source_target_pairs={{0,1},{1,0},{2,3},{3,2},{4,5},{5,4},{6,7},{7,6},{8,9},{9,8},{10,11... | collective-permute-start | bytes 27656 | tf_op jit(solution)/shard_map/ppermute | solution.py:190
  335.4 3.8 collective-permute-start.30
  339.3 4.3 collective-permute-start.31
  343.6 4.1 collective-permute-start.32
  347.7 14.8 %collective-permute-start.12 = (bf16[192,1024]{1,0:T(8,128)(2,1)}, bf16[192,1024]{1,0:T(8,128)(2,1)}, u32[]{:S(2)}, u32[]{:S(2)}) collective-permute-start(bf16[192,1024]{1,0:T(8,128)(2,1)} %get-tuple-element.76), channel_id=1, source_target_pairs={{0,1},{1,0},{2,3},{3,2},{4,5},{5,4},{6,7},{7,6},{8,9},{9,8},{10,11... | collective-permute-start | bytes 1179656 | tf_op jit(solution)/shard_map/ppermute | solution.py:228
  351.2 48.0 %copy-start.19 = (bf16[192,1024]{1,0:T(8,128)(2,1)S(1)}, bf16[192,1024]{1,0:T(8,128)(2,1)}, u32[]{:S(2)}) copy-start(bf16[192,1024]{1,0:T(8,128)(2,1)} %get-tuple-element.74) | copy-start | bytes 1179652
  351.2 59.5 %copy-start.17 = (bf16[2,2,1,2,2,96,192]{6,5,4,3,2,1,0:T(8,128)(2,1)S(1)}, bf16[2,2,1,2,2,96,192]{6,5,4,3,2,1,0:T(8,128)(2,1)}, u32[]{:S(2)}) copy-start(bf16[2,2,1,2,2,96,192]{6,5,4,3,2,1,0:T(8,128)(2,1)} %constant_dynamic-slice_fusion.21) | copy-start | bytes 1769476
  352.3 30.0 %collective-permute-start.16 = (bf16[192,1024]{1,0:T(8,128)(2,1)}, bf16[192,1024]{1,0:T(8,128)(2,1)S(1)}, u32[]{:S(2)}, u32[]{:S(2)}) collective-permute-start(bf16[192,1024]{1,0:T(8,128)(2,1)} %get-tuple-element.72), channel_id=1, source_target_pairs={{0,2},{1,3},{2,0},{3,1},{4,6},{5,7},{6,4},{7,5},{8,10},{9,11},{10,... | collective-permute-start | bytes 1179656 | tf_op jit(solution)/shard_map/ppermute | solution.py:228
  354.8 56.9 %copy-start.7 = (bf16[4,768,192]{2,1,0:T(8,128)(2,1)S(1)}, bf16[4,768,192]{2,1,0:T(8,128)(2,1)}, u32[]{:S(2)}) copy-start(bf16[4,768,192]{2,1,0:T(8,128)(2,1)} %copy-done.6) | copy-start | bytes 3538948
  362.5 36.7 %collective-permute-start.13 = (bf16[192,1024]{1,0:T(8,128)(2,1)}, bf16[192,1024]{1,0:T(8,128)(2,1)S(1)}, u32[]{:S(2)}, u32[]{:S(2)}) collective-permute-start(bf16[192,1024]{1,0:T(8,128)(2,1)} %get-tuple-element.75), channel_id=1, source_target_pairs={{0,2},{1,3},{2,0},{3,1},{4,6},{5,7},{6,4},{7,5},{8,10},{9,11},{10,... | collective-permute-start | bytes 1179656 | tf_op jit(solution)/shard_map/ppermute | solution.py:228
  382.3 18.0 %collective-permute-start.17 = (bf16[192,1024]{1,0:T(8,128)(2,1)}, bf16[192,1024]{1,0:T(8,128)(2,1)S(1)}, u32[]{:S(2)}, u32[]{:S(2)}) collective-permute-start(bf16[192,1024]{1,0:T(8,128)(2,1)} %get-tuple-element.71), channel_id=1, source_target_pairs={{0,3},{1,2},{2,1},{3,0},{4,7},{5,6},{6,5},{7,4},{8,11},{9,10},{10,... | collective-permute-start | bytes 1179656 | tf_op jit(solution)/shard_map/ppermute | solution.py:228
  399.2 15.5 %copy-start.9 = (bf16[4,768,192]{2,1,0:T(8,128)(2,1)S(1)}, bf16[4,768,192]{2,1,0:T(8,128)(2,1)}, u32[]{:S(2)}) copy-start(bf16[4,768,192]{2,1,0:T(8,128)(2,1)} %copy.110) | copy-start | bytes 3538948
  399.2 11.5 %collective-permute-start.14 = (bf16[192,1024]{1,0:T(8,128)(2,1)S(1)}, bf16[192,1024]{1,0:T(8,128)(2,1)S(1)}, u32[]{:S(2)}, u32[]{:S(2)}) collective-permute-start(bf16[192,1024]{1,0:T(8,128)(2,1)S(1)} %copy-done.19), channel_id=1, source_target_pairs={{0,3},{1,2},{2,1},{3,0},{4,7},{5,6},{6,5},{7,4},{8,11},{9,10},{10,... | collective-permute-start | bytes 1179656 | tf_op jit(solution)/shard_map/ppermute | solution.py:228
  400.4 52.2 %collective-permute-start.18 = (bf16[2,2,1,2,2,96,384]{6,5,4,3,2,1,0:T(8,128)(2,1)S(1)}, bf16[2,2,1,2,2,96,384]{6,5,4,3,2,1,0:T(8,128)(2,1)S(1)}, u32[]{:S(2)}, u32[]{:S(2)}) collective-permute-start(bf16[2,2,1,2,2,96,384]{6,5,4,3,2,1,0:T(8,128)(2,1)S(1)} %constant_dynamic-slice_fusion.26), channel_id=1, source_target_pairs={{0,16},{16,0},{1,17},{17,1},{2,18},{18,2},{3,19},{19,3},{4,20},{20... | collective-permute-start | bytes 3538952 | tf_op jit(solution)/shard_map/ppermute | solution.py:190
  410.7 4.0 collective-permute-start.23
  413.1 12.1 %collective-permute-start.34 = (bf16[2,2,1,1,2,96,192]{6,5,4,3,2,1,0:T(8,128)(2,1)S(1)}, bf16[2,2,1,1,2,96,192]{6,5,4,3,2,1,0:T(8,128)(2,1)S(1)}, u32[]{:S(2)}, u32[]{:S(2)}) collective-permute-start(bf16[2,2,1,1,2,96,192]{6,5,4,3,2,1,0:T(8,128)(2,1)S(1)} %constant_dynamic-slice_fusion.12), channel_id=1, source_target_pairs={{0,8},{4,12},{8,0},{12,4},{1,9},{5,13},{9,1},{13,5},{2,10},{6,14},... | collective-permute-start | bytes 884744 | tf_op jit(solution)/shard_map/ppermute | solution.py:190
  415.0 18.1 %collective-permute-start.24 = (bf16[2,2,1,1,2,96,192]{6,5,4,3,2,1,0:T(8,128)(2,1)S(1)}, bf16[2,2,1,1,2,96,192]{6,5,4,3,2,1,0:T(8,128)(2,1)S(1)}, u32[]{:S(2)}, u32[]{:S(2)}) collective-permute-start(bf16[2,2,1,1,2,96,192]{6,5,4,3,2,1,0:T(8,128)(2,1)S(1)} %constant_dynamic-slice_fusion.20), channel_id=1, source_target_pairs={{0,8},{4,12},{8,0},{12,4},{1,9},{5,13},{9,1},{13,5},{2,10},{6,14},... | collective-permute-start | bytes 884744 | tf_op jit(solution)/shard_map/ppermute | solution.py:190
  425.3 9.8 %collective-permute-start.35 = (bf16[2,2,1,1,1,96,192]{6,5,4,3,2,1,0:T(8,128)(2,1)S(1)}, bf16[2,2,1,1,1,96,192]{6,5,4,3,2,1,0:T(8,128)(2,1)S(1)}, u32[]{:S(2)}, u32[]{:S(2)}) collective-permute-start(bf16[2,2,1,1,1,96,192]{6,5,4,3,2,1,0:T(8,128)(2,1)S(1)} %constant_dynamic-slice_fusion.11), channel_id=1, source_target_pairs={{0,4},{4,0},{8,12},{12,8},{1,5},{5,1},{9,13},{13,9},{2,6},{6,2},{1... | collective-permute-start | bytes 442376 | tf_op jit(solution)/shard_map/ppermute | solution.py:190
  433.3 14.5 %collective-permute-start.25 = (bf16[2,2,1,1,1,96,192]{6,5,4,3,2,1,0:T(8,128)(2,1)S(1)}, bf16[2,2,1,1,1,96,192]{6,5,4,3,2,1,0:T(8,128)(2,1)S(1)}, u32[]{:S(2)}, u32[]{:S(2)}) collective-permute-start(bf16[2,2,1,1,1,96,192]{6,5,4,3,2,1,0:T(8,128)(2,1)S(1)} %constant_dynamic-slice_fusion.19), channel_id=1, source_target_pairs={{0,4},{4,0},{8,12},{12,8},{1,5},{5,1},{9,13},{13,9},{2,6},{6,2},{1... | collective-permute-start | bytes 442376 | tf_op jit(solution)/shard_map/ppermute | solution.py:190
  435.2 17.3 %collective-permute-start.36 = (bf16[1,2,1,1,1,96,192]{6,5,4,3,2,1,0:T(8,128)(2,1)S(1)}, bf16[1,2,1,1,1,96,192]{6,5,4,3,2,1,0:T(8,128)(2,1)S(1)}, u32[]{:S(2)}, u32[]{:S(2)}) collective-permute-start(bf16[1,2,1,1,1,96,192]{6,5,4,3,2,1,0:T(8,128)(2,1)S(1)} %constant_dynamic-slice_fusion.10), channel_id=1, source_target_pairs={{0,2},{1,3},{2,0},{3,1},{4,6},{5,7},{6,4},{7,5},{8,10},{9,11},{10,... | collective-permute-start | bytes 221192 | tf_op jit(solution)/shard_map/ppermute | solution.py:190
  447.8 20.9 %slice-start.6 = ((s8[4718592]{0:T(1024)(128)(4,1)}), s8[4194304]{0:T(1024)(128)(4,1)S(1)}, s32[]{:S(2)}) async-start(s8[4718592]{0:T(1024)(128)(4,1)} %bitcast.212), calls=%async_computation.10 | async-start | bytes 8388608
  447.9 7.9 %collective-permute-start.26 = (bf16[1,2,1,1,1,96,192]{6,5,4,3,2,1,0:T(8,128)(2,1)S(1)}, bf16[1,2,1,1,1,96,192]{6,5,4,3,2,1,0:T(8,128)(2,1)S(1)}, u32[]{:S(2)}, u32[]{:S(2)}) collective-permute-start(bf16[1,2,1,1,1,96,192]{6,5,4,3,2,1,0:T(8,128)(2,1)S(1)} %constant_dynamic-slice_fusion.18), channel_id=1, source_target_pairs={{0,2},{1,3},{2,0},{3,1},{4,6},{5,7},{6,4},{7,5},{8,10},{9,11},{10,... | collective-permute-start | bytes 221192 | tf_op jit(solution)/shard_map/ppermute | solution.py:190
  452.6 16.1 %slice-start.7 = ((s8[4718592]{0:T(1024)(128)(4,1)}), s8[524288]{0:T(1024)(128)(4,1)S(1)}, s32[]{:S(2)}) async-start(s8[4718592]{0:T(1024)(128)(4,1)} %bitcast.212), calls=%async_computation.11 | async-start | bytes 1048576
  453.0 13.8 %collective-permute-start.19 = (bf16[2,2,1,2,1,96,384]{6,5,4,3,2,1,0:T(8,128)(2,1)S(1)}, bf16[2,2,1,2,1,96,384]{6,5,4,3,2,1,0:T(8,128)(2,1)S(1)}, u32[]{:S(2)}, u32[]{:S(2)}) collective-permute-start(bf16[2,2,1,2,1,96,384]{6,5,4,3,2,1,0:T(8,128)(2,1)S(1)} %constant_dynamic-slice_fusion.25), channel_id=1, source_target_pairs={{0,4},{4,0},{8,12},{12,8},{1,5},{5,1},{9,13},{13,9},{2,6},{6,2},{1... | collective-permute-start | bytes 1769480 | tf_op jit(solution)/shard_map/ppermute | solution.py:190
  454.8 4.7 collective-permute-start.37
  455.9 21.6 %collective-permute-start.27 = (bf16[1,1,1,1,1,96,192]{6,5,4,3,2,1,0:T(8,128)(2,1)S(1)}, bf16[1,1,1,1,1,96,192]{6,5,4,3,2,1,0:T(8,128)(2,1)S(1)}, u32[]{:S(2)}, u32[]{:S(2)}) collective-permute-start(bf16[1,1,1,1,1,96,192]{6,5,4,3,2,1,0:T(8,128)(2,1)S(1)} %constant_dynamic-slice_fusion.17), channel_id=1, source_target_pairs={{0,1},{1,0},{2,3},{3,2},{4,5},{5,4},{6,7},{7,6},{8,9},{9,8},{10,11... | collective-permute-start | bytes 110600 | tf_op jit(solution)/shard_map/ppermute | solution.py:190
  467.0 9.4 %collective-permute-start.20 = (bf16[2,2,1,1,1,96,384]{6,5,4,3,2,1,0:T(8,128)(2,1)S(1)}, bf16[2,2,1,1,1,96,384]{6,5,4,3,2,1,0:T(8,128)(2,1)S(1)}, u32[]{:S(2)}, u32[]{:S(2)}) collective-permute-start(bf16[2,2,1,1,1,96,384]{6,5,4,3,2,1,0:T(8,128)(2,1)S(1)} %constant_dynamic-slice_fusion.24), channel_id=1, source_target_pairs={{0,8},{4,12},{8,0},{12,4},{1,9},{5,13},{9,1},{13,5},{2,10},{6,14},... | collective-permute-start | bytes 884744 | tf_op jit(solution)/shard_map/ppermute | solution.py:190
  471.1 28.0 %collective-permute-start.44 = (bf16[2,2,1,1,2,96,768]{6,5,4,3,2,1,0:T(8,128)(2,1)S(1)}, bf16[2,2,1,1,2,96,768]{6,5,4,3,2,1,0:T(8,128)(2,1)S(1)}, u32[]{:S(2)}, u32[]{:S(2)}) collective-permute-start(bf16[2,2,1,1,2,96,768]{6,5,4,3,2,1,0:T(8,128)(2,1)S(1)} %constant_dynamic-slice_fusion.2), channel_id=1, source_target_pairs={{0,8},{4,12},{8,0},{12,4},{1,9},{5,13},{9,1},{13,5},{2,10},{6,14},... | collective-permute-start | bytes 3538952 | tf_op jit(solution)/shard_map/ppermute | solution.py:190
  474.5 26.8 %collective-permute-start.39 = (bf16[2,2,1,2,1,96,768]{6,5,4,3,2,1,0:T(8,128)(2,1)S(1)}, bf16[2,2,1,2,1,96,768]{6,5,4,3,2,1,0:T(8,128)(2,1)S(1)}, u32[]{:S(2)}, u32[]{:S(2)}) collective-permute-start(bf16[2,2,1,2,1,96,768]{6,5,4,3,2,1,0:T(8,128)(2,1)S(1)} %constant_dynamic-slice_fusion.7), channel_id=1, source_target_pairs={{0,4},{4,0},{8,12},{12,8},{1,5},{5,1},{9,13},{13,9},{2,6},{6,2},{1... | collective-permute-start | bytes 3538952 | tf_op jit(solution)/shard_map/ppermute | solution.py:190
  476.6 6.1 %collective-permute-start.21 = (bf16[1,2,1,1,1,96,384]{6,5,4,3,2,1,0:T(8,128)(2,1)S(1)}, bf16[1,2,1,1,1,96,384]{6,5,4,3,2,1,0:T(8,128)(2,1)S(1)}, u32[]{:S(2)}, u32[]{:S(2)}) collective-permute-start(bf16[1,2,1,1,1,96,384]{6,5,4,3,2,1,0:T(8,128)(2,1)S(1)} %constant_dynamic-slice_fusion.23), channel_id=1, source_target_pairs={{0,2},{1,3},{2,0},{3,1},{4,6},{5,7},{6,4},{7,5},{8,10},{9,11},{10,... | collective-permute-start | bytes 442376 | tf_op jit(solution)/shard_map/ppermute | solution.py:190
  482.8 21.1 %collective-permute-start.22 = (bf16[1,1,1,1,1,96,384]{6,5,4,3,2,1,0:T(8,128)(2,1)S(1)}, bf16[1,1,1,1,1,96,384]{6,5,4,3,2,1,0:T(8,128)(2,1)S(1)}, u32[]{:S(2)}, u32[]{:S(2)}) collective-permute-start(bf16[1,1,1,1,1,96,384]{6,5,4,3,2,1,0:T(8,128)(2,1)S(1)} %constant_dynamic-slice_fusion.22), channel_id=1, source_target_pairs={{0,1},{1,0},{2,3},{3,2},{4,5},{5,4},{6,7},{7,6},{8,9},{9,8},{10,11... | collective-permute-start | bytes 221192 | tf_op jit(solution)/shard_map/ppermute | solution.py:190
  499.5 12.9 %collective-permute-start.45 = (bf16[2,2,1,1,1,96,768]{6,5,4,3,2,1,0:T(8,128)(2,1)S(1)}, bf16[2,2,1,1,1,96,768]{6,5,4,3,2,1,0:T(8,128)(2,1)}, u32[]{:S(2)}, u32[]{:S(2)}) collective-permute-start(bf16[2,2,1,1,1,96,768]{6,5,4,3,2,1,0:T(8,128)(2,1)S(1)} %constant_dynamic-slice_fusion.1), channel_id=1, source_target_pairs={{0,4},{4,0},{8,12},{12,8},{1,5},{5,1},{9,13},{13,9},{2,6},{6,2},{1... | collective-permute-start | bytes 1769480 | tf_op jit(solution)/shard_map/ppermute | solution.py:190
  502.4 12.7 %collective-permute-start.40 = (bf16[2,2,1,1,1,96,768]{6,5,4,3,2,1,0:T(8,128)(2,1)}, bf16[2,2,1,1,1,96,768]{6,5,4,3,2,1,0:T(8,128)(2,1)}, u32[]{:S(2)}, u32[]{:S(2)}) collective-permute-start(bf16[2,2,1,1,1,96,768]{6,5,4,3,2,1,0:T(8,128)(2,1)} %constant_dynamic-slice_fusion.6), channel_id=1, source_target_pairs={{0,8},{4,12},{8,0},{12,4},{1,9},{5,13},{9,1},{13,5},{2,10},{6,14},... | collective-permute-start | bytes 1769480 | tf_op jit(solution)/shard_map/ppermute | solution.py:190
  513.6 22.4 %collective-permute-start.46 = (bf16[1,2,1,1,1,96,768]{6,5,4,3,2,1,0:T(8,128)(2,1)S(1)}, bf16[1,2,1,1,1,96,768]{6,5,4,3,2,1,0:T(8,128)(2,1)S(1)}, u32[]{:S(2)}, u32[]{:S(2)}) collective-permute-start(bf16[1,2,1,1,1,96,768]{6,5,4,3,2,1,0:T(8,128)(2,1)S(1)} %constant_dynamic-slice_fusion), channel_id=1, source_target_pairs={{0,2},{1,3},{2,0},{3,1},{4,6},{5,7},{6,4},{7,5},{8,10},{9,11},{10,... | collective-permute-start | bytes 884744 | tf_op jit(solution)/shard_map/ppermute | solution.py:190
  516.4 22.7 %collective-permute-start.41 = (bf16[1,2,1,1,1,96,768]{6,5,4,3,2,1,0:T(8,128)(2,1)S(1)}, bf16[1,2,1,1,1,96,768]{6,5,4,3,2,1,0:T(8,128)(2,1)S(1)}, u32[]{:S(2)}, u32[]{:S(2)}) collective-permute-start(bf16[1,2,1,1,1,96,768]{6,5,4,3,2,1,0:T(8,128)(2,1)S(1)} %constant_dynamic-slice_fusion.5), channel_id=1, source_target_pairs={{0,2},{1,3},{2,0},{3,1},{4,6},{5,7},{6,4},{7,5},{8,10},{9,11},{10,... | collective-permute-start | bytes 884744 | tf_op jit(solution)/shard_map/ppermute | solution.py:190
  536.1 6.8 %collective-permute-start.47 = (bf16[1,1,1,1,1,96,768]{6,5,4,3,2,1,0:T(8,128)(2,1)S(1)}, bf16[1,1,1,1,1,96,768]{6,5,4,3,2,1,0:T(8,128)(2,1)S(1)}, u32[]{:S(2)}, u32[]{:S(2)}) collective-permute-start(bf16[1,1,1,1,1,96,768]{6,5,4,3,2,1,0:T(8,128)(2,1)S(1)} %constant_dynamic-slice_fusion.16), channel_id=1, source_target_pairs={{0,1},{1,0},{2,3},{3,2},{4,5},{5,4},{6,7},{7,6},{8,9},{9,8},{10,11... | collective-permute-start | bytes 442376 | tf_op jit(solution)/shard_map/ppermute | solution.py:190
  539.3 6.1 %collective-permute-start.42 = (bf16[1,1,1,1,1,96,768]{6,5,4,3,2,1,0:T(8,128)(2,1)S(1)}, bf16[1,1,1,1,1,96,768]{6,5,4,3,2,1,0:T(8,128)(2,1)S(1)}, u32[]{:S(2)}, u32[]{:S(2)}) collective-permute-start(bf16[1,1,1,1,1,96,768]{6,5,4,3,2,1,0:T(8,128)(2,1)S(1)} %constant_dynamic-slice_fusion.4), channel_id=1, source_target_pairs={{0,1},{1,0},{2,3},{3,2},{4,5},{5,4},{6,7},{7,6},{8,9},{9,8},{10,11... | collective-permute-start | bytes 442376 | tf_op jit(solution)/shard_map/ppermute | solution.py:190
  (32 other events, 128.9 us)
Sparse Core Ops, SparseCore 0:
  10.9 87.2 all-gather.2
  101.1 78.7 all-gather.4

commit v4 on v3

--- a/solution.py
+++ b/solution.py
@@ -186,50 +186,253 @@
     return [(name, 1 << b) for b in reversed(range(size.bit_length() - 1))]
 
 
-def swap(a, name, bit):
-    return lax.ppermute(a, name, [(i, i ^ bit) for i in range(lax.axis_size(name))])
-
-
 def my_bit(name, bit):
     return (lax.axis_index(name) // bit) % 2
 
 
-def gather_blocks(shard, order):
-    dims = axis_bits("col") + axis_bits("dp") + axis_bits("row")
-    a = shard.reshape((1,) * len(dims) + shard.shape)
-    for name, bit in order:
-        dim = dims.index((name, bit))
-        other = swap(a, name, bit)
-        high = my_bit(name, bit) == 1
-        a = jnp.concatenate([jnp.where(high, other, a), jnp.where(high, a, other)], axis=dim)
-    return a.reshape(lax.axis_size("col"), -1, shard.shape[1])
-
-
-def scatter_blocks(grad, order):
-    dims = axis_bits("col") + axis_bits("dp") + axis_bits("row")
-    rows = grad.shape[0] * grad.shape[1] >> len(dims)
-    a = grad.astype(BF).reshape((2,) * len(dims) + (rows, grad.shape[2]))
-    for name, bit in order:
-        dim = dims.index((name, bit))
-        mine = my_bit(name, bit)
-        other = swap(lax.dynamic_index_in_dim(a, 1 - mine, dim), name, bit)
-        a = lax.dynamic_index_in_dim(a, mine, dim).astype(F32) + other.astype(F32)
-        a = a.astype(BF)
-    return a.reshape(rows, grad.shape[2]).astype(F32)
-
-
-def spread_windows(a):
+def partner(name, bit):
+    return {name: lax.axis_index(name) + bit * (1 - 2 * my_bit(name, bit))}
+
+
+def all_bits():
+    return axis_bits("col") + axis_bits("dp") + axis_bits("row")
+
+
+def col_peer(step):
     cols = lax.axis_size("col")
     col = lax.axis_index("col")
-    rows, seq = a.shape[0] // cols, a.shape[1]
-    parts = [lax.dynamic_slice_in_dim(a, col * rows, rows, axis=0)]
+    return (col + step) % cols, (col + cols - step) % cols
+
+
+def remote(src, dst, send, recv, device):
+    return pltpu.make_async_remote_copy(
+        src_ref=src, dst_ref=dst, send_sem=send, recv_sem=recv, device_id=device,
+        device_id_type=pl.DeviceIdType.MESH,
+    )
+
+
+def meet_partners():
+    barrier = pltpu.get_barrier_semaphore()
+    devices = [partner(name, bit) for name, bit in axis_bits("dp") + axis_bits("row")]
+    devices += [{"col": col_peer(step)[0]} for step in range(1, lax.axis_size("col"))]
+    for device in devices:
+        pl.semaphore_signal(barrier, inc=1, device_id=device, device_id_type=pl.DeviceIdType.MESH)
+    pl.semaphore_wait(barrier, len(devices))
+
+
+def head_kernel(
+    orders, qk_ref, vo_ref, tokens_ref, vectors_ref, full_qk_ref, full_vo_ref, x_ref, all_vectors_ref,
+    own_sem, block_send, block_recv, col_send, col_recv,
+):
+    dims = all_bits()
+    cols, col = lax.axis_size("col"), lax.axis_index("col")
+    feats, seq = tokens_ref.shape[0], x_ref.shape[1]
+    place = [my_bit(name, bit) for name, bit in dims]
+    pieces = [(qk_ref, full_qk_ref), (vo_ref, full_vo_ref)]
+    my_feats = pl.ds(pl.multiple_of(col * feats, 8), feats)
+    own = [pltpu.make_async_copy(src, dst.at[tuple(place)], own_sem.at[i]) for i, (src, dst) in enumerate(pieces)]
+    own.append(
+        pltpu.make_async_copy(
+            tokens_ref.at[:, pl.ds(pl.multiple_of(col * seq, 128), seq)], x_ref.at[my_feats], own_sem.at[2]
+        )
+    )
+    own.append(pltpu.make_async_copy(vectors_ref, all_vectors_ref.at[col], own_sem.at[3]))
+    for copy in own:
+        copy.start()
+    meet_partners()
+
+    def stage(piece, step):
+        src, full = pieces[piece]
+        done = orders[piece][:step]
+        index = tuple(slice(None) if bit in done else at for bit, at in zip(dims, place))
+        return remote(
+            src if step == 0 else full.at[index], full.at[index], block_send.at[piece, step],
+            block_recv.at[piece, step], partner(*orders[piece][step]),
+        )
+
+    stages = [[stage(piece, step) for step in range(len(dims))] for piece in range(2)]
+    for piece in range(2):
+        stages[piece][0].start()
+    transposes = []
     for step in range(1, cols):
-        block = lax.dynamic_slice_in_dim(a, (col ^ step) * rows, rows, axis=0)
-        parts.append(lax.ppermute(block, "col", [(i, i ^ step) for i in range(cols)]))
-    out = jnp.zeros((rows, cols * seq), F32)
-    for step, part in enumerate(parts):
-        out = lax.dynamic_update_slice_in_dim(out, part.astype(F32), (col ^ step) * seq, axis=1)
-    return out
+        to, _ = col_peer(step)
+        transposes.append(
+            remote(vectors_ref, all_vectors_ref.at[col], col_send.at[0, step], col_recv.at[0, step], {"col": to})
+        )
+        transposes.append(
+            remote(
+                tokens_ref.at[:, pl.ds(pl.multiple_of(to * seq, 128), seq)], x_ref.at[my_feats],
+                col_send.at[1, step], col_recv.at[1, step], {"col": to},
+            )
+        )
+    for copy in transposes:
+        copy.start()
+    for copy in own:
+        copy.wait()
+    for step in range(len(dims)):
+        for piece in range(2):
+            stages[piece][step].wait()
+            if step + 1 < len(dims):
+                stages[piece][step + 1].start()
+    for copy in transposes:
+        copy.wait()
+
+
+def head(orders, qk, vo, tokens, vectors):
+    dims = all_bits()
+    cols = lax.axis_size("col")
+    twos = (2,) * len(dims)
+    vmem = pl.BlockSpec(memory_space=pltpu.VMEM)
+    return pl.pallas_call(
+        lambda *refs: head_kernel(orders, *refs),
+        in_specs=[vmem] * 4,
+        out_specs=[vmem] * 4,
+        out_shape=[
+            jax.ShapeDtypeStruct(twos + qk.shape, BF),
+            jax.ShapeDtypeStruct(twos + vo.shape, BF),
+            jax.ShapeDtypeStruct((cols * tokens.shape[0], SEQ_MAX), BF),
+            jax.ShapeDtypeStruct((cols,) + vectors.shape, F32),
+        ],
+        scratch_shapes=[
+            pltpu.SemaphoreType.DMA((4,)),
+            pltpu.SemaphoreType.DMA((2, len(dims))), pltpu.SemaphoreType.DMA((2, len(dims))),
+            pltpu.SemaphoreType.DMA((2, cols)), pltpu.SemaphoreType.DMA((2, cols)),
+        ],
+        compiler_params=pltpu.CompilerParams(collective_id=0, has_side_effects=True),
+        name="head",
+    )(qk, vo, tokens, vectors)
+
+
+def tail_kernel(orders, *refs):
+    dims = all_bits()
+    levels = len(dims)
+    count = len(orders)
+    cols, col = lax.axis_size("col"), lax.axis_index("col")
+    grads, (token_ref, small_ref) = refs[:count], refs[count : count + 2]
+    refs = refs[count + 2 :]
+    sums, (out_ref, own_ref) = refs[:count], refs[count : count + 2]
+    refs = refs[count + 2 :]
+    landed = [refs[i * levels : (i + 1) * levels] for i in range(count)]
+    refs = refs[count * levels :]
+    (
+        token_landed, small_landed, small_sum, block_send, block_recv, col_send, col_recv, small_send, small_recv,
+    ) = refs
+    feats, seq = token_landed.shape[1], token_landed.shape[2]
+    small_bits = axis_bits("row") + axis_bits("dp")
+    meet_partners()
+
+    def views(piece, step):
+        left = [bit for bit in dims if bit not in orders[piece][:step]]
+        axis = left.index(orders[piece][step])
+        return grads[piece] if step == 0 else landed[piece][step - 1], axis, my_bit(*orders[piece][step])
+
+    def stage(piece, step):
+        operand, axis, mine = views(piece, step)
+        return remote(
+            operand.at[(slice(None),) * axis + (1 - mine,)], landed[piece][step], block_send.at[piece, step],
+            block_recv.at[piece, step], partner(*orders[piece][step]),
+        )
+
+    def add(piece, step):
+        operand, axis, mine = views(piece, step)
+        arrived = landed[piece][step]
+        free = levels - 1 - step
+
+        def body(i, carry):
+            index = [(i // 2 ** (free - 1 - k)) % 2 for k in range(free)]
+            kept = operand[tuple(index[:axis] + [mine] + index[axis:])].astype(F32)
+            total = kept + arrived[tuple(index)].astype(F32)
+            if free:
+                arrived[tuple(index)] = total.astype(BF)
+            else:
+                sums[piece][...] = total
+            return carry
+
+        if free:
+            lax.fori_loop(0, 2**free, body, 0)
+        else:
+            body(0, 0)
+
+    stages = [[stage(piece, step) for step in range(levels)] for piece in range(count)]
+    for piece in range(count):
+        stages[piece][0].start()
+    small_copies = []
+    token_copies = []
+    for step in range(1, cols):
+        to, _ = col_peer(step)
+        small_copies.append(
+            remote(small_ref.at[to], small_landed.at[step], col_send.at[0, step], col_recv.at[0, step], {"col": to})
+        )
+        token_copies.append(
+            remote(
+                token_ref.at[pl.ds(pl.multiple_of(to * feats, 8), feats)], token_landed.at[step],
+                col_send.at[1, step], col_recv.at[1, step], {"col": to},
+            )
+        )
+    for copy in small_copies + token_copies:
+        copy.start()
+    out_ref[:, pl.ds(pl.multiple_of(col * seq, 128), seq)] = token_ref[
+        pl.ds(pl.multiple_of(col * feats, 8), feats)
+    ].astype(F32)
+    for copy in small_copies:
+        copy.wait()
+    total = small_ref[col]
+    for step in range(1, cols):
+        total = total + small_landed[step]
+    small_sum[0] = total
+    for step in range(max(levels, len(small_bits))):
+        if step < len(small_bits):
+            small_copy = remote(
+                small_sum.at[step], small_landed.at[cols + step], small_send.at[step], small_recv.at[step],
+                partner(*small_bits[step]),
+            )
+            small_copy.start()
+        for piece in range(count):
+            if step < levels:
+                stages[piece][step].wait()
+                add(piece, step)
+                if step + 1 < levels:
+                    stages[piece][step + 1].start()
+        if step < len(small_bits):
+            small_copy.wait()
+            small_sum[step + 1] = small_sum[step] + small_landed[cols + step]
+    own_ref[...] = small_sum[len(small_bits)]
+    for step in range(1, cols):
+        _, source = col_peer(step)
+        token_copies[step - 1].wait()
+        out_ref[:, pl.ds(pl.multiple_of(source * seq, 128), seq)] = token_landed[step].astype(F32)
+
+
+def tail(orders, grads, token_grad, small):
+    dims = all_bits()
+    levels = len(dims)
+    cols = lax.axis_size("col")
+    rows = grads[0].shape[0] * grads[0].shape[1] >> levels
+    feats = token_grad.shape[0] // cols
+    grads = [g.reshape((2,) * levels + (rows, g.shape[2])) for g in grads]
+    widths = [g.shape[-1] for g in grads]
+    small_bits = axis_bits("row") + axis_bits("dp")
+    vmem = pl.BlockSpec(memory_space=pltpu.VMEM)
+    dma = pltpu.SemaphoreType.DMA
+    return pl.pallas_call(
+        lambda *refs: tail_kernel(orders, *refs),
+        in_specs=[vmem] * (len(grads) + 2),
+        out_specs=[vmem] * (len(grads) + 2),
+        out_shape=[jax.ShapeDtypeStruct((rows, w), F32) for w in widths]
+        + [jax.ShapeDtypeStruct((feats, cols * SEQ_MAX), F32), jax.ShapeDtypeStruct(small.shape[1:], F32)],
+        scratch_shapes=[
+            pltpu.VMEM((2,) * (levels - 1 - step) + (rows, w), BF) for w in widths for step in range(levels)
+        ]
+        + [
+            pltpu.VMEM((cols, feats, SEQ_MAX), BF),
+            pltpu.VMEM((cols + len(small_bits),) + small.shape[1:], F32),
+            pltpu.VMEM((len(small_bits) + 1,) + small.shape[1:], F32),
+            dma((len(grads), levels)), dma((len(grads), levels)), dma((2, cols)), dma((2, cols)),
+            dma((len(small_bits),)), dma((len(small_bits),)),
+        ],
+        compiler_params=pltpu.CompilerParams(collective_id=1, has_side_effects=True),
+        name="tail",
+    )(*grads, token_grad, small)
 
 
 def local(
@@ -251,23 +454,18 @@
     def gather(shard):
         return lax.all_gather(shard, OWNERS, axis=0, tiled=True).reshape(cols, d, shard.shape[1])
 
-    w_flat = w_qkv.reshape(rows, 3 * width)
-    full_qk = gather_blocks(w_flat[:, : 2 * width], near_first)
-    full_vo = gather_blocks(jnp.concatenate([w_flat[:, 2 * width :], w_attn_out], axis=1), far_first)
     full_in = gather(w_in)
     full_out = gather(w_out)
+    vectors = jnp.concatenate(
+        [bias_qv, bias_attn_out[None], bias_out[None], norm_gains, norm_biases, bias_in.reshape(-1, width)], axis=0
+    )
+    w_flat = w_qkv.reshape(rows, 3 * width)
+    w_vo = jnp.concatenate([w_flat[:, 2 * width :], w_attn_out], axis=1)
+    full_qk, full_vo, x, vectors = head((near_first, far_first), w_flat[:, : 2 * width], w_vo, tokens, vectors)
+    full_qk = full_qk.reshape(cols, d, 2 * width)
+    full_vo = full_vo.reshape(cols, d, 2 * width)
     full_v = full_vo[:, :, :width]
     full_attn = full_vo[:, :, width:]
-
-    vectors = jnp.concatenate(
-        [bias_qv, bias_attn_out[None], bias_out[None], norm_gains, norm_biases, bias_in.reshape(-1, width)], axis=0
-    )
-    vectors = vectors.reshape((1,) * len(col_bits) + vectors.shape)
-    for dim, (name, bit) in enumerate(col_bits):
-        other = swap(vectors, name, bit)
-        high = my_bit(name, bit) == 1
-        vectors = jnp.concatenate([jnp.where(high, other, vectors), jnp.where(high, vectors, other)], axis=dim)
-    vectors = vectors.reshape(cols, -1, width)
     bias_q, bias_v = vectors[:, 0], vectors[:, 1]
     bias_attn_out, bias_out = vectors[:, 2].reshape(d), vectors[:, 3].reshape(d)
     gains = [vectors[:, 4].reshape(d), vectors[:, 5].reshape(d)]
@@ -277,7 +475,6 @@
     def to_window(a):
         return lax.all_to_all(a, "col", split_axis=1, concat_axis=0, tiled=True)
 
-    x = to_window(tokens)
     up = to_window(cotangent)
     length = lax.dynamic_index_in_dim(seq_lengths, col, keepdims=False)
     offset = lax.dynamic_index_in_dim(seq_offsets, col, keepdims=False)
@@ -308,7 +505,8 @@
         normed + jnp.einsum("cdf,cft->dt", full_out, active, preferred_element_type=F32) + bias_out[:, None]
     )
     result, xhat2, rstd2 = norm_forward(second_sum, gains[1], shifts[1])
-    activations = spread_windows((result * live).astype(BF))
+    activations = lax.all_to_all((result * live).astype(BF), "col", split_axis=0, concat_axis=1, tiled=True)
+    activations = activations.astype(F32)
 
     upstream = up.astype(F32) * live
     gain_two = jnp.sum(upstream * xhat2, axis=1)
@@ -317,12 +515,13 @@
     g_bias_out = jnp.sum(d_second, axis=1)
     d_second_low = d_second.astype(BF)
     g_out = jnp.einsum("dt,cft->cdf", d_second_low, active, preferred_element_type=F32)
-    g_out = scatter_blocks(g_out, dp_bits + row_bits + col_bits)
     d_hidden = jnp.einsum("cdf,dt->cft", full_out, d_second_low, preferred_element_type=F32) * slope
     g_bias_in = jnp.sum(d_hidden, axis=2)
     d_hidden_low = d_hidden.astype(BF)
     g_in = jnp.einsum("dt,cft->cdf", normed_low, d_hidden_low, preferred_element_type=F32)
-    g_in = scatter_blocks(g_in, dp_bits + row_bits[::-1] + col_bits)
+    g_both = jnp.stack([g_in.astype(BF).reshape(-1, rows, hid), g_out.astype(BF).reshape(-1, rows, hid)], axis=1)
+    g_both = lax.psum_scatter(g_both, OWNERS, scatter_dimension=0, tiled=True).astype(F32)
+    g_in, g_out = g_both[0, 0], g_both[0, 1]
     d_normed = d_second + jnp.einsum("cdf,cft->dt", full_in, d_hidden_low, preferred_element_type=F32)
     gain_one = jnp.sum(d_normed * xhat1, axis=1)
     shift_one = jnp.sum(d_normed, axis=1)
@@ -332,33 +531,25 @@
     d_attended = jnp.einsum("cde,dt->cet", full_attn, d_first_low, preferred_element_type=F32).astype(BF)
     d_attended = d_attended.reshape(heads, HEAD_DIM, SEQ_MAX)
     g_attn = jnp.einsum("dt,cet->cde", d_first_low, attended_cols, preferred_element_type=F32)
-    g_attn = scatter_blocks(g_attn, dp_bits + row_bits + col_bits)
     d_qk, d_v, bias_sums = attend_backward(qk, values, key_mask, attended, total, d_attended)
     d_qk = d_qk.reshape(cols, 2 * width, SEQ_MAX)
     d_v = d_v.reshape(cols, width, SEQ_MAX)
     bias_sums = jnp.sum(bias_sums, axis=3)
     g_bias_q, g_bias_v = bias_sums[:, 0].reshape(d), bias_sums[:, 1].reshape(d)
     g_qk = jnp.einsum("dt,cnt->cdn", x, d_qk, preferred_element_type=F32)
-    g_qk = scatter_blocks(g_qk, dp_bits + row_bits[::-1] + col_bits)
     g_v = jnp.einsum("dt,cnt->cdn", x, d_v, preferred_element_type=F32)
-    g_v = scatter_blocks(g_v, dp_bits + row_bits + col_bits)
     token_grad = (
         d_first + jnp.einsum("cdn,cnt->dt", full_qk, d_qk, preferred_element_type=F32)
         + jnp.einsum("cdn,cnt->dt", full_v, d_v, preferred_element_type=F32)
     )
-    token_grad = spread_windows(token_grad.astype(BF))
-
     small = jnp.stack([g_bias_q, g_bias_v, g_bias_attn, g_bias_out, gain_one, gain_two, shift_one, shift_two])
     small = small.reshape(8, cols, width).transpose(1, 0, 2)
     small = jnp.concatenate([small, g_bias_in.reshape(cols, -1, width)], axis=1)
-    small = small.reshape((2,) * len(col_bits) + small.shape[1:])
-    for dim, (name, bit) in enumerate(col_bits):
-        mine = my_bit(name, bit)
-        other = swap(lax.dynamic_index_in_dim(small, 1 - mine, dim), name, bit)
-        small = lax.dynamic_index_in_dim(small, mine, dim) + other
-    own = small.reshape(small.shape[-2:])
-    for name, bit in row_bits + dp_bits:
-        own = own + swap(own, name, bit)
+    near = dp_bits + row_bits[::-1] + col_bits
+    far = dp_bits + row_bits + col_bits
+    g_qk, g_v, g_attn, token_grad, own = tail(
+        (near, far, far), [g.astype(BF) for g in (g_qk, g_v, g_attn)], token_grad.astype(BF), small
+    )
     return (
         activations, token_grad, jnp.concatenate([g_qk, g_v], axis=1).reshape(rows, 3, width), own[0:2],
         g_attn, own[2], g_in, own[8:].reshape(hid), g_out, own[3], own[4:6], own[6:8],

time: 563 us -> 490 us (0.87)
  Pallas kernels: 82.3 us -> 295 us
  waiting for transfers between devices: 170 us -> 1.42 us
  starting transfers between devices: 79.7 us -> 10 us
  local copies, waits for them, and re-layouts: 59 us -> 29.7 us
  other arithmetic: 46.7 us -> 25.7 us
  matrix products: 98.2 us -> 109 us
    pallas_call x0 -> x2, Pallas kernels: none -> 213 us  [the longest x1 131 us: head(): pl.pallas_call(lambda *refs: head_kernel(orders, *refs), in_specs=[vmem]...]
    ppermute x48 -> x0, waiting for transfers between devices: 169 us -> none  [the longest x42 121 us: swap(): lax.ppermute(a, name, [(i, i ^ bit) for i in range(lax.axis_size(name))])]
    ppermute x48 -> x0, starting transfers between devices: 71.4 us -> none  [the longest x42 64.5 us: swap(): lax.ppermute(a, name, [(i, i ^ bit) for i in range(lax.axis_size(name))])]
    dot_general x1, matrix products: 6.49 us -> 21.7 us  [local(): jnp.einsum('cdf,cft->dt', full_in, d_hidden_low, preferred_element_type=F32)]
    dynamic_update_slice x8 -> x0, other arithmetic: 11.7 us -> none  [spread_windows(): lax.dynamic_update_slice_in_dim(out, part.astype(F32), (col ^ step) * seq...]
    convert_element_type x25 -> x1, other arithmetic: 12.6 us -> 1.19 us  [local(): lax.psum_scatter(g_both, OWNERS, scatter_dimension=0, tiled=True)]
    dynamic_slice x28 -> x0, local copies, waits for them, and re-layouts: 10.8 us -> none  [the longest x25 8.06 us: scatter_blocks(): other = swap(lax.dynamic_index_in_dim(a, 1 - mine, dim), name, bit)]
    concatenate x8 -> x1, local copies, waits for them, and re-layouts: 10.5 us -> 0.15 us  [local(): jnp.concatenate([g_qk, g_v], axis=1).reshape(rows, 3, width)]
  transfers between devices with their start and end apart: 52 -> 5, of which waited for: 24 -> 0; matrix products, arithmetic and copies ran while one was open for 24% -> 23% of each run, Pallas kernels for 8% -> 61%
where the time goes in v4:
time: 490 us; the launch traced here: 486 us
  Pallas kernels  295 us (60%)
  matrix products  109 us (22%)
  local copies, waits for them, and re-layouts  29.7 us (6%)
  other arithmetic  25.7 us (5%)
  between operations  15.7 us (3%)
  starting transfers between devices  10 us (2%)
    pallas_call x1, Pallas kernels, head(): pl.pallas_call(lambda *refs: head_kernel(orders, *refs), in_specs=[vmem]...  131 us
    pallas_call x1, Pallas kernels, tail(): pl.pallas_call(lambda *refs: tail_kernel(orders, *refs), in_specs=[vmem]...  81.4 us
    pallas_call x1, Pallas kernels, attend_forward(): pl.pallas_call(attend_forward_kernel, grid=(heads,), in_specs=qkv_specs(p...  41.6 us
    pallas_call x1, Pallas kernels, attend_backward(): pl.pallas_call(attend_backward_kernel, grid=(heads,), in_specs=qkv_specs(...  40.7 us
    dot_general x1, matrix products, local(): jnp.einsum('cdf,cft->dt', full_in, d_hidden_low, preferred_element_type=F32)  21.7 us
    dot_general x1, matrix products, local(): jnp.einsum('cdf,dt->cft', full_in, normed_low, preferred_element_type=F32)  13.5 us
    dot_general x1, matrix products, local(): jnp.einsum('cdf,dt->cft', full_out, d_second_low, preferred_element_type=...  10.3 us
  transfers between devices with their start and end apart: 5, of which 0 were waited for; matrix products, arithmetic and copies ran while one was open for 23% of the time, Pallas kernels for 61%

profile of v4, /device:TPU:0, one launch (start us, length us, event | category | flops | bytes accessed | tf_op | source)
XLA Modules:
  0.0 486.0 jit_solution(6477660376648213436)
XLA Ops:
  7.2 0.7 all-gather.3.cloned.1.call-update
  8.0 0.7 all-gather.5.cloned.1.call-update
  8.8 2.9 copy.113
  11.7 6.3 %all-to-all-start.1 = ((bf16[192,4,1024]{2,0,1:T(8,128)(2,1)}), bf16[192,4,1024]{2,0,1:T(8,128)(2,1)S(1)}, u32[]{:S(2)}, u32[]{:S(2)}) async-start(bf16[192,4,1024]{2,0,1:T(8,128)(2,1)} %bitcast.167), calls=%async_computation.1 | async-start | bytes 3145728 | tf_op jit(solution)/shard_map/all_to_all | solution.py:476
  18.0 0.2 copy.67
  18.2 0.6 dynamic_slice.7
  18.8 0.6 dynamic_slice.8
  19.5 0.7 copy.103.refs_0_
  20.2 0.1 copy.104
  20.4 1.2 concatenate.17.refs_3_
  21.6 0.7 pad_maximum_fusion.2.refs_1_
  22.3 131.3 %head.1 = (bf16[2,2,2,2,2,96,384]{6,5,4,3,2,1,0:T(8,128)(2,1)}, bf16[2,2,2,2,2,96,384]{6,5,4,3,2,1,0:T(8,128)(2,1)}, bf16[768,1024]{1,0:T(8,128)(2,1)}, f32[4,12,192]{2,1,0:T(8,128)}) custom-call(bf16[96,384]{1,0:T(8,128)(2,1)} %copy.103.refs_0_, bf16[96,384]{1,0:T(8,128)(2,1)} %pad_maximum_fusion.2.refs_1_, bf16[192,4096]{1,0:T(8,128)(2,1)} %refs_2_.1, ...), custom_call_target="tpu_custom_call" | custom-call | tf_op jit(solution)/shard_map/head/pallas_call | solution.py:286
  153.6 0.8 slice.78
  154.4 0.1 add.138
  154.5 1.2 slice_reduce_fusion.7
  157.5 0.7 fusion.57
  158.2 1.2 and_select_fusion.mask_ref
  159.4 4.6 add_convert_fusion.1
  164.0 4.0 add_convert_fusion
  168.0 41.6 %attend_forward.1 = (bf16[12,64,1024]{2,1,0:T(8,128)(2,1)}, f32[12,1,1024]{2,1,0:T(1,128)}) custom-call(bf16[4,2,3,64,1024]{4,3,2,1,0:T(8,128)(2,1)} %bitcast.198, bf16[4,2,3,64,1024]{4,3,2,1,0:T(8,128)(2,1)} %bitcast.199, bf16[4,1,3,64,1024]{4,3,2,1,0:T(8,128)(2,1)} %bitcast.204, f32[1,1024]{1,0:T(1,128)} %and_select_fusion.mask_ref), custom_call_target="tpu_custom_call" | custom-call | flops 12884901888 | bytes 6291456 | tf_op jit(solution)/shard_map/attend_forward/pallas_call | solution.py:140
  209.6 4.6 fusion.65
  214.2 0.4 multiply_reduce_fusion.5
  214.6 1.3 copy-done
  215.8 0.7 bitcast_reduce_fusion
  216.6 13.5 %fusion.8 = (bf16[4,768,1024]{1,2,0:T(8,128)(2,1)}, f32[1024,4,768]{2,0,1:T(8,128)}) fusion(f32[4,768]{1,0:T(4,128)S(1)} %add.138, bf16[4,768,768]{2,1,0:T(8,128)(2,1)} %bitcast.186, f32[768,1024]{1,0:T(8,128)} %copy-done, f32[768]{0:T(1024)S(1)} %add.135, f32[768]{0:T(1024)S(1)} %mul.163, f32[1024]{0:T(1024)S(1)} %add_rsqrt_fusion.1, ...), kind=kOutput, calls=%fused_computation.11 | convolution fusion | flops 4854644736 | bytes 26765312 | tf_op jit(solution)/shard_map/cdf,dt->cft/dot_general | solution.py:500
  230.0 9.5 %fusion.66 = (f32[1024]{0:T(1024)S(1)}, f32[768,1024]{1,0:T(8,128)S(1)}) fusion(f32[768]{0:T(1024)S(1)} %add.145, bf16[4,768,1024]{1,2,0:T(8,128)(2,1)} %get-tuple-element.109, bf16[4,768,768]{2,1,0:T(8,128)(2,1)} %bitcast.188, f32[768]{0:T(1024)S(1)} %add.135, f32[768]{0:T(1024)S(1)} %mul.163, f32[1024]{0:T(1024)S(1)} %add_rsqrt_fusion.1, ...), kind=kOutput, calls=%fused_computation.112 | convolution fusion | flops 4837342208 | bytes 17323008 | tf_op jit(solution)/shard_map/cdf,cft->dt/dot_general | solution.py:505
  239.6 0.4 multiply_reduce_fusion.4
  240.0 1.2 multiply_reduce_fusion
  241.2 2.8 fusion.61
  244.1 6.8 %convolution_convert_fusion = bf16[4,768,768]{1,2,0:T(8,128)(2,1)} fusion(bf16[4,768,1024]{1,2,0:T(8,128)(2,1)S(1)} %copy-done.21, f32[768,1024]{1,0:T(8,128)S(1)} %get-tuple-element.93), kind=kOutput, calls=%fused_computation.46 | convolution fusion | flops 4834983936 | bytes 14155776 | tf_op jit(solution)/shard_map/dt,cft->cdf/dot_general | solution.py:517
  250.9 10.3 %fusion.67 = (f32[4,768]{1,0:T(4,128)S(1)}, bf16[4,768,1024]{1,2,0:T(8,128)(2,1)S(1)}) fusion(f32[1024,4,768]{2,0,1:T(8,128)S(1)} %bitcast.212, f32[4,768]{1,0:T(4,128)S(1)} %add.138, bf16[4,768,768]{2,1,0:T(8,128)(2,1)S(1)} %bitcast.191, f32[768,1024]{1,0:T(8,128)S(1)} %get-tuple-element.93), kind=kOutput, calls=%fused_computation.113 | convolution fusion | flops 4870370304 | bytes 26763264 | tf_op jit(solution)/shard_map/cdf,dt->cft/dot_general | solution.py:518
  261.2 7.1 %fusion.18 = bf16[4,768,768]{1,2,0:T(8,128)(2,1)} fusion(bf16[4,768,1024]{1,2,0:T(8,128)(2,1)S(1)} %get-tuple-element.115, f32[768,1024]{1,0:T(8,128)S(1)} %copy-done.1, f32[768]{0:T(1024)S(1)} %add.135, f32[768]{0:T(1024)S(1)} %mul.163, f32[1024]{0:T(1024)S(1)} %add_rsqrt_fusion.1, f32[1024]{0:T(1024)S(1)} %broadcast_multiply_fusion.5), kind=kOutput, calls=%fused_computation.47 | convolution fusion | flops 4838129664 | bytes 14170112 | tf_op jit(solution)/shard_map/dt,cft->cdf/dot_general | solution.py:521
  268.2 8.3 %pad_maximum_fusion = bf16[32,2,96,768]{3,2,1,0:T(8,128)(2,1)} fusion(bf16[32,1,96,768]{3,2,1,0:T(8,128)(2,1)} %bitcast.173, bf16[32,1,96,768]{3,2,1,0:T(8,128)(2,1)} %bitcast.174), kind=kLoop, calls=%fused_computation.12 | loop fusion | flops 4718592 | bytes 18874368 | tf_op jit(solution)/shard_map/stack | solution.py:522
  276.6 21.7 %multiply_reduce_fusion.1 = (f32[768]{0:T(1024)S(1)}, f32[1024]{0:T(1024)S(1)}, f32[1024]{0:T(1024)S(1)}, f32[768]{0:T(1024)S(1)}, f32[768,1024]{1,0:T(8,128)}) fusion(f32[768,1024]{1,0:T(8,128)S(1)} %copy-done.1, f32[1024]{0:T(1024)S(1)} %add_rsqrt_fusion.1, f32[1024]{0:T(1024)S(1)} %broadcast_multiply_fusion.5, f32[768]{0:T(1024)S(1)} %mul.163, ...), kind=kOutput, calls=%fused_computation.28 | convolution fusion | flops 4839698432 | bytes 20472832 | tf_op jit(solution)/shard_map/cdf,cft->dt/dot_general | solution.py:525
  298.5 4.7 fusion.62
  303.4 0.1 reshape.213
  303.5 3.6 all-to-all-start
  307.0 4.0 fusion.41
  311.1 1.6 copy.81
  312.6 5.5 %convolution_convert_fusion.1 = bf16[4,192,1024]{2,1,0:T(8,128)(2,1)} fusion(bf16[4,768,384]{2,1,0:T(8,128)(2,1)} %bitcast.196, f32[768,1024]{1,0:T(8,128)} %get-tuple-element.95), kind=kOutput, calls=%fused_computation.51 | convolution fusion | flops 1209532416 | bytes 6291456 | tf_op jit(solution)/shard_map/cde,dt->cet/dot_general | solution.py:531
  318.1 40.7 %attend_backward.1 = (bf16[4,2,3,64,1024]{4,3,2,1,0:T(8,128)(2,1)}, bf16[4,1,3,64,1024]{4,3,2,1,0:T(8,128)(2,1)}, f32[12,2,64,128]{3,2,1,0:T(8,128)}) custom-call(bf16[4,2,3,64,1024]{4,3,2,1,0:T(8,128)(2,1)} %bitcast.200, bf16[4,2,3,64,1024]{4,3,2,1,0:T(8,128)(2,1)} %bitcast.201, bf16[4,1,3,64,1024]{4,3,2,1,0:T(8,128)(2,1)} %bitcast.205, ...), custom_call_target="tpu_custom_call" | custom-call | flops 32212254720 | bytes 12582912 | tf_op jit(solution)/shard_map/attend_backward/pallas_call | solution.py:160
  358.8 1.4 reduce_sum.152
  360.4 6.5 %convert_bitcast_fusion.1 = bf16[4,768,384]{1,2,0:T(8,128)(2,1)} fusion(bf16[4,384,1024]{2,1,0:T(8,128)(2,1)} %bitcast.202, bf16[768,1024]{1,0:T(8,128)(2,1)} %get-tuple-element.26), kind=kOutput, calls=%fused_computation.50 | convolution fusion | flops 2417098752 | bytes 7077888 | tf_op jit(solution)/shard_map/dt,cnt->cdn/dot_general | solution.py:539
  366.9 4.3 copy.79
  371.2 3.5 fusion.44
  374.7 1.5 copy.80
  376.3 0.6 pad_maximum_fusion.3.refs_4_
  376.9 3.5 fusion.48
  380.5 1.0 copy-done.19
  381.4 3.7 fusion.10.refs_3_
  385.1 81.4 %tail.1 = (f32[96,384]{1,0:T(8,128)}, f32[96,192]{1,0:T(8,128)}, f32[96,192]{1,0:T(8,128)}, f32[192,4096]{1,0:T(8,128)}, f32[12,192]{1,0:T(8,128)}) custom-call(bf16[2,2,2,2,2,96,384]{6,5,4,3,2,1,0:T(8,128)(2,1)} %bitcast.169, bf16[2,2,2,2,2,96,192]{6,5,4,3,2,1,0:T(8,128)(2,1)} %bitcast.172, bf16[2,2,2,2,2,96,192]{6,5,4,3,2,1,0:T(8,128)(2,1)} %bitcast.171, ...), custom_call_target="tpu_custom_call" | custom-call | tf_op jit(solution)/shard_map/tail/pallas_call | solution.py:417
  466.5 0.7 slice.87
  467.2 0.7 reshape.215
  467.9 1.0 pad_maximum_fusion.1
  468.9 0.1 copy.84
  469.0 0.9 copy.89
  469.9 1.3 fusion.64
  471.3 1.4 fusion.63
  472.7 0.4 convert_bitcast_fusion
  473.1 1.9 copy.108
  474.9 1.2 convert_element_type.126
  476.1 0.8 slice_bitcast_fusion
  477.0 1.7 copy.117
  478.7 0.6 copy.118
  (93 shorter events, 1.6 us)
Async XLA Ops:
  7.2 209.4 %all-gather.3.cloned.1.call-start = ((), (), s32[]{:S(2)}) async-start(), calls=%async_computation.3 | async-start | bytes 4866048 | tf_op jit(solution)/shard_map/all_gather | solution.py:455
  7.9 222.1 %all-gather.5.cloned.1.call-start = ((), (), s32[]{:S(2)}) async-start(), calls=%async_computation.4 | async-start | bytes 4866048 | tf_op jit(solution)/shard_map/all_gather | solution.py:455
  8.7 9.3 %copy-start.5 = (bf16[96,3,192]{2,0,1:T(8,128)(2,1)S(1)}, bf16[96,3,192]{2,0,1:T(8,128)(2,1)}, u32[]{:S(2)}) copy-start(bf16[96,3,192]{2,0,1:T(8,128)(2,1)} %param.15) | copy-start | bytes 331780
  8.7 9.5 %copy-start.17 = (s32[4]{0:T(128)S(1)}, s32[4]{0:T(128)}, u32[]{:S(2)}) copy-start(s32[4]{0:T(128)} %param.26) | copy-start | bytes 52
  8.7 10.1 %copy-start.18 = (s32[4]{0:T(128)S(1)}, s32[4]{0:T(128)}, u32[]{:S(2)}) copy-start(s32[4]{0:T(128)} %param.25) | copy-start | bytes 52
  8.7 10.7 %copy-start.8 = (f32[768]{0:T(1024)S(1)}, f32[768]{0:T(1024)}, u32[]{:S(2)}) copy-start(f32[768]{0:T(1024)} %param.20) | copy-start | bytes 9220
  8.7 11.6 %copy-start.9 = (f32[2,192]{1,0:T(2,128)S(1)}, f32[2,192]{1,0:T(2,128)}, u32[]{:S(2)}) copy-start(f32[2,192]{1,0:T(2,128)} %param.16) | copy-start | bytes 4612
  8.7 11.6 %copy-start.10 = (f32[2,192]{1,0:T(2,128)S(1)}, f32[2,192]{1,0:T(2,128)}, u32[]{:S(2)}) copy-start(f32[2,192]{1,0:T(2,128)} %param.23) | copy-start | bytes 4612
  8.7 11.6 %copy-start.11 = (f32[2,192]{1,0:T(2,128)S(1)}, f32[2,192]{1,0:T(2,128)}, u32[]{:S(2)}) copy-start(f32[2,192]{1,0:T(2,128)} %param.24) | copy-start | bytes 4612
  8.7 11.6 %copy-start.12 = (f32[192]{0:T(256)S(1)}, f32[192]{0:T(256)}, u32[]{:S(2)}) copy-start(f32[192]{0:T(256)} %param.18) | copy-start | bytes 2308
  8.7 11.6 %copy-start.13 = (f32[192]{0:T(256)S(1)}, f32[192]{0:T(256)}, u32[]{:S(2)}) copy-start(f32[192]{0:T(256)} %param.22) | copy-start | bytes 2308
  8.8 12.8 %copy-start.7 = (bf16[96,192]{1,0:T(8,128)(2,1)S(1)}, bf16[96,192]{1,0:T(8,128)(2,1)}, u32[]{:S(2)}) copy-start(bf16[96,192]{1,0:T(8,128)(2,1)} %param.17) | copy-start | bytes 110596
  11.7 204.2 %all-to-all-start.1 = ((bf16[192,4,1024]{2,0,1:T(8,128)(2,1)}), bf16[192,4,1024]{2,0,1:T(8,128)(2,1)S(1)}, u32[]{:S(2)}, u32[]{:S(2)}) async-start(bf16[192,4,1024]{2,0,1:T(8,128)(2,1)} %bitcast.167), calls=%async_computation.1 | async-start | bytes 3145728 | tf_op jit(solution)/shard_map/all_to_all | solution.py:476
  18.0 456.9 %reduce-scatter.2.cloned.1.call-start = ((), (), s32[]{:S(2)}) async-start(), calls=%async_computation.5 | async-start | bytes 9732096 | tf_op jit(solution)/shard_map/reduce_scatter | solution.py:523
  159.4 4.6 copy-start.14
  159.4 4.6 copy-start.16
  214.2 1.7 copy-start
  240.0 4.1 copy-start.21
  241.2 9.7 %slice-start = ((s8[4718592]{0:T(1024)(128)(4,1)}), s8[4194304]{0:T(1024)(128)(4,1)S(1)}, s32[]{:S(2)}) async-start(s8[4718592]{0:T(1024)(128)(4,1)} %bitcast.189), calls=%async_computation.6 | async-start | bytes 8388608
  241.2 9.7 %slice-start.2 = ((s8[12582912]{0:T(1024)(128)(4,1)}), s8[4194304]{0:T(1024)(128)(4,1)S(1)}, s32[]{:S(2)}) async-start(s8[12582912]{0:T(1024)(128)(4,1)} %bitcast.211), calls=%async_computation.8 | async-start | bytes 8388608
  244.0 6.8 %copy-start.4 = (f32[768,1024]{1,0:T(8,128)}, f32[768,1024]{1,0:T(8,128)S(1)}, u32[]{:S(2)}) copy-start(f32[768,1024]{1,0:T(8,128)S(1)} %get-tuple-element.93) | copy-start | bytes 9437188
  244.0 6.8 %slice-start.1 = ((s8[4718592]{0:T(1024)(128)(4,1)}), s8[524288]{0:T(1024)(128)(4,1)S(1)}, s32[]{:S(2)}) async-start(s8[4718592]{0:T(1024)(128)(4,1)} %bitcast.189), calls=%async_computation.7 | async-start | bytes 1048576
  244.0 6.8 %slice-start.3 = ((s8[12582912]{0:T(1024)(128)(4,1)}), s8[4194304]{0:T(1024)(128)(4,1)S(1)}, s32[]{:S(2)}) async-start(s8[12582912]{0:T(1024)(128)(4,1)} %bitcast.211), calls=%async_computation.9 | async-start | bytes 8388608
  244.0 6.8 %slice-start.4 = ((s8[12582912]{0:T(1024)(128)(4,1)}), s8[4194304]{0:T(1024)(128)(4,1)S(1)}, s32[]{:S(2)}) async-start(s8[12582912]{0:T(1024)(128)(4,1)} %bitcast.211), calls=%async_computation.10 | async-start | bytes 8388608
  250.9 10.3 %copy-start.1 = (f32[768,1024]{1,0:T(8,128)S(1)}, f32[768,1024]{1,0:T(8,128)}, u32[]{:S(2)}) copy-start(f32[768,1024]{1,0:T(8,128)} %copy-done) | copy-start | bytes 9437188
  261.2 7.1 %copy-start.20 = (bf16[4,768,1024]{1,2,0:T(8,128)(2,1)}, bf16[4,768,1024]{1,2,0:T(8,128)(2,1)S(1)}, u32[]{:S(2)}) copy-start(bf16[4,768,1024]{1,2,0:T(8,128)(2,1)S(1)} %get-tuple-element.115) | copy-start | bytes 18874372
  303.5 169.2 %all-to-all-start = ((bf16[4,192,1024]{2,1,0:T(8,128)(2,1)}), bf16[4,192,1024]{2,1,0:T(8,128)(2,1)S(1)}, u32[]{:S(2)}, u32[]{:S(2)}) async-start(bf16[4,192,1024]{2,1,0:T(8,128)(2,1)} %bitcast.170), calls=%async_computation | async-start | bytes 3145728 | tf_op jit(solution)/shard_map/all_to_all | solution.py:508
  376.9 3.5 copy-start.3
  376.9 3.6 copy-start.15
  376.9 4.5 copy-start.19
  473.1 3.9 copy-start.2
  477.0 1.7 copy-start.6
Sparse Core Ops, SparseCore 0:
  10.9 110.0 all-gather.2
  123.8 69.0 all-gather.4
  276.7 187.6 reduce-scatter.1

commit v5 on v4

--- a/solution.py
+++ b/solution.py
@@ -59,23 +59,6 @@
     high = row.astype(BF).astype(F32)
     middle = (row - high).astype(BF).astype(F32)
     return high, middle, row - high - middle
-
-
-def attend_forward_kernel(q_ref, k_ref, v_ref, mask_ref, out_ref, total_ref):
-    seq = q_ref.shape[-1]
-    one = jnp.ones((1, seq), F32)
-    keys = jnp.concatenate([k_ref[0, 0, 0], stack_rows([mask_ref[...]], seq)], axis=0).T
-    queries = jnp.concatenate([q_ref[0, 0, 0], stack_rows([one], seq)], axis=0)
-    values = v_ref[0, 0, 0]
-    for j in range(seq // QBLOCK):
-        cols = slice(j * QBLOCK, (j + 1) * QBLOCK)
-        scores = dot_nn(keys, queries[:, cols])
-        largest = jnp.max(scores, axis=0, keepdims=True)
-        exponent = jnp.exp2((scores - largest) * (SCALE * LOG2E))
-        total = jnp.sum(exponent, axis=0, keepdims=True)
-        weights = (exponent * (1.0 / total)).astype(BF)
-        out_ref[0, :, cols] = dot_nn(values, weights).astype(BF)
-        total_ref[0, :, cols] = largest + jnp.log(total) * (1.0 / SCALE)
 
 
 def attend_backward_kernel(
@@ -134,26 +117,6 @@
     ]
 
 
-def attend_forward(qk, v, mask):
-    cols, _, per_col, _, seq = qk.shape
-    heads = cols * per_col
-    return pl.pallas_call(
-        attend_forward_kernel,
-        grid=(heads,),
-        in_specs=qkv_specs(per_col, seq),
-        out_specs=[head_spec(HEAD_DIM, seq), head_spec(1, seq)],
-        out_shape=[
-            jax.ShapeDtypeStruct((heads, HEAD_DIM, seq), BF),
-            jax.ShapeDtypeStruct((heads, 1, seq), F32),
-        ],
-        cost_estimate=pl.CostEstimate(
-            flops=heads * seq * seq * HEAD_DIM * 16, bytes_accessed=heads * seq * HEAD_DIM * 8,
-            transcendentals=heads * seq * seq,
-        ),
-        name="attend_forward",
-    )(qk, qk, v, mask)
-
-
 def attend_backward(qk, v, mask, attended, total, d_attended):
     cols, _, per_col, _, seq = qk.shape
     heads = cols * per_col
@@ -220,6 +183,75 @@
     pl.semaphore_wait(barrier, len(devices))
 
 
+def attend_forward_kernel(
+    pieces, events, q_ref, k_ref, v_ref, mask_ref, *refs
+):
+    count = 1 + max(which for which, _, _ in pieces)
+    shards, (out_ref, total_ref), fulls = refs[:count], refs[count : count + 2], refs[count + 2 : 2 * count + 2]
+    own_sem, block_send, block_recv = refs[2 * count + 2 :]
+    dims = all_bits()
+    levels = len(dims)
+    head = pl.program_id(0)
+    place = [my_bit(name, bit) for name, bit in dims]
+
+    def stage(piece, step):
+        which, cols, order = pieces[piece]
+        index = tuple(slice(None) if bit in order[:step] else at for bit, at in zip(dims, place))
+        target = fulls[which].at[index + (slice(None), cols)]
+        return remote(
+            shards[which].at[:, cols] if step == 0 else target, target, block_send.at[piece, step],
+            block_recv.at[piece, step], partner(*order[step]),
+        )
+
+    def own(which):
+        return pltpu.make_async_copy(shards[which], fulls[which].at[tuple(place)], own_sem.at[which])
+
+    def advance(piece, step):
+        stage(piece, step).wait()
+        if step + 1 < levels:
+            stage(piece, step + 1).start()
+
+    @pl.when(head == 0)
+    def _():
+        for which in range(count):
+            own(which).start()
+        meet_partners()
+        for piece in range(len(pieces)):
+            stage(piece, 0).start()
+        for which in range(count):
+            own(which).wait()
+
+    for at, moves in events:
+        if at >= 0:
+
+            @pl.when(head == at)
+            def _(moves=moves):
+                for piece, step in moves:
+                    advance(piece, step)
+
+    seq = q_ref.shape[-1]
+    one = jnp.ones((1, seq), F32)
+    keys = jnp.concatenate([k_ref[0, 0, 0], stack_rows([mask_ref[...]], seq)], axis=0).T
+    queries = jnp.concatenate([q_ref[0, 0, 0], stack_rows([one], seq)], axis=0)
+    values = v_ref[0, 0, 0]
+    for j in range(seq // QBLOCK):
+        cols = slice(j * QBLOCK, (j + 1) * QBLOCK)
+        scores = dot_nn(keys, queries[:, cols])
+        largest = jnp.max(scores, axis=0, keepdims=True)
+        exponent = jnp.exp2((scores - largest) * (SCALE * LOG2E))
+        total = jnp.sum(exponent, axis=0, keepdims=True)
+        weights = (exponent * (1.0 / total)).astype(BF)
+        out_ref[0, :, cols] = dot_nn(values, weights).astype(BF)
+        total_ref[0, :, cols] = largest + jnp.log(total) * (1.0 / SCALE)
+
+    @pl.when(head == pl.num_programs(0) - 1)
+    def _():
+        for at, moves in events:
+            if at < 0:
+                for piece, step in moves:
+                    advance(piece, step)
+
+
 def head_kernel(
     orders, qk_ref, vo_ref, tokens_ref, vectors_ref, full_qk_ref, full_vo_ref, x_ref, all_vectors_ref,
     own_sem, block_send, block_recv, col_send, col_recv,
@@ -301,6 +333,44 @@
         compiler_params=pltpu.CompilerParams(collective_id=0, has_side_effects=True),
         name="head",
     )(qk, vo, tokens, vectors)
+
+
+def attend_forward(qk, v, mask, shards, orders):
+    cols, _, per_col, _, seq = qk.shape
+    heads = cols * per_col
+    dims = all_bits()
+    levels = len(dims)
+    half = shards[0].shape[1] // len(orders)
+    pieces = [
+        (which, pl.ds(k * half, half), orders[k]) for which in range(len(shards)) for k in range(len(orders))
+    ]
+    first, second = [0, 1], [2, 3]
+    events = [(1, [(p, 0) for p in first]), (5, [(p, 1) for p in first] + [(p, 0) for p in second])]
+    events += [(7, [(p, 2) for p in first]), (9, [(p, 1) for p in second])]
+    for step in range(3, levels + 1):
+        events.append((-1, [(p, step) for p in first if step < levels] + [(p, step - 1) for p in second]))
+    twos = (2,) * levels
+    return pl.pallas_call(
+        lambda *refs: attend_forward_kernel(pieces, events, *refs),
+        grid=(heads,),
+        in_specs=qkv_specs(per_col, seq) + [pl.BlockSpec(a.shape, lambda h: (0, 0)) for a in shards],
+        out_specs=[head_spec(HEAD_DIM, seq), head_spec(1, seq)] + [pl.BlockSpec(memory_space=pl.ANY)] * len(shards),
+        out_shape=[
+            jax.ShapeDtypeStruct((heads, HEAD_DIM, seq), BF),
+            jax.ShapeDtypeStruct((heads, 1, seq), F32),
+        ]
+        + [jax.ShapeDtypeStruct(twos + a.shape, BF) for a in shards],
+        scratch_shapes=[
+            pltpu.SemaphoreType.DMA((len(shards),)),
+            pltpu.SemaphoreType.DMA((len(pieces), levels)), pltpu.SemaphoreType.DMA((len(pieces), levels)),
+        ],
+        compiler_params=pltpu.CompilerParams(collective_id=2, has_side_effects=True),
+        cost_estimate=pl.CostEstimate(
+            flops=heads * seq * seq * HEAD_DIM * 16, bytes_accessed=heads * seq * HEAD_DIM * 8,
+            transcendentals=heads * seq * seq,
+        ),
+        name="attend_forward",
+    )(qk, qk, v, mask, *shards)
 
 
 def tail_kernel(orders, *refs):
@@ -451,11 +521,6 @@
     near_first = col_bits[::-1] + row_bits[::-1] + dp_bits
     far_first = col_bits[::-1] + row_bits + dp_bits
 
-    def gather(shard):
-        return lax.all_gather(shard, OWNERS, axis=0, tiled=True).reshape(cols, d, shard.shape[1])
-
-    full_in = gather(w_in)
-    full_out = gather(w_out)
     vectors = jnp.concatenate(
         [bias_qv, bias_attn_out[None], bias_out[None], norm_gains, norm_biases, bias_in.reshape(-1, width)], axis=0
     )
@@ -475,7 +540,6 @@
     def to_window(a):
         return lax.all_to_all(a, "col", split_axis=1, concat_axis=0, tiled=True)
 
-    up = to_window(cotangent)
     length = lax.dynamic_index_in_dim(seq_lengths, col, keepdims=False)
     offset = lax.dynamic_index_in_dim(seq_offsets, col, keepdims=False)
     places = lax.broadcasted_iota(jnp.int32, (1, SEQ_MAX), 1)
@@ -489,7 +553,13 @@
 
     qk = project(full_qk, jnp.concatenate([bias_q, jnp.zeros_like(bias_q)], axis=1))
     values = project(full_v, bias_v)
-    attended, total = attend_forward(qk, values, key_mask)
+    attended, total, full_in, full_out = attend_forward(
+        qk, values, key_mask, (w_in, w_out), (near_first, far_first)
+    )
+    full_in = full_in.reshape(cols, d, hid)
+    full_out = full_out.reshape(cols, d, hid)
+    attended, cotangent = lax.optimization_barrier((attended, cotangent))
+    up = to_window(cotangent)
     attended_cols = attended.reshape(cols, width, SEQ_MAX)
     first_sum = (
         x.astype(F32) + jnp.einsum("cde,cet->dt", full_attn, attended_cols, preferred_element_type=F32)

time: 490 us -> 471 us (0.961)
  Pallas kernels: 295 us -> 272 us
  matrix products: 109 us -> 90.4 us
  waiting for transfers between devices: 1.42 us -> 14.9 us
  other arithmetic: 25.7 us -> 30.7 us
    pallas_call x1, Pallas kernels: 131 us -> 83.3 us  [head(): pl.pallas_call(lambda *refs: head_kernel(orders, *refs), in_specs=[vmem]...]
    pallas_call x1, Pallas kernels: 41.6 us -> 68.4 us  [attend_forward(): pl.pallas_call(lambda *refs: attend_forward_kernel(pieces, events, *refs)...]
    all_to_all x1, waiting for transfers between devices: 0.01 us -> 14.9 us  [to_window(): return lax.all_to_all(a, 'col', split_axis=1, concat_axis=0, tiled=True)]
    dot_general x1, matrix products: 21.7 us -> 10.9 us  [local(): jnp.einsum('cdf,cft->dt', full_in, d_hidden_low, preferred_element_type=F32)]
  transfers between devices with their start and end apart: 5 -> 3, of which waited for: 0 -> 1; matrix products, arithmetic and copies ran while one was open for 23% -> 18% of each run, Pallas kernels for 61% -> 26%
where the time goes in v5:
time: 471 us; the launch traced here: 463 us
  Pallas kernels  272 us (58%)
  matrix products  90.4 us (19%)
  local copies, waits for them, and re-layouts  30.7 us (7%)
  other arithmetic  30.7 us (7%)
  between operations  16.2 us (3%)
  waiting for transfers between devices  14.9 us (3%)
  starting transfers between devices  8.21 us (2%)
    pallas_call x1, Pallas kernels, head(): pl.pallas_call(lambda *refs: head_kernel(orders, *refs), in_specs=[vmem]...  83.3 us
    pallas_call x1, Pallas kernels, tail(): pl.pallas_call(lambda *refs: tail_kernel(orders, *refs), in_specs=[vmem]...  80 us
    pallas_call x1, Pallas kernels, attend_forward(): pl.pallas_call(lambda *refs: attend_forward_kernel(pieces, events, *refs)...  68.4 us
    pallas_call x1, Pallas kernels, attend_backward(): pl.pallas_call(attend_backward_kernel, grid=(heads,), in_specs=qkv_specs(...  40.7 us
    all_to_all x1, waiting for transfers between devices, to_window(): return lax.all_to_all(a, 'col', split_axis=1, concat_axis=0, tiled=True)  14.9 us
    dot_general x1, matrix products, local(): jnp.einsum('cdf,cft->dt', full_in, d_hidden_low, preferred_element_type=F32)  10.9 us
    dot_general x1, matrix products, local(): jnp.einsum('cdf,dt->cft', full_out, d_second_low, preferred_element_type=...  10.4 us
    dot_general x1, matrix products, local(): jnp.einsum('cdf,dt->cft', full_in, normed_low, preferred_element_type=F32)  10.1 us
  transfers between devices with their start and end apart: 3, of which 1 were waited for; matrix products, arithmetic and copies ran while one was open for 18% of the time, Pallas kernels for 26%

profile of v5, /device:TPU:0, one launch (start us, length us, event | category | flops | bytes accessed | tf_op | source)
XLA Modules:
  0.0 463.5 jit_solution(17814155714486820862)
XLA Ops:
  7.2 1.1 copy.59
  8.3 1.2 dynamic_slice.7
  9.5 1.2 dynamic_slice.8
  12.1 1.2 and_select_fusion.refs_3_.mask_ref
  13.3 0.8 reshape.199
  14.1 0.7 copy.84.refs_0_
  14.8 0.1 copy.85
  14.9 1.5 pad_maximum_fusion.2.refs_1_
  16.4 2.0 concatenate.17.refs_3_
  18.4 83.3 %head.1 = (bf16[2,2,2,2,2,96,384]{6,5,4,3,2,1,0:T(8,128)(2,1)}, bf16[2,2,2,2,2,96,384]{6,5,4,3,2,1,0:T(8,128)(2,1)}, bf16[768,1024]{1,0:T(8,128)(2,1)}, f32[4,12,192]{2,1,0:T(8,128)}) custom-call(bf16[96,384]{1,0:T(8,128)(2,1)} %copy.84.refs_0_, bf16[96,384]{1,0:T(8,128)(2,1)} %pad_maximum_fusion.2.refs_1_, bf16[192,4096]{1,0:T(8,128)(2,1)} %refs_2_.1, ...), custom_call_target="tpu_custom_call" | custom-call | tf_op jit(solution)/shard_map/head/pallas_call | solution.py:318
  101.6 1.3 slice_reduce_fusion.7
  103.0 4.6 add_convert_fusion.1
  107.6 4.0 add_convert_fusion
  111.6 68.4 %attend_forward.1 = (bf16[12,64,1024]{2,1,0:T(8,128)(2,1)}, f32[12,1,1024]{2,1,0:T(1,128)}, bf16[2,2,2,2,2,96,768]{6,5,4,3,2,1,0:T(8,128)(2,1)}, bf16[2,2,2,2,2,96,768]{6,5,4,3,2,1,0:T(8,128)(2,1)}) custom-call(bf16[4,2,3,64,1024]{4,3,2,1,0:T(8,128)(2,1)} %bitcast.178, bf16[4,2,3,64,1024]{4,3,2,1,0:T(8,128)(2,1)} %bitcast.179, ...), custom_call_target="tpu_custom_call" | custom-call | flops 12884901888 | bytes 6291456 | tf_op jit(solution)/shard_map/attend_forward/pallas_call | solution.py:353
  180.0 1.4 copy.94
  181.4 4.3 all-to-all-start.1
  185.8 0.7 fusion.53
  186.5 0.8 slice.78
  187.2 0.1 add.135
  187.8 4.7 %fusion.61 = (f32[1024]{0:T(1024)S(1)}, f32[768,1024]{1,0:T(8,128)S(1)}) fusion(f32[768]{0:T(1024)S(1)} %add.128, bf16[4,192,1024]{2,1,0:T(8,128)(2,1)} %bitcast.186, bf16[4,768,384]{2,1,0:T(8,128)(2,1)} %bitcast.165, bf16[768,1024]{1,0:T(8,128)(2,1)} %get-tuple-element.30), kind=kOutput, calls=%fused_computation.107 | convolution fusion | flops 1211104256 | bytes 7871488 | tf_op jit(solution)/shard_map/cde,cet->dt/dot_general | solution.py:565
  192.5 0.4 multiply_reduce_fusion.5
  193.0 10.1 %multiply_convert_fusion = (bf16[4,768,1024]{2,1,0:T(8,128)(2,1)S(1)}, f32[4,768,1024]{2,1,0:T(8,128)}) fusion(f32[4,768]{1,0:T(4,128)S(1)} %add.135, bf16[4,768,768]{2,1,0:T(8,128)(2,1)S(1)} %bitcast.171, f32[768,1024]{1,0:T(8,128)S(1)} %get-tuple-element.116, f32[768]{0:T(1024)S(1)} %add.132, f32[768]{0:T(1024)S(1)} %mul.163, ...), kind=kOutput, calls=%fused_computation.6 | convolution fusion | flops 4854644736 | bytes 26765312 | tf_op jit(solution)/shard_map/cdf,dt->cft/dot_general | solution.py:570
  203.0 5.2 %fusion.62 = (f32[1024]{0:T(1024)S(1)}, f32[768,1024]{1,0:T(8,128)S(1)}) fusion(f32[768]{0:T(1024)S(1)} %add.141, bf16[4,768,768]{2,1,0:T(8,128)(2,1)S(1)} %bitcast.174, bf16[4,768,1024]{2,1,0:T(8,128)(2,1)S(1)} %get-tuple-element.117, f32[768]{0:T(1024)S(1)} %add.132, f32[768]{0:T(1024)S(1)} %mul.163, f32[1024]{0:T(1024)S(1)} %add_rsqrt_fusion.1, ...), kind=kOutput, calls=%fused_computation.108 | convolution fusion | flops 4837342208 | bytes 17323008 | tf_op jit(solution)/shard_map/cdf,cft->dt/dot_general | solution.py:575
  208.3 0.4 multiply_reduce_fusion.4
  208.7 14.9 %all-to-all-done.1 = bf16[192,4,1024]{2,0,1:T(8,128)(2,1)} async-done(((bf16[192,4,1024]{2,0,1:T(8,128)(2,1)}), bf16[192,4,1024]{2,0,1:T(8,128)(2,1)}, u32[]{:S(2)}, u32[]{:S(2)}) %all-to-all-start.1) | async-done | bytes 1572896 | tf_op jit(solution)/shard_map/all_to_all | solution.py:541
  223.6 2.1 bitcast_reduce_fusion
  225.7 2.6 multiply_reduce_fusion
  228.3 4.1 fusion.57
  232.5 7.0 %convolution_convert_fusion = bf16[4,768,768]{1,2,0:T(8,128)(2,1)} fusion(bf16[4,768,1024]{2,1,0:T(8,128)(2,1)S(1)} %copy-done.13, f32[768,1024]{1,0:T(8,128)S(1)} %get-tuple-element.101), kind=kOutput, calls=%fused_computation.42 | convolution fusion | flops 4834983936 | bytes 14155776 | tf_op jit(solution)/shard_map/dt,cft->cdf/dot_general | solution.py:587
  239.5 10.4 %fusion.63 = (f32[4,768]{1,0:T(4,128)S(1)}, bf16[4,768,1024]{2,1,0:T(8,128)(2,1)S(1)}) fusion(f32[4,768,1024]{2,1,0:T(8,128)S(1)} %bitcast.192, f32[4,768]{1,0:T(4,128)S(1)} %add.135, bf16[4,768,768]{2,1,0:T(8,128)(2,1)S(1)} %bitcast.177, f32[768,1024]{1,0:T(8,128)S(1)} %get-tuple-element.101), kind=kOutput, calls=%fused_computation.109 | convolution fusion | flops 4870370304 | bytes 26763264 | tf_op jit(solution)/shard_map/cdf,dt->cft/dot_general | solution.py:588
  250.0 7.0 %fusion.14 = bf16[4,768,768]{1,2,0:T(8,128)(2,1)} fusion(bf16[4,768,1024]{2,1,0:T(8,128)(2,1)S(1)} %get-tuple-element.123, f32[768,1024]{1,0:T(8,128)S(1)} %copy-done.1, f32[768]{0:T(1024)S(1)} %add.132, f32[768]{0:T(1024)S(1)} %mul.163, f32[1024]{0:T(1024)S(1)} %add_rsqrt_fusion.1, f32[1024]{0:T(1024)S(1)} %broadcast_multiply_fusion.5), kind=kOutput, calls=%fused_computation.43 | convolution fusion | flops 4838129664 | bytes 14170112 | tf_op jit(solution)/shard_map/dt,cft->cdf/dot_general | solution.py:591
  257.1 8.3 %pad_maximum_fusion = bf16[32,2,96,768]{3,2,1,0:T(8,128)(2,1)} fusion(bf16[32,1,96,768]{3,2,1,0:T(8,128)(2,1)} %bitcast.149, bf16[32,1,96,768]{3,2,1,0:T(8,128)(2,1)} %bitcast.150), kind=kLoop, calls=%fused_computation.8 | loop fusion | flops 4718592 | bytes 18874368 | tf_op jit(solution)/shard_map/stack | solution.py:592
  265.5 10.9 %multiply_reduce_fusion.1 = (f32[768]{0:T(1024)S(1)}, f32[1024]{0:T(1024)S(1)}, f32[1024]{0:T(1024)S(1)}, f32[768]{0:T(1024)S(1)}, f32[768,1024]{1,0:T(8,128)}) fusion(f32[768,1024]{1,0:T(8,128)S(1)} %copy-done.1, f32[1024]{0:T(1024)S(1)} %add_rsqrt_fusion.1, f32[1024]{0:T(1024)S(1)} %broadcast_multiply_fusion.5, f32[768]{0:T(1024)S(1)} %mul.163, ...), kind=kOutput, calls=%fused_computation.24 | convolution fusion | flops 4839698432 | bytes 20472832 | tf_op jit(solution)/shard_map/cdf,cft->dt/dot_general | solution.py:595
  276.6 4.7 %fusion.58 = (f32[768]{0:T(1024)S(1)}, f32[768,1024]{1,0:T(8,128)}) fusion(f32[1024]{0:T(1024)S(1)} %broadcast_multiply_fusion, f32[768,1024]{1,0:T(8,128)S(1)} %copy-done.1, f32[1024]{0:T(1024)S(1)} %broadcast_multiply_fusion.5, f32[1024]{0:T(1024)S(1)} %broadcast_multiply_fusion.1, f32[768,1024]{1,0:T(8,128)} %get-tuple-element.121, f32[768]{0:T(1024)S(1)} %mul.163, ...), kind=kLoop, calls=%fused_computation.104 | loop fusion | flops 6290688 | bytes 9459712 | tf_op jit(solution)/shard_map/reduce_sum | solution.py:599
  281.4 0.1 reshape.213
  281.5 3.8 all-to-all-start
  285.4 4.0 fusion.37
  289.4 1.6 copy.71
  291.0 5.5 %convolution_convert_fusion.1 = bf16[4,192,1024]{2,1,0:T(8,128)(2,1)} fusion(bf16[4,768,384]{2,1,0:T(8,128)(2,1)} %bitcast.166, f32[768,1024]{1,0:T(8,128)} %get-tuple-element.103), kind=kOutput, calls=%fused_computation.47 | convolution fusion | flops 1209532416 | bytes 6291456 | tf_op jit(solution)/shard_map/cde,dt->cet/dot_general | solution.py:601
  296.4 40.7 %attend_backward.1 = (bf16[4,2,3,64,1024]{4,3,2,1,0:T(8,128)(2,1)}, bf16[4,1,3,64,1024]{4,3,2,1,0:T(8,128)(2,1)}, f32[12,2,64,128]{3,2,1,0:T(8,128)}) custom-call(bf16[4,2,3,64,1024]{4,3,2,1,0:T(8,128)(2,1)} %bitcast.180, bf16[4,2,3,64,1024]{4,3,2,1,0:T(8,128)(2,1)} %bitcast.181, bf16[4,1,3,64,1024]{4,3,2,1,0:T(8,128)(2,1)} %bitcast.185, ...), custom_call_target="tpu_custom_call" | custom-call | flops 32212254720 | bytes 12582912 | tf_op jit(solution)/shard_map/attend_backward/pallas_call | solution.py:123
  337.1 1.4 reduce_sum.152
  338.7 6.5 %convert_bitcast_fusion.1 = bf16[4,768,384]{1,2,0:T(8,128)(2,1)} fusion(bf16[4,384,1024]{2,1,0:T(8,128)(2,1)} %bitcast.182, bf16[768,1024]{1,0:T(8,128)(2,1)} %get-tuple-element.30), kind=kOutput, calls=%fused_computation.46 | convolution fusion | flops 2417098752 | bytes 7077888 | tf_op jit(solution)/shard_map/dt,cnt->cdn/dot_general | solution.py:609
  345.2 4.3 copy.69
  349.5 3.3 fusion.40
  352.8 1.5 copy.70
  354.4 0.6 pad_maximum_fusion.3.refs_4_
  355.1 3.5 fusion.44
  358.6 0.1 copy-done.8
  358.7 1.0 copy-done.10
  359.7 3.7 fusion.5.refs_3_
  363.4 80.0 %tail.1 = (f32[96,384]{1,0:T(8,128)}, f32[96,192]{1,0:T(8,128)}, f32[96,192]{1,0:T(8,128)}, f32[192,4096]{1,0:T(8,128)}, f32[12,192]{1,0:T(8,128)}) custom-call(bf16[2,2,2,2,2,96,384]{6,5,4,3,2,1,0:T(8,128)(2,1)} %bitcast.145, bf16[2,2,2,2,2,96,192]{6,5,4,3,2,1,0:T(8,128)(2,1)} %bitcast.148, bf16[2,2,2,2,2,96,192]{6,5,4,3,2,1,0:T(8,128)(2,1)} %bitcast.147, ...), custom_call_target="tpu_custom_call" | custom-call | tf_op jit(solution)/shard_map/tail/pallas_call | solution.py:487
  443.4 0.7 slice.87
  444.1 0.7 reshape.215
  444.8 1.0 pad_maximum_fusion.1
  445.8 0.1 copy.74
  445.9 0.9 copy.77
  446.8 1.3 fusion.60
  448.2 1.4 fusion.59
  449.6 0.4 convert_bitcast_fusion
  450.0 1.9 copy.89
  451.8 1.2 convert_element_type.126
  453.0 0.8 slice_bitcast_fusion
  453.9 1.7 copy.98
  455.6 0.6 copy.99
  (81 shorter events, 1.3 us)
Async XLA Ops:
  103.0 4.6 copy-start.7
  103.0 4.6 copy-start.9
  111.6 68.4 %copy-start.5 = (bf16[192,4096]{1,0:T(8,128)(2,1)S(1)}, bf16[192,4096]{1,0:T(8,128)(2,1)}, u32[]{:S(2)}) copy-start(bf16[192,4096]{1,0:T(8,128)(2,1)} %param.27) | copy-start | bytes 4718596
  181.4 42.2 %all-to-all-start.1 = ((bf16[192,4,1024]{2,0,1:T(8,128)(2,1)}), bf16[192,4,1024]{2,0,1:T(8,128)(2,1)}, u32[]{:S(2)}, u32[]{:S(2)}) async-start(bf16[192,4,1024]{2,0,1:T(8,128)(2,1)} %bitcast.143), calls=%async_computation.1 | async-start | bytes 3145728 | tf_op jit(solution)/shard_map/all_to_all | solution.py:541
  185.7 266.1 %reduce-scatter.2.cloned.1.call-start = ((), (), s32[]{:S(2)}) async-start(), calls=%async_computation.3 | async-start | bytes 9732096 | tf_op jit(solution)/shard_map/reduce_scatter | solution.py:593
  187.8 5.1 %slice-start = ((s8[4718592]{0:T(1024)(128)(4,1)}), s8[4194304]{0:T(1024)(128)(4,1)S(1)}, s32[]{:S(2)}) async-start(s8[4718592]{0:T(1024)(128)(4,1)} %bitcast.169), calls=%async_computation.4 | async-start | bytes 8388608
  187.8 5.2 %slice-start.1 = ((s8[4718592]{0:T(1024)(128)(4,1)}), s8[524288]{0:T(1024)(128)(4,1)S(1)}, s32[]{:S(2)}) async-start(s8[4718592]{0:T(1024)(128)(4,1)} %bitcast.169), calls=%async_computation.5 | async-start | bytes 1048576
  192.5 10.5 %copy-start = (f32[768,1024]{1,0:T(8,128)}, f32[768,1024]{1,0:T(8,128)S(1)}, u32[]{:S(2)}) copy-start(f32[768,1024]{1,0:T(8,128)S(1)} %get-tuple-element.116) | copy-start | bytes 9437188
  192.5 10.5 %slice-start.2 = ((s8[4718592]{0:T(1024)(128)(4,1)}), s8[4194304]{0:T(1024)(128)(4,1)S(1)}, s32[]{:S(2)}) async-start(s8[4718592]{0:T(1024)(128)(4,1)} %bitcast.172), calls=%async_computation.6 | async-start | bytes 8388608
  192.9 10.1 %slice-start.3 = ((s8[4718592]{0:T(1024)(128)(4,1)}), s8[524288]{0:T(1024)(128)(4,1)S(1)}, s32[]{:S(2)}) async-start(s8[4718592]{0:T(1024)(128)(4,1)} %bitcast.172), calls=%async_computation.7 | async-start | bytes 1048576
  203.0 5.2 %copy-start.12 = (bf16[4,768,1024]{2,1,0:T(8,128)(2,1)}, bf16[4,768,1024]{2,1,0:T(8,128)(2,1)S(1)}, u32[]{:S(2)}) copy-start(bf16[4,768,1024]{2,1,0:T(8,128)(2,1)S(1)} %get-tuple-element.117) | copy-start | bytes 18874372
  225.7 6.8 %copy-start.13 = (bf16[4,768,1024]{2,1,0:T(8,128)(2,1)S(1)}, bf16[4,768,1024]{2,1,0:T(8,128)(2,1)}, u32[]{:S(2)}) copy-start(bf16[4,768,1024]{2,1,0:T(8,128)(2,1)} %copy-done.12) | copy-start | bytes 18874372
  228.3 11.2 %slice-start.4 = ((s8[4718592]{0:T(1024)(128)(4,1)}), s8[4194304]{0:T(1024)(128)(4,1)S(1)}, s32[]{:S(2)}) async-start(s8[4718592]{0:T(1024)(128)(4,1)} %bitcast.175), calls=%async_computation.8 | async-start | bytes 8388608
  228.3 11.1 %slice-start.6 = ((s8[12582912]{0:T(1024)(128)(4,1)}), s8[4194304]{0:T(1024)(128)(4,1)S(1)}, s32[]{:S(2)}) async-start(s8[12582912]{0:T(1024)(128)(4,1)} %bitcast.191), calls=%async_computation.10 | async-start | bytes 8388608
  232.5 7.0 %copy-start.4 = (f32[768,1024]{1,0:T(8,128)}, f32[768,1024]{1,0:T(8,128)S(1)}, u32[]{:S(2)}) copy-start(f32[768,1024]{1,0:T(8,128)S(1)} %get-tuple-element.101) | copy-start | bytes 9437188
  232.5 7.0 %slice-start.5 = ((s8[4718592]{0:T(1024)(128)(4,1)}), s8[524288]{0:T(1024)(128)(4,1)S(1)}, s32[]{:S(2)}) async-start(s8[4718592]{0:T(1024)(128)(4,1)} %bitcast.175), calls=%async_computation.9 | async-start | bytes 1048576
  232.5 7.0 %slice-start.7 = ((s8[12582912]{0:T(1024)(128)(4,1)}), s8[4194304]{0:T(1024)(128)(4,1)S(1)}, s32[]{:S(2)}) async-start(s8[12582912]{0:T(1024)(128)(4,1)} %bitcast.191), calls=%async_computation.11 | async-start | bytes 8388608
  232.5 7.0 %slice-start.8 = ((s8[12582912]{0:T(1024)(128)(4,1)}), s8[4194304]{0:T(1024)(128)(4,1)S(1)}, s32[]{:S(2)}) async-start(s8[12582912]{0:T(1024)(128)(4,1)} %bitcast.191), calls=%async_computation.12 | async-start | bytes 8388608
  239.5 10.5 %copy-start.1 = (f32[768,1024]{1,0:T(8,128)S(1)}, f32[768,1024]{1,0:T(8,128)}, u32[]{:S(2)}) copy-start(f32[768,1024]{1,0:T(8,128)} %copy-done) | copy-start | bytes 9437188
  250.0 7.1 %copy-start.11 = (bf16[4,768,1024]{2,1,0:T(8,128)(2,1)}, bf16[4,768,1024]{2,1,0:T(8,128)(2,1)S(1)}, u32[]{:S(2)}) copy-start(bf16[4,768,1024]{2,1,0:T(8,128)(2,1)S(1)} %get-tuple-element.123) | copy-start | bytes 18874372
  281.5 168.0 %all-to-all-start = ((bf16[4,192,1024]{2,1,0:T(8,128)(2,1)}), bf16[4,192,1024]{2,1,0:T(8,128)(2,1)S(1)}, u32[]{:S(2)}, u32[]{:S(2)}) async-start(bf16[4,192,1024]{2,1,0:T(8,128)(2,1)} %bitcast.146), calls=%async_computation | async-start | bytes 3145728 | tf_op jit(solution)/shard_map/all_to_all | solution.py:578
  355.1 3.5 copy-start.3
  355.1 3.6 copy-start.8
  355.1 4.7 %copy-start.10 = (bf16[4,2,3,64,1024]{4,3,2,1,0:T(8,128)(2,1)S(1)}, bf16[4,2,3,64,1024]{4,3,2,1,0:T(8,128)(2,1)}, u32[]{:S(2)}) copy-start(bf16[4,2,3,64,1024]{4,3,2,1,0:T(8,128)(2,1)} %get-tuple-element.40) | copy-start | bytes 9437188
  449.9 3.9 copy-start.2
  453.9 1.7 copy-start.6
Sparse Core Ops, SparseCore 0:
  265.5 162.7 reduce-scatter.1
